TPU v7x, 32 devices: a whole 2x2x4 slice. The times are simulated.
32 devices in a mesh: groups: 2 (over y), orient: 4 (over z), cls: 2 (over x), dom: 2 (over core).
Axes of the slice: x: 2, y: 2, z: 4, core: 2. Of those that a mesh axis runs over, the one named last changes fastest.
Arguments:
- particles: bfloat16 [256, 2, 16512], P(('groups', 'orient', 'cls', 'dom')), parts along dimension 0, may hold values from -10 to 10
- ctf_index: int32 [256], P(('groups', 'orient', 'cls', 'dom')), parts along dimension 0, may hold values from 0 to 15
- beta: bfloat16 [256], P(('groups', 'orient', 'cls', 'dom')), parts along dimension 0, may hold values from 10 to 60
- significant: int32 [128, 1], P(('groups', 'orient', 'cls', 'dom')), parts along dimension 0, may hold values from 0 to 3; in each aligned block of 4 rows (0 to 3, 4 to 7, ...) at most 2 rows name the same one
- ctf_table: bfloat16 [16, 16512], replicated, may hold values from 0.049804688 to 1
- references: bfloat16 [4, 4, 4, 2, 16512], P(('groups', 'cls'), 'orient'), parts along dimension 0, may hold values from -4 to 4
- offsets: int32 [10, 2], P('groups'), parts along dimension 0, may hold values from -3 to 3, as said below
Outputs:
- class_post: float32 [256, 2], P(('groups', 'orient', 'cls', 'dom')), parts along dimension 0
- log_evidence: float32 [256], P(('groups', 'orient', 'cls', 'dom')), parts along dimension 0
There are 2 independent parts, one for each index of `groups`. A program takes and returns all parts, laid end to end along the dimension named above; an argument that names none is the same for every part. Nothing has to cross between parts.
Inputs may be any that keep to these rules, and one draw needn't show every extreme that they name: `significant`: each block of 2 particles names 1 different orientation groups; the 4 blocks of one device name any one group at most 2 times. The 5 offsets are distinct pairs.
All inputs are finite; a program needn't handle non-finite values.
Results may differ from a plain program's by a relative error of at most 0.0003.
Values may be sent and summed in bfloat16 or wider, within the bound.
No kernel may reach another device: no remote copies, remote signals or barrier semaphores. Data moves between devices by JAX's collectives and lax.ppermute only.
A program may use at most 128 MiB of HBM per device.

v0:
```python
import math

import jax
import jax.numpy as jnp
from jax import lax
from jax.sharding import PartitionSpec as P

BOX = 256
KX = 129
KY = 128


EPSILON = 1e-06


def phase_tables(offsets):
    pixel_index = jnp.arange(KX * KY, dtype=jnp.int32)
    freq_x = pixel_index % KX
    freq_y = pixel_index // KX - KY // 2
    phase_rotations = jnp.mod(
        offsets[:, 0:1] * freq_x[None, :] + offsets[:, 1:2] * freq_y[None, :], BOX
    )
    angles = phase_rotations.astype(jnp.float32) * (2.0 * math.pi / BOX)
    return (jnp.cos(angles), jnp.sin(angles))


def shifted_table(refs_now, cosines, sines):
    real_part = refs_now[:, 0, :].astype(jnp.float32)
    imag_part = refs_now[:, 1, :].astype(jnp.float32)
    translation_real = real_part[None] * cosines[:, None] + imag_part[None] * sines[:, None]
    shift_imag = imag_part[None] * cosines[:, None] - real_part[None] * sines[:, None]
    shifted = jnp.stack([translation_real, shift_imag], axis=2).astype(jnp.bfloat16)
    return shifted.reshape(shifted.shape[0] * shifted.shape[1], 2 * shifted.shape[3])


def ref_energy(refs_now):
    return jnp.sum(jnp.square(refs_now.astype(jnp.float32)), axis=1)


def class_evidence(weighted, image_power, inverse_noise, power_of, refs_now, cosines, sines):
    shifted = shifted_table(refs_now, cosines, sines)
    intersection = lax.dot_general(
        weighted, shifted, (((1,), (1,)), ((), ())), preferred_element_type=jnp.float32
    )
    ref_power = power_of(ref_energy(refs_now))
    orients = refs_now.shape[0]
    intersection = intersection.reshape(intersection.shape[0], -1, orients)
    normalizer = jnp.sqrt(image_power[:, None] * ref_power + EPSILON)
    logits = inverse_noise[:, None, None] * intersection / normalizer[:, None, :]
    return jnp.sum(jnp.exp(logits), axis=(1, 2))


def local(particles, ctf_index, beta, significant, ctf_table, references, offsets):
    groups = lax.axis_size("orient")
    blocks = significant.shape[0]
    listed_count = significant.shape[1]
    per_block = particles.shape[0] // blocks
    pixels = particles.shape[2]
    ctf_codes = ctf_table.shape[0]
    capacity = max(2, 2 * blocks * listed_count // groups)
    cosines, sines = phase_tables(offsets)
    member_entry = jnp.any(
        significant[:, :, None] == jnp.arange(groups, dtype=jnp.int32)[None, None, :], axis=1
    ).astype(jnp.int32)
    slot_rank = jnp.cumsum(member_entry, axis=0) - member_entry
    placed = member_entry[:, :, None] * (
        slot_rank[:, :, None] == jnp.arange(capacity, dtype=jnp.int32)[None, None, :]
    ).astype(jnp.int32)
    routing = (
        jnp.transpose(placed, (1, 2, 0)).reshape(groups * capacity, blocks).astype(jnp.float32)
    )
    routing_half = routing.astype(jnp.bfloat16)

    def dispatch(values):
        flattened = values.reshape(blocks, -1)
        dispatched = jnp.dot(routing_half, flattened, preferred_element_type=jnp.float32).astype(
            jnp.bfloat16
        )
        return dispatched.reshape((groups, capacity * per_block) + values.shape[2:])

    particle_blocks = dispatch(particles.reshape(blocks, per_block, 2, pixels))
    extras = jnp.stack([ctf_index.astype(jnp.bfloat16), beta], axis=1)
    outgoing = (particle_blocks, dispatch(extras.reshape(blocks, per_block, 2)))

    def prepare(received):
        particle_images = received[0]
        slot_count = particle_images.shape[0] * particle_images.shape[1]
        flattened = particle_images.reshape(slot_count, 2, pixels)
        image_power = jnp.sum(jnp.square(flattened.astype(jnp.float32)), axis=(1, 2))
        extras = received[1].reshape(slot_count, 2)
        ctf_select = (
            extras[:, 0:1].astype(jnp.float32) == jnp.arange(ctf_codes, dtype=jnp.float32)[None, :]
        ).astype(jnp.float32)
        inverse_noise = extras[:, 1].astype(jnp.float32)
        ctf_rows = jnp.dot(
            ctf_select.astype(jnp.bfloat16), ctf_table, preferred_element_type=jnp.float32
        ).astype(jnp.bfloat16)
        table_squares = jnp.square(ctf_table.astype(jnp.float32))

        def power_of(energy):
            table_power = lax.dot_general(
                table_squares,
                energy,
                (((1,), (1,)), ((), ())),
                precision=lax.Precision.HIGHEST,
                preferred_element_type=jnp.float32,
            )
            return jnp.dot(
                ctf_select,
                table_power,
                precision=lax.Precision.HIGHEST,
                preferred_element_type=jnp.float32,
            )

        weighted = (
            ctf_rows.astype(jnp.float32)[:, None, :] * flattened.astype(jnp.float32)
        ).astype(jnp.bfloat16)
        return (
            weighted.reshape(slot_count, 2 * pixels),
            image_power,
            inverse_noise,
            power_of,
            slot_count,
        )

    every_class = lax.all_gather(references, "cls", axis=0, tiled=True)
    received = (
        lax.all_to_all(outgoing[0], "orient", split_axis=0, concat_axis=0, tiled=True),
        lax.all_to_all(outgoing[1], "orient", split_axis=0, concat_axis=0, tiled=True),
    )
    weighted, image_power, inverse_noise, power_of, slot_count = prepare(received)
    columns = [
        class_evidence(
            weighted, image_power, inverse_noise, power_of, every_class[class_id, 0], cosines, sines
        )
        for class_id in range(every_class.shape[0])
    ]
    marginal_evidence = jnp.stack(columns, axis=1)
    shaped = marginal_evidence.reshape(
        received[0].shape[0], received[0].shape[1], marginal_evidence.shape[1]
    )
    returned = lax.all_to_all(shaped, "orient", split_axis=0, concat_axis=0, tiled=True)
    class_total = returned.shape[2]
    returned_rows = returned.reshape(groups * capacity, per_block * class_total)
    home_sums = lax.dot_general(
        routing,
        returned_rows,
        (((0,), (0,)), ((), ())),
        precision=lax.Precision.HIGHEST,
        preferred_element_type=jnp.float32,
    )
    evidence_home = home_sums.reshape(blocks * per_block, class_total)
    all_classes = jnp.sum(evidence_home, axis=1)
    return (evidence_home / all_classes[:, None], jnp.log(all_classes))


def solution(mesh):
    placed = (
        P(("groups", "orient", "cls", "dom"), None, None),
        P(("groups", "orient", "cls", "dom")),
        P(("groups", "orient", "cls", "dom")),
        P(("groups", "orient", "cls", "dom"), None),
        P(),
        P(("groups", "cls"), "orient", None, None, None),
        P("groups", None),
    )
    return jax.shard_map(
        local,
        mesh=mesh,
        in_specs=placed,
        out_specs=(
            P(("groups", "orient", "cls", "dom"), None),
            P(("groups", "orient", "cls", "dom")),
        ),
        check_vma=False,
    )
```

profile of v0, /device:TPU:0, one launch (start us, length us, event | category | flops | bytes accessed | tf_op | source)
XLA Modules:
  0.0 75.0 jit_solution(8348397335872190462)
XLA Ops:
  0.6 0.7 fusion.67
  1.4 0.7 fusion.66
  2.2 0.7 bitcast_subtract_fusion
  2.9 0.7 convert_bitcast_fusion
  3.5 0.7 pad_maximum_fusion.1
  4.7 0.7 copy.23
  5.4 6.3 %all-to-all-start = ((bf16[4,4,2]{1,2,0:T(2,128)(2,1)}), bf16[4,4,2]{1,2,0:T(2,128)(2,1)S(1)}, u32[]{:S(2)}, u32[]{:S(2)}) async-start(bf16[4,4,2]{1,2,0:T(2,128)(2,1)} %copy.23), calls=%async_computation | async-start | bytes 4096 | tf_op jit(solution)/shard_map/all_to_all | solution.py:129
  12.4 0.8 %slice_bitcast_fusion.7 = (s32[5]{0:T(128)S(1)}, s32[5]{0:T(128)S(1)}) fusion(s32[5,2]{0,1:T(2,128)} %param.13), kind=kLoop, calls=%fused_computation.88 | loop fusion | bytes 80 | tf_op jit(solution)/shard_map/mul | solution.py:21
  13.2 1.1 %copy.26 = bf16[1,1,4,2,16512]{4,2,3,1,0:T(4,128)(2,1)S(1)} copy(bf16[1,1,4,2,16512]{4,3,2,1,0:T(2,128)(2,1)} %param.12) | data formatting | bytes 528384 | tf_op args[5]
  14.2 8.5 %all_gather.3 = bf16[2,1,4,2,16512]{4,2,3,1,0:T(4,128)(2,1)S(1)} all-gather(bf16[1,1,4,2,16512]{4,2,3,1,0:T(4,128)(2,1)S(1)} %copy.26), channel_id=1, replica_groups=mesh['groups'=2,'orient'=4,'cls'=2,'dom'=2] {'cls'}, dimensions={0}, use_global_device_ids=true | all-gather | bytes 792576 | tf_op jit(solution)/shard_map/all_gather | solution.py:126
  23.7 0.9 %fusion.53 = (f32[4,16512]{1,0:T(4,128)S(1)}, f32[4,16512]{1,0:T(4,128)}, f32[4,16512]{1,0:T(4,128)}, f32[4,16512]{1,0:T(4,128)}) fusion(bf16[4,2,16512]{2,0,1:T(4,128)(2,1)S(1)} %get-tuple-element.17, bf16[4,2,16512]{2,0,1:T(4,128)(2,1)S(1)} %get-tuple-element.16), kind=kLoop, calls=%fused_computation.54 | loop fusion | flops 264192 | bytes 1585152 | tf_op jit(solution)/shard_map/convert_element_type | solution.py:28
  24.6 2.2 %fusion.51 = (f32[5,16512]{1,0:T(8,128)S(1)}, f32[5,16512]{1,0:T(8,128)S(1)}) fusion(s32[16512]{0:T(1024)S(1)} %copy-done.4, s32[5]{0:T(128)S(1)} %get-tuple-element.27, s32[16512]{0:T(1024)S(1)} %get-tuple-element.30, s32[5]{0:T(128)S(1)} %get-tuple-element.26), kind=kLoop, calls=%fused_computation.48 | loop fusion | flops 1320960 | bytes 792616 | tf_op jit(solution)/shard_map/cos | solution.py:24
  26.8 1.3 %reshape.429 = bf16[4,4,2,16512]{3,2,1,0:T(2,128)(2,1)} reshape(bf16[8,66048]{1,0:T(8,128)(2,1)S(1)} %convolution_convert_fusion) | data formatting | bytes 2113536 | tf_op jit(solution)/shard_map/reshape | solution.py:79
  28.0 4.8 %all-to-all-start.1 = ((bf16[4,4,2,16512]{3,2,1,0:T(2,128)(2,1)}), bf16[4,4,2,16512]{3,2,1,0:T(2,128)(2,1)S(1)}, u32[]{:S(2)}, u32[]{:S(2)}) async-start(bf16[4,4,2,16512]{3,2,1,0:T(2,128)(2,1)} %reshape.429), calls=%async_computation.1 | async-start | bytes 2113536 | tf_op jit(solution)/shard_map/all_to_all | solution.py:128
  32.8 3.6 %add_convert_fusion.1 = (bf16[5,4,1,16512]{3,0,2,1:T(8,128)(2,1)}, bf16[5,4,1,16512]{3,0,2,1:T(8,128)(2,1)}, bf16[5,4,1,16512]{3,0,2,1:T(8,128)(2,1)}, bf16[5,4,1,16512]{3,0,2,1:T(8,128)(2,1)}) fusion(f32[5,16512]{1,0:T(8,128)S(1)} %get-tuple-element.23, f32[4,16512]{1,0:T(4,128)} %get-tuple-element.32, f32[5,16512]{1,0:T(8,128)S(1)} %get-tuple-element.22, ...), kind=kLoop, calls=%fused_computation.17 | loop fusion | flops 5283840 | bytes 4359168 | tf_op jit(solution)/shard_map/convert.9
  36.9 1.4 %fusion.45 = f32[16,4]{0,1:T(4,128)S(1)} fusion(f32[4,16512]{1,0:T(4,128)S(1)} %get-tuple-element.9, bf16[16,16512]{1,0:T(8,128)(2,1)S(1)} %copy-done), kind=kOutput, calls=%fused_computation.37 | convolution fusion | flops 13209600 | bytes 792832 | tf_op jit(solution)/shard_map/dot_general | solution.py:101
  38.2 1.4 %fusion.46 = f32[16,4]{0,1:T(4,128)S(1)} fusion(f32[4,16512]{1,0:T(4,128)S(1)} %get-tuple-element.8, bf16[16,16512]{1,0:T(8,128)(2,1)S(1)} %copy-done), kind=kOutput, calls=%fused_computation.38 | convolution fusion | flops 13209600 | bytes 792832 | tf_op jit(solution)/shard_map/dot_general | solution.py:101
  39.7 1.4 %fusion = f32[16,16512]{1,0:T(8,128)} fusion(bf16[16,16512]{1,0:T(8,128)(2,1)S(1)} %copy-done, f32[16]{0:T(128)S(1)} %get-tuple-element.29), kind=kOutput, calls=%fused_computation.2 | convolution fusion | flops 8983296 | bytes 1585216 | tf_op jit(solution)/shard_map/dot_general | solution.py:95
  41.1 16.2 %all-to-all-done.1 = bf16[4,4,2,16512]{3,2,1,0:T(2,128)(2,1)S(1)} async-done(((bf16[4,4,2,16512]{3,2,1,0:T(2,128)(2,1)}), bf16[4,4,2,16512]{3,2,1,0:T(2,128)(2,1)S(1)}, u32[]{:S(2)}, u32[]{:S(2)}) %all-to-all-start.1) | async-done | bytes 1056800 | tf_op jit(solution)/shard_map/all_to_all | solution.py:128
  57.3 1.2 %multiply_reduce_fusion = f32[4,4]{1,0:T(4,128)S(1)} fusion(bf16[4,4,2,16512]{3,2,1,0:T(2,128)(2,1)S(1)} %all-to-all-done.1), kind=kLoop, calls=%fused_computation.15 | loop fusion | flops 1585136 | bytes 1056832 | tf_op jit(solution)/shard_map/reduce_sum | solution.py:89
  58.9 0.8 %bitcast_convert_fusion.2 = f32[16,2,16512]{2,1,0:T(2,128)S(1)} fusion(bf16[4,4,2,16512]{3,2,1,0:T(2,128)(2,1)S(1)} %all-to-all-done.1), kind=kLoop, calls=%fused_computation.93 | loop fusion | flops 528384 | bytes 3170304 | tf_op jit(solution)/shard_map/convert_element_type | solution.py:116
  59.9 2.5 %fusion.34 = f32[16]{0:T(128)S(1)} fusion(bf16[5,4,1,16512]{3,0,2,1:T(8,128)(2,1)} %get-tuple-element.14, bf16[5,4,1,16512]{3,0,2,1:T(8,128)(2,1)} %get-tuple-element.15, f32[16,4]{0,1:T(4,128)S(1)} %fusion.41, f32[16]{0:T(128)S(1)} %get-tuple-element.28, f32[16,2,16512]{2,1,0:T(2,128)S(1)} %bitcast_convert_fusion.2, f32[16,16512]{1,0:T(8,128)S(1)} %copy-done.1), kind=kOutput, calls=%fused_computation.26 | convolution fusion | flops 24834992 | bytes 4491648 | tf_op jit(solution)/shard_map/dot_general | solution.py:42
  62.7 2.4 %fusion.37 = f32[16]{0:T(128)S(1)} fusion(bf16[5,4,1,16512]{3,0,2,1:T(8,128)(2,1)} %get-tuple-element.11, bf16[5,4,1,16512]{3,0,2,1:T(8,128)(2,1)} %get-tuple-element.10, f32[16,4]{0,1:T(4,128)S(1)} %fusion.43, f32[16]{0:T(128)S(1)} %get-tuple-element.28, f32[16,2,16512]{2,1,0:T(2,128)S(1)} %bitcast_convert_fusion.2, f32[16,16512]{1,0:T(8,128)S(1)} %copy-done.2), kind=kOutput, calls=%fused_computation.27 | convolution fusion | flops 24834992 | bytes 4491648 | tf_op jit(solution)/shard_map/dot_general | solution.py:42
  65.1 8.1 %all_to_all.15 = f32[4,4,2]{1,2,0:T(2,128)S(1)} all-to-all(f32[4,4,2]{1,2,0:T(2,128)S(1)} %copy.27), channel_id=1, replica_groups=mesh['groups'=2,'orient'=4,'cls'=2,'dom'=2] {'orient'}, dimensions={0} | all-to-all | bytes 256 | tf_op jit(solution)/shard_map/all_to_all | solution.py:142
  (41 shorter events, 5.5 us)
Async XLA Ops:
  0.6 22.3 %copy-start.3 = (bf16[8,2,16512]{2,1,0:T(2,128)(2,1)S(1)}, bf16[8,2,16512]{2,1,0:T(2,128)(2,1)}, u32[]{:S(2)}) copy-start(bf16[8,2,16512]{2,1,0:T(2,128)(2,1)} %param.7) | copy-start | bytes 1585156
  5.4 22.6 %all-to-all-start = ((bf16[4,4,2]{1,2,0:T(2,128)(2,1)}), bf16[4,4,2]{1,2,0:T(2,128)(2,1)S(1)}, u32[]{:S(2)}, u32[]{:S(2)}) async-start(bf16[4,4,2]{1,2,0:T(2,128)(2,1)} %copy.23), calls=%async_computation | async-start | bytes 4096 | tf_op jit(solution)/shard_map/all_to_all | solution.py:129
  23.3 1.3 %copy-start.4 = (s32[16512]{0:T(1024)S(1)}, s32[16512]{0:T(1024)}, u32[]{:S(2)}) copy-start(s32[16512]{0:T(1024)} %get-tuple-element.31) | copy-start | bytes 198148
  28.0 29.3 %all-to-all-start.1 = ((bf16[4,4,2,16512]{3,2,1,0:T(2,128)(2,1)}), bf16[4,4,2,16512]{3,2,1,0:T(2,128)(2,1)S(1)}, u32[]{:S(2)}, u32[]{:S(2)}) async-start(bf16[4,4,2,16512]{3,2,1,0:T(2,128)(2,1)} %reshape.429), calls=%async_computation.1 | async-start | bytes 2113536 | tf_op jit(solution)/shard_map/all_to_all | solution.py:128
  32.8 4.0 %copy-start = (bf16[16,16512]{1,0:T(8,128)(2,1)S(1)}, bf16[16,16512]{1,0:T(8,128)(2,1)}, u32[]{:S(2)}) copy-start(bf16[16,16512]{1,0:T(8,128)(2,1)} %param.11) | copy-start | bytes 1585156
  58.7 1.2 %copy-start.1 = (f32[16,16512]{1,0:T(8,128)S(1)}, f32[16,16512]{1,0:T(8,128)}, u32[]{:S(2)}) copy-start(f32[16,16512]{1,0:T(8,128)} %fusion) | copy-start | bytes 3170308
  59.9 2.8 %copy-start.2 = (f32[16,16512]{1,0:T(8,128)S(1)}, f32[16,16512]{1,0:T(8,128)}, u32[]{:S(2)}) copy-start(f32[16,16512]{1,0:T(8,128)} %fusion) | copy-start | bytes 3170308
where the time goes:
time: 75.5 us; the launch traced here: 75 us
  blocking collectives  16.6 us (22%)
  waiting for transfers between devices  16.2 us (21%)
  other arithmetic  13.5 us (18%)
  starting transfers between devices  11.2 us (15%)
  matrix products  10.1 us (13%)
  local copies, waits for them, and re-layouts  6.68 us (9%)
    all_to_all x1, waiting for transfers between devices, local(): lax.all_to_all(outgoing[0], 'orient', split_axis=0, concat_axis=0, tiled=...  16.2 us
    all_gather x1, blocking collectives, local(): every_class = lax.all_gather(references, 'cls', axis=0, tiled=True)  8.47 us
    all_to_all x1, blocking collectives, local(): lax.all_to_all(shaped, 'orient', split_axis=0, concat_axis=0, tiled=True)  8.11 us
    all_to_all x1, starting transfers between devices, local(): lax.all_to_all(outgoing[1], 'orient', split_axis=0, concat_axis=0, tiled=...  6.35 us
    dot_general x2, matrix products, class_evidence(): lax.dot_general(weighted, shifted, (((1,), (1,)), ((), ())), preferred_el...  4.82 us
    all_to_all x1, starting transfers between devices, local(): lax.all_to_all(outgoing[0], 'orient', split_axis=0, concat_axis=0, tiled=...  4.81 us
    another operation x1, other arithmetic  3.64 us
    dot_general x2, matrix products, power_of(): lax.dot_general(table_squares, energy, (((1,), (1,)), ((), ())), precisio...  2.77 us
  transfers between devices with their start and end apart: 2, of which 1 were waited for; matrix products, arithmetic and copies ran while one was open for 21% of the time, Pallas kernels for 0%

commit v1 on v0

v1 whole, which is shorter than its diff:
```python
import functools
import math

import jax
import jax.numpy as jnp
from jax import lax
from jax.experimental import pallas as pl
from jax.experimental.pallas import tpu as pltpu
from jax.sharding import PartitionSpec as P

BOX = 256
KX = 129
KY = 128

EPSILON = 1e-06
LANES = 128
SET = 4


def phase_tables(offsets):
    pixel_index = jnp.arange(KX * KY, dtype=jnp.int32)
    freq_x = pixel_index % KX
    freq_y = pixel_index // KX - KY // 2
    phase_rotations = jnp.mod(
        offsets[:, 0:1] * freq_x[None, :] + offsets[:, 1:2] * freq_y[None, :], BOX
    )
    angles = phase_rotations.astype(jnp.float32) * (2.0 * math.pi / BOX)
    return (jnp.cos(angles), jnp.sin(angles))


def tiled(values):
    rows, parts, pixels = values.shape
    split = values.reshape(rows, parts, pixels // LANES, LANES)
    return jnp.transpose(split, (0, 2, 1, 3))


def evidence_kernel(dims, *refs):
    n_img, n_full, rows, oris, tiles, shifts, codes, sig = dims
    refs = list(refs)
    gids = refs.pop(0)
    meta = refs.pop(0)
    ctf, cosines, sines = refs.pop(0), refs.pop(0), refs.pop(0)
    images = [refs.pop(0) for _ in range(n_img)]
    full = [refs.pop(0) for _ in range(n_full)]
    halves = [refs.pop(0) for _ in range(2)]
    outs = [refs.pop(0) for _ in range(n_img)]
    img_buf, ref_buf, ctf_rows, lhs, rhs, img_sem, ref_sem = refs

    pair = 2 * rows
    chunk_rows = 2 * oris
    chunk_pad = rhs.shape[0] // SET
    n_chunks = n_full + 1
    w_rows = n_img * pair

    def image_copies(i):
        return [
            pltpu.make_async_copy(images[i].at[p], img_buf.at[i, :, p], img_sem.at[i])
            for p in range(rows)
        ]

    def chunk_copies(c):
        if c < n_full:
            sources = [full[c].at[o] for o in range(oris)]
        else:
            half = oris // 2
            sources = [halves[o // half].at[o % half] for o in range(oris)]
        slot = c % SET
        return [
            pltpu.make_async_copy(sources[o], ref_buf.at[slot, :, o], ref_sem.at[slot])
            for o in range(oris)
        ]

    for i in range(n_img):
        for copy in image_copies(i):
            copy.start()
    for c in range(min(SET, n_chunks)):
        for copy in chunk_copies(c):
            copy.start()

    def lane(k):
        return pl.ds(pl.multiple_of(k * LANES, LANES), LANES)

    def square_step(k, carry):
        value = ctf[:, lane(k)].astype(jnp.float32)
        square = value * value
        high = square.astype(jnp.bfloat16)
        lhs[w_rows : w_rows + codes, lane(k)] = high
        lhs[w_rows + codes : w_rows + 2 * codes, lane(k)] = (
            square - high.astype(jnp.float32)
        ).astype(jnp.bfloat16)
        return carry

    lax.fori_loop(0, tiles, square_step, 0, unroll=3)

    code_ids = lax.broadcasted_iota(jnp.int32, (1, codes), 1).astype(jnp.float32)
    powers = []
    for i in range(n_img):
        span = slice(i * pair, (i + 1) * pair)
        pick = (meta[span, 0:1] == code_ids).astype(jnp.bfloat16)
        ctf_rows[...] = jnp.dot(pick, ctf[...], preferred_element_type=jnp.float32)
        for copy in image_copies(i):
            copy.wait()

        def weigh(k, total, i=i, span=span):
            value = img_buf[i, k].reshape(pair, LANES).astype(jnp.float32)
            lhs[span, lane(k)] = (ctf_rows[:, lane(k)] * value).astype(jnp.bfloat16)
            return total + value * value

        total = lax.fori_loop(
            0, tiles, weigh, jnp.zeros((pair, LANES), jnp.float32), unroll=3
        )
        powers.append(jnp.sum(total, axis=1, keepdims=True))
    power = jnp.concatenate(powers, axis=0)
    power = power + pltpu.roll(jnp.broadcast_to(power, (w_rows, LANES)), w_rows - 1, 0)[
        :, 0:1
    ]
    beta = meta[:, 1:2]
    pick_all = (meta[:, 0:1] == code_ids).astype(jnp.float32)
    pick_all = jnp.concatenate([pick_all, pick_all], axis=1)

    columns = rhs.shape[0]
    row_id = lax.broadcasted_iota(jnp.int32, (w_rows, columns), 0)
    col_id = lax.broadcasted_iota(jnp.int32, (w_rows, columns), 1)
    within = col_id % chunk_pad
    same_part = (row_id % 2) == (col_id % 2)
    odd = lax.broadcasted_iota(jnp.int32, (chunk_rows, LANES), 0) % 2 == 1

    evidence = jnp.zeros((w_rows, 1), jnp.float32)
    for first in range(0, n_chunks, SET):
        live = min(SET, n_chunks - first)
        for c in range(first, first + live):
            if first:
                for copy in chunk_copies(c):
                    copy.start()
        for c in range(first, first + live):
            for copy in chunk_copies(c):
                copy.wait()

        def shift_step(k, carry, live=live):
            cos = [cosines[t : t + 1, lane(k)] for t in range(shifts)]
            sin = [sines[t : t + 1, lane(k)] for t in range(shifts)]
            for slot in range(live):
                value = ref_buf[slot, k].reshape(chunk_rows, LANES).astype(jnp.float32)
                turned = jnp.where(
                    odd,
                    -pltpu.roll(value, 1, 0),
                    pltpu.roll(value, chunk_rows - 1, 0),
                )
                parts = [value * cos[t] + turned * sin[t] for t in range(shifts)]
                square = value * value
                high = square.astype(jnp.bfloat16).astype(jnp.float32)
                parts += [high, square - high]
                spare = chunk_pad - len(parts) * chunk_rows
                if spare:
                    parts.append(jnp.zeros((spare, LANES), jnp.float32))
                rhs[slot * chunk_pad : (slot + 1) * chunk_pad, lane(k)] = jnp.concatenate(
                    parts, axis=0
                ).astype(jnp.bfloat16)
            return carry

        lax.fori_loop(0, tiles, shift_step, 0)
        product = lax.dot_general(
            lhs[...], rhs[...], (((1,), (1,)), ((), ())), preferred_element_type=jnp.float32
        )
        cross = jnp.where(same_part, product[:w_rows], 0.0)
        cross = cross + pltpu.roll(cross, w_rows - 1, 0)
        cross = cross + pltpu.roll(cross, columns - 1, 1)
        energy = jnp.dot(
            pick_all,
            product[w_rows:],
            precision=lax.Precision.HIGHEST,
            preferred_element_type=jnp.float32,
        )
        energy = energy + pltpu.roll(energy, columns - chunk_rows, 1)
        energy = energy + pltpu.roll(energy, columns - 1, 1)
        spread = jnp.zeros_like(energy)
        for t in range(shifts):
            moved = pltpu.roll(energy, columns - (shifts - t) * chunk_rows, 1)
            spread = jnp.where(within // chunk_rows == t, moved, spread)
        wanted = (within < shifts * chunk_rows) & (col_id % 2 == 0)
        named = jnp.zeros((w_rows, columns), jnp.bool_)
        for slot in range(live):
            gid = gids[first + slot]
            for s in range(sig):
                hit = meta[:, 2 + s : 3 + s].astype(jnp.int32) == gid
                named = named | (hit & (col_id // chunk_pad == slot))
        wanted = wanted & named & (row_id % 2 == 0)
        normalizer = jnp.sqrt(power * spread + EPSILON)
        logits = jnp.where(wanted, beta * cross / jnp.where(wanted, normalizer, 1.0), 0.0)
        evidence = evidence + jnp.sum(
            jnp.where(wanted, jnp.exp(logits), 0.0), axis=1, keepdims=True
        )
    particle = lax.broadcasted_iota(jnp.int32, (w_rows, LANES), 0)
    place = lax.broadcasted_iota(jnp.int32, (w_rows, LANES), 1)
    for i in range(n_img):
        chosen = (particle == i * pair + 2 * place) & (place < rows)
        outs[i][...] = jnp.sum(jnp.where(chosen, evidence, 0.0), axis=0, keepdims=True)


def finish_kernel(rows, me, *refs):
    n_cls = len(refs) - 2
    post, log_out = refs[-2:]
    x = me[0]
    own = [r[...] for r in refs[:n_cls]]
    total = own[0]
    for value in own[1:]:
        total = total + value
    row = lax.broadcasted_iota(jnp.int32, (n_cls, LANES), 0)
    table = jnp.zeros((n_cls, LANES), jnp.float32)
    for k in range(n_cls):
        table = jnp.where(row == (x ^ k), own[k], table)
    post[...] = (table / total)[:, :rows]
    log_out[...] = jnp.log(total)[:, :rows]


def local(particles, ctf_index, beta, significant, ctf_table, references, offsets):
    groups = lax.axis_size("orient")
    n_cls = lax.axis_size("cls")
    cores = lax.axis_size("dom")
    blocks, sig = significant.shape
    rows, _, pixels = particles.shape
    per_block = rows // blocks
    codes = ctf_table.shape[0]
    oris = references.shape[2]
    shifts = offsets.shape[0]
    tiles = pixels // LANES
    refs_own = references.reshape(oris, 2, pixels)
    z = lax.axis_index("orient")
    x = lax.axis_index("cls")
    d = lax.axis_index("dom")
    steps = list(range(1, groups))

    def core_step(first, second):
        pairs = []
        for a in range(groups):
            for core in range(cores):
                step = second if core else first
                pairs.append((a * cores + core, (a ^ step) * cores + core))
        return pairs

    swap = [(c, cores - 1 - c) for c in range(cores)]
    direct, order = [], []
    while len(steps) > 1:
        first, second = steps.pop(0), steps.pop(0)
        direct.append(lax.ppermute(refs_own, ("orient", "dom"), core_step(first, second)))
        order.append((first, second))

    def across(values, k):
        return lax.ppermute(values, "cls", [(c, c ^ k) for c in range(n_cls)])

    images = [particles] + [across(particles, k) for k in range(1, n_cls)]
    last = steps.pop(0)
    half = oris // 2
    part = lax.dynamic_slice_in_dim(refs_own, d * half, half, axis=0)
    near_half = lax.ppermute(part, "orient", [(a, a ^ last) for a in range(groups)])
    own_meta = jnp.concatenate(
        [
            ctf_index.astype(jnp.float32)[:, None],
            beta.astype(jnp.float32)[:, None],
            jnp.repeat(significant.astype(jnp.float32), per_block, axis=0),
        ],
        axis=1,
    )
    metas = [own_meta] + [across(own_meta, k) for k in range(1, n_cls)]
    meta = jnp.repeat(jnp.concatenate(metas, axis=0), 2, axis=0)
    cosines, sines = phase_tables(offsets)
    mates = [lax.ppermute(values, "dom", swap) for values in direct]
    far_half = lax.ppermute(near_half, "dom", swap)

    chunks, ids = [refs_own], [z]
    for (first, second), near, mate in zip(order, direct, mates):
        chunks += [near, mate]
        ids += [z ^ jnp.where(d == 0, first, second), z ^ jnp.where(d == 0, second, first)]
    ids.append(z ^ last)
    gids = jnp.stack(ids).astype(jnp.int32)

    n_img = len(images)
    chunk_pad = -(-(shifts + 2) * 2 * oris // 16) * 16
    dims = (n_img, len(chunks), rows, oris, tiles, shifts, codes, sig)
    anywhere = pl.BlockSpec(memory_space=pl.ANY)
    vmem = pl.BlockSpec(memory_space=pltpu.VMEM)
    smem = pl.BlockSpec(memory_space=pltpu.SMEM)
    evidence = pl.pallas_call(
        functools.partial(evidence_kernel, dims),
        name="evidence",
        out_shape=[jax.ShapeDtypeStruct((1, LANES), jnp.float32)] * n_img,
        in_specs=[smem, vmem, vmem, vmem, vmem] + [anywhere] * (n_img + len(chunks) + 2),
        out_specs=[vmem] * n_img,
        scratch_shapes=[
            pltpu.VMEM((n_img, tiles, rows, 2, LANES), jnp.bfloat16),
            pltpu.VMEM((SET, tiles, oris, 2, LANES), jnp.bfloat16),
            pltpu.VMEM((2 * rows, pixels), jnp.float32),
            pltpu.VMEM((n_img * 2 * rows + 2 * codes, pixels), jnp.bfloat16),
            pltpu.VMEM((SET * chunk_pad, pixels), jnp.bfloat16),
            pltpu.SemaphoreType.DMA((n_img,)),
            pltpu.SemaphoreType.DMA((SET,)),
        ],
        compiler_params=pltpu.CompilerParams(vmem_limit_bytes=40 << 20),
    )(
        gids,
        meta,
        ctf_table,
        cosines,
        sines,
        *[tiled(v) for v in images],
        *[tiled(v) for v in chunks],
        tiled(near_half),
        tiled(far_half),
    )
    gathered = [evidence[0]] + [across(evidence[k], k) for k in range(1, n_cls)]
    post, log_total = pl.pallas_call(
        functools.partial(finish_kernel, rows),
        name="finish",
        out_shape=[
            jax.ShapeDtypeStruct((n_cls, rows), jnp.float32),
            jax.ShapeDtypeStruct((1, rows), jnp.float32),
        ],
        in_specs=[smem] + [vmem] * n_cls,
        out_specs=[vmem, vmem],
    )(x.astype(jnp.int32)[None], *gathered)
    return (post.T, log_total.reshape(rows))


def solution(mesh):
    placed = (
        P(("groups", "orient", "cls", "dom"), None, None),
        P(("groups", "orient", "cls", "dom")),
        P(("groups", "orient", "cls", "dom")),
        P(("groups", "orient", "cls", "dom"), None),
        P(),
        P(("groups", "cls"), "orient", None, None, None),
        P("groups", None),
    )
    return jax.shard_map(
        local,
        mesh=mesh,
        in_specs=placed,
        out_specs=(
            P(("groups", "orient", "cls", "dom"), None),
            P(("groups", "orient", "cls", "dom")),
        ),
        check_vma=False,
    )
```

time: 75.5 us -> 49.6 us (0.66)
  Pallas kernels: 0 us -> 20.9 us
  blocking collectives: 16.6 us -> 0 us
  other arithmetic: 13.5 us -> 2.36 us
  matrix products: 10.1 us -> 0 us
  waiting for transfers between devices: 16.2 us -> 12.8 us
  starting transfers between devices: 11.2 us -> 8.35 us
  local copies, waits for them, and re-layouts: 6.68 us -> 4.29 us
    pallas_call x0 -> x2, Pallas kernels: none -> 20.9 us  [the longest x1 19.6 us: local(): pl.pallas_call(functools.partial(evidence_kernel, dims), name='evidence',...]
    all_to_all x2 -> x0, waiting for transfers between devices: 16.2 us -> none  [the longest x1 16.2 us: local(): lax.all_to_all(outgoing[0], 'orient', split_axis=0, concat_axis=0, tiled=...]
    ppermute x0 -> x7, waiting for transfers between devices: none -> 12.8 us  [the longest x1 8.34 us: local(): lax.ppermute(refs_own, ('orient', 'dom'), core_step(first, second))]
    all_to_all x2 -> x0, starting transfers between devices: 11.2 us -> none  [the longest x1 6.35 us: local(): lax.all_to_all(outgoing[1], 'orient', split_axis=0, concat_axis=0, tiled=...]
    dot_general x10 -> x0, matrix products: 10.1 us -> none  [the longest x2 4.82 us: class_evidence(): lax.dot_general(weighted, shifted, (((1,), (1,)), ((), ())), preferred_el...]
    all_gather x1 -> x0, blocking collectives: 8.47 us -> none  [local(): every_class = lax.all_gather(references, 'cls', axis=0, tiled=True)]
    ppermute x0 -> x7, starting transfers between devices: none -> 8.35 us  [the longest x1 5.08 us: local(): lax.ppermute(part, 'orient', [(a, a ^ last) for a in range(groups)])]
    all_to_all x1 -> x0, blocking collectives: 8.11 us -> none  [local(): lax.all_to_all(shaped, 'orient', split_axis=0, concat_axis=0, tiled=True)]
  transfers between devices with their start and end apart: 2 -> 7, of which waited for: 1 -> 4; matrix products, arithmetic and copies ran while one was open for 21% -> 5% of each run, Pallas kernels for 0% -> 0%
where the time goes in v1:
time: 49.6 us; the launch traced here: 49.4 us
  Pallas kernels  20.9 us (42%)
  waiting for transfers between devices  12.8 us (26%)
  starting transfers between devices  8.35 us (17%)
  local copies, waits for them, and re-layouts  4.29 us (9%)
  other arithmetic  2.36 us (5%)
  between operations  0.73 us (1%)
    pallas_call x1, Pallas kernels, local(): pl.pallas_call(functools.partial(evidence_kernel, dims), name='evidence',...  19.6 us
    ppermute x1, waiting for transfers between devices, local(): lax.ppermute(refs_own, ('orient', 'dom'), core_step(first, second))  8.34 us
    ppermute x1, starting transfers between devices, local(): lax.ppermute(part, 'orient', [(a, a ^ last) for a in range(groups)])  5.08 us
    ppermute x3, waiting for transfers between devices, across(): return lax.ppermute(values, 'cls', [(c, c ^ k) for c in range(n_cls)])  3.37 us
    ppermute x3, starting transfers between devices, across(): return lax.ppermute(values, 'cls', [(c, c ^ k) for c in range(n_cls)])  2.69 us
    unnamed x19, local copies, waits for them, and re-layouts  2.43 us
    sin x1, other arithmetic, phase_tables(): return (jnp.cos(angles), jnp.sin(angles))  2.16 us
    dynamic_slice x1, local copies, waits for them, and re-layouts, local(): part = lax.dynamic_slice_in_dim(refs_own, d * half, half, axis=0)  1.69 us
  transfers between devices with their start and end apart: 7, of which 4 were waited for; matrix products, arithmetic and copies ran while one was open for 5% of the time, Pallas kernels for 0%

profile of v1, /device:TPU:0, one launch (start us, length us, event | category | flops | bytes accessed | tf_op | source)
XLA Modules:
  0.0 49.4 jit_solution(16132570130782919700)
XLA Ops:
  0.7 1.7 %dynamic-slice_bitcast_fusion = bf16[2,2,16512]{2,1,0:T(2,128)(2,1)} fusion(bf16[1,1,4,2,16512]{4,3,2,1,0:T(2,128)(2,1)} %param.12, s32[]{:T(128)S(6)} %select_n.41), kind=kLoop, calls=%fused_computation.8 | loop fusion | bytes 264196 | tf_op jit(solution)/shard_map/dynamic_slice | solution.py:254
  2.4 5.1 %collective-permute-start.4 = (bf16[2,2,16512]{2,1,0:T(2,128)(2,1)}, bf16[2,2,16512]{2,1,0:T(2,128)(2,1)}, u32[]{:S(2)}, u32[]{:S(2)}) collective-permute-start(bf16[2,2,16512]{2,1,0:T(2,128)(2,1)} %dynamic-slice_bitcast_fusion), channel_id=1, source_target_pairs={{0,12},{4,8},{8,4},{12,0},{1,13},{5,9},{9,5},{13,1},{2,14},{6,10},... | collective-permute-start | bytes 396296 | tf_op jit(solution)/shard_map/ppermute | solution.py:255
  7.4 0.1 broadcast_in_dim.26
  7.5 0.1 broadcast_in_dim.27
  7.6 0.6 %copy-done.6 = bf16[8]{0:T(256)(128)(2,1)S(1)} copy-done((bf16[8]{0:T(256)(128)(2,1)S(1)}, bf16[8]{0:T(256)(128)(2,1)}, u32[]{:S(2)}) %copy-start.6) | copy-done | bytes 40
  8.2 0.7 %copy-done.7 = s32[8]{0:T(128)S(1)} copy-done((s32[8]{0:T(128)S(1)}, s32[8]{0:T(128)}, u32[]{:S(2)}) %copy-start.7) | copy-done | bytes 56
  8.8 1.6 %collective-permute-start = (f32[8,3]{0,1:T(4,128)S(1)}, f32[8,3]{0,1:T(4,128)S(1)}, u32[]{:S(2)}, u32[]{:S(2)}) collective-permute-start(f32[8,3]{0,1:T(4,128)S(1)} %pad_maximum_fusion), channel_id=1, source_target_pairs={{0,2},{2,0},{1,3},{3,1},{4,6},{6,4},{5,7},{7,5},{8,10},{10,8},{9,1... | collective-permute-start | bytes 296 | tf_op jit(solution)/shard_map/ppermute | solution.py:249
  10.4 0.0 collective-permute-start.2
  10.4 0.6 %collective-permute-start.1 = (bf16[8,2,16512]{2,1,0:T(2,128)(2,1)}, bf16[8,2,16512]{2,1,0:T(2,128)(2,1)S(1)}, u32[]{:S(2)}, u32[]{:S(2)}) collective-permute-start(bf16[8,2,16512]{2,1,0:T(2,128)(2,1)} %param.7), channel_id=1, source_target_pairs={{0,2},{2,0},{1,3},{3,1},{4,6},{6,4},{5,7},{7,5},{8,10},{10,8},{9,1... | collective-permute-start | bytes 1585160 | tf_op jit(solution)/shard_map/ppermute | solution.py:249
  11.0 0.0 copy-done.4
  11.1 8.3 %collective-permute-done.2 = bf16[4,2,16512]{2,1,0:T(2,128)(2,1)S(1)} collective-permute-done((bf16[4,2,16512]{2,1,0:T(2,128)(2,1)S(1)}, bf16[4,2,16512]{2,1,0:T(2,128)(2,1)S(1)}, u32[]{:S(2)}, u32[]{:S(2)}) %collective-permute-start.2) | collective-permute-done | bytes 264224 | tf_op jit(solution)/shard_map/ppermute | solution.py:245
  19.4 2.2 %fusion.3 = (f32[5,16512]{1,0:T(8,128)S(1)}, f32[5,16512]{1,0:T(8,128)S(1)}) fusion(s32[16512]{0:T(1024)S(1)} %get-tuple-element.15, s32[5]{0:T(128)S(1)} %get-tuple-element.13, s32[16512]{0:T(1024)S(1)} %get-tuple-element.14, s32[5]{0:T(128)S(1)} %get-tuple-element.12), kind=kLoop, calls=%fused_computation.6 | loop fusion | flops 1320960 | bytes 792616 | tf_op jit(solution)/shard_map/sin | solution.py:28
  21.6 0.6 %collective-permute-start.5 = (bf16[2,2,16512]{2,1,0:T(2,128)(2,1)}, bf16[2,2,16512]{2,1,0:T(2,128)(2,1)}, u32[]{:S(2)}, u32[]{:S(2)}) collective-permute-start(bf16[2,2,16512]{2,1,0:T(2,128)(2,1)} %collective-permute-done.4), channel_id=1, source_target_pairs={{0,1},{1,0},{2,3},{3,2},{4,5},{5,4},{6,7},{7,6},{8,9},{9,8},{10,11... | collective-permute-start | bytes 396296 | tf_op jit(solution)/shard_map/ppermute | solution.py:268
  22.2 0.1 pad_add_fusion.refs_0_
  22.3 0.1 pad_maximum_fusion.1
  22.3 0.1 copy.12
  22.4 1.1 %collective-permute-done.5 = bf16[2,2,16512]{2,1,0:T(2,128)(2,1)} collective-permute-done((bf16[2,2,16512]{2,1,0:T(2,128)(2,1)}, bf16[2,2,16512]{2,1,0:T(2,128)(2,1)}, u32[]{:S(2)}, u32[]{:S(2)}) %collective-permute-start.5) | collective-permute-done | bytes 132128 | tf_op jit(solution)/shard_map/ppermute | solution.py:268
  23.5 0.3 collective-permute-done.1
  23.9 19.6 %evidence.1 = (f32[1,128]{1,0:T(1,128)S(1)}, f32[1,128]{1,0:T(1,128)S(1)}) custom-call(s32[4]{0:T(128)S(1)} %pad_add_fusion.refs_0_, f32[32,3]{1,0:T(8,128)S(1)} %bitcast.49, bf16[16,16512]{1,0:T(8,128)(2,1)S(1)} %copy-done.1, f32[5,16512]{1,0:T(8,128)S(1)} %get-tuple-element.11.refs_3_, f32[5,16512]{1,0:T(8,128)S(1)} %get-tuple-element.10.refs_4_, ...), custom_call_target="tpu_custom_call" | custom-call | tf_op jit(solution)/shard_map/evidence/pallas_call | solution.py:283
  43.5 0.5 %copy-done.3 = f32[1,128]{1,0:T(1,128)} copy-done((f32[1,128]{1,0:T(1,128)}, f32[1,128]{1,0:T(1,128)S(1)}, u32[]{:S(2)}) %copy-start.3) | copy-done | bytes 536
  44.1 0.5 %collective-permute-start.6 = (f32[1,128]{1,0:T(1,128)S(1)}, f32[1,128]{1,0:T(1,128)S(1)}, u32[]{:S(2)}, u32[]{:S(2)}) collective-permute-start(f32[1,128]{1,0:T(1,128)S(1)} %get-tuple-element.7), channel_id=1, source_target_pairs={{0,2},{2,0},{1,3},{3,1},{4,6},{6,4},{5,7},{7,5},{8,10},{10,8},{9,1... | collective-permute-start | bytes 1544 | tf_op jit(solution)/shard_map/ppermute | solution.py:249
  44.6 3.0 %collective-permute-done.6.refs_1_ = f32[1,128]{1,0:T(1,128)S(1)} collective-permute-done((f32[1,128]{1,0:T(1,128)S(1)}, f32[1,128]{1,0:T(1,128)S(1)}, u32[]{:S(2)}, u32[]{:S(2)}) %collective-permute-start.6) | collective-permute-done | bytes 544 | tf_op jit(solution)/shard_map/ppermute | solution.py:249
  47.6 0.5 %copy-done.8 = f32[1,128]{1,0:T(1,128)} copy-done((f32[1,128]{1,0:T(1,128)}, f32[1,128]{1,0:T(1,128)S(1)}, u32[]{:S(2)}) %copy-start.8) | copy-done | bytes 536
  48.2 1.2 %finish.1 = (f32[2,8]{1,0:T(2,128)}, f32[1,8]{1,0:T(1,128)}) custom-call(s32[1]{0:T(128)} %bitcast.me, f32[1,128]{1,0:T(1,128)} %copy-done.3, f32[1,128]{1,0:T(1,128)} %copy-done.8), custom_call_target="tpu_custom_call" | custom-call | tf_op jit(solution)/shard_map/finish/pallas_call | solution.py:311
  (24 shorter events, 0.1 us)
Async XLA Ops:
  0.6 9.8 %copy-start = (bf16[1,1,4,2,16512]{4,3,2,1,0:T(2,128)(2,1)S(1)}, bf16[1,1,4,2,16512]{4,3,2,1,0:T(2,128)(2,1)}, u32[]{:S(2)}) copy-start(bf16[1,1,4,2,16512]{4,3,2,1,0:T(2,128)(2,1)} %param.12) | copy-start | bytes 792580
  0.6 6.8 %copy-start.5 = (s32[4,1]{0,1:T(1,128)S(1)}, s32[4,1]{0,1:T(1,128)}, u32[]{:S(2)}) copy-start(s32[4,1]{0,1:T(1,128)} %param.10) | copy-start | bytes 52
  2.4 19.3 %collective-permute-start.4 = (bf16[2,2,16512]{2,1,0:T(2,128)(2,1)}, bf16[2,2,16512]{2,1,0:T(2,128)(2,1)}, u32[]{:S(2)}, u32[]{:S(2)}) collective-permute-start(bf16[2,2,16512]{2,1,0:T(2,128)(2,1)} %dynamic-slice_bitcast_fusion), channel_id=1, source_target_pairs={{0,12},{4,8},{8,4},{12,0},{1,13},{5,9},{9,5},{13,1},{2,14},{6,10},... | collective-permute-start | bytes 396296 | tf_op jit(solution)/shard_map/ppermute | solution.py:255
  7.5 0.7 %copy-start.6 = (bf16[8]{0:T(256)(128)(2,1)S(1)}, bf16[8]{0:T(256)(128)(2,1)}, u32[]{:S(2)}) copy-start(bf16[8]{0:T(256)(128)(2,1)} %param.9) | copy-start | bytes 52
  8.2 0.7 %copy-start.7 = (s32[8]{0:T(128)S(1)}, s32[8]{0:T(128)}, u32[]{:S(2)}) copy-start(s32[8]{0:T(128)} %param.8) | copy-start | bytes 100
  8.8 13.4 %collective-permute-start = (f32[8,3]{0,1:T(4,128)S(1)}, f32[8,3]{0,1:T(4,128)S(1)}, u32[]{:S(2)}, u32[]{:S(2)}) collective-permute-start(f32[8,3]{0,1:T(4,128)S(1)} %pad_maximum_fusion), channel_id=1, source_target_pairs={{0,2},{2,0},{1,3},{3,1},{4,6},{6,4},{5,7},{7,5},{8,10},{10,8},{9,1... | collective-permute-start | bytes 296 | tf_op jit(solution)/shard_map/ppermute | solution.py:249
  10.4 0.7 %copy-start.4 = (s32[5,2]{0,1:T(2,128)S(1)}, s32[5,2]{0,1:T(2,128)}, u32[]{:S(2)}) copy-start(s32[5,2]{0,1:T(2,128)} %param.13) | copy-start | bytes 124
  10.4 9.0 %collective-permute-start.2 = (bf16[4,2,16512]{2,1,0:T(2,128)(2,1)S(1)}, bf16[4,2,16512]{2,1,0:T(2,128)(2,1)S(1)}, u32[]{:S(2)}, u32[]{:S(2)}) collective-permute-start(bf16[4,2,16512]{2,1,0:T(2,128)(2,1)S(1)} %bitcast.43), channel_id=1, source_target_pairs={{0,4},{1,9},{4,0},{5,13},{8,12},{9,1},{12,8},{13,5},{2,6},{3,11},{... | collective-permute-start | bytes 792584 | tf_op jit(solution)/shard_map/ppermute | solution.py:245
  10.4 13.5 %collective-permute-start.1 = (bf16[8,2,16512]{2,1,0:T(2,128)(2,1)}, bf16[8,2,16512]{2,1,0:T(2,128)(2,1)S(1)}, u32[]{:S(2)}, u32[]{:S(2)}) collective-permute-start(bf16[8,2,16512]{2,1,0:T(2,128)(2,1)} %param.7), channel_id=1, source_target_pairs={{0,2},{2,0},{1,3},{3,1},{4,6},{6,4},{5,7},{7,5},{8,10},{10,8},{9,1... | collective-permute-start | bytes 1585160 | tf_op jit(solution)/shard_map/ppermute | solution.py:249
  19.4 4.1 %collective-permute-start.3 = (bf16[4,2,16512]{2,1,0:T(2,128)(2,1)S(1)}, bf16[4,2,16512]{2,1,0:T(2,128)(2,1)S(1)}, u32[]{:S(2)}, u32[]{:S(2)}) collective-permute-start(bf16[4,2,16512]{2,1,0:T(2,128)(2,1)S(1)} %collective-permute-done.2), channel_id=1, source_target_pairs={{0,1},{1,0},{2,3},{3,2},{4,5},{5,4},{6,7},{7,6},{8,9},{9,8},{10,11... | collective-permute-start | bytes 792584 | tf_op jit(solution)/shard_map/ppermute | solution.py:267
  19.4 4.4 %copy-start.1 = (bf16[16,16512]{1,0:T(8,128)(2,1)S(1)}, bf16[16,16512]{1,0:T(8,128)(2,1)}, u32[]{:S(2)}) copy-start(bf16[16,16512]{1,0:T(8,128)(2,1)} %refs_2_.1) | copy-start | bytes 1585156
  19.4 4.4 %copy-start.2 = (bf16[8,2,16512]{2,1,0:T(2,128)(2,1)S(1)}, bf16[8,2,16512]{2,1,0:T(2,128)(2,1)}, u32[]{:S(2)}) copy-start(bf16[8,2,16512]{2,1,0:T(2,128)(2,1)} %param.7) | copy-start | bytes 1585156
  21.6 1.9 %collective-permute-start.5 = (bf16[2,2,16512]{2,1,0:T(2,128)(2,1)}, bf16[2,2,16512]{2,1,0:T(2,128)(2,1)}, u32[]{:S(2)}, u32[]{:S(2)}) collective-permute-start(bf16[2,2,16512]{2,1,0:T(2,128)(2,1)} %collective-permute-done.4), channel_id=1, source_target_pairs={{0,1},{1,0},{2,3},{3,2},{4,5},{5,4},{6,7},{7,6},{8,9},{9,8},{10,11... | collective-permute-start | bytes 396296 | tf_op jit(solution)/shard_map/ppermute | solution.py:268
  43.5 0.5 %copy-start.3 = (f32[1,128]{1,0:T(1,128)}, f32[1,128]{1,0:T(1,128)S(1)}, u32[]{:S(2)}) copy-start(f32[1,128]{1,0:T(1,128)S(1)} %get-tuple-element.6.refs_0_) | copy-start | bytes 1540
  44.1 3.6 %collective-permute-start.6 = (f32[1,128]{1,0:T(1,128)S(1)}, f32[1,128]{1,0:T(1,128)S(1)}, u32[]{:S(2)}, u32[]{:S(2)}) collective-permute-start(f32[1,128]{1,0:T(1,128)S(1)} %get-tuple-element.7), channel_id=1, source_target_pairs={{0,2},{2,0},{1,3},{3,1},{4,6},{6,4},{5,7},{7,5},{8,10},{10,8},{9,1... | collective-permute-start | bytes 1544 | tf_op jit(solution)/shard_map/ppermute | solution.py:249
  47.6 0.5 %copy-start.8 = (f32[1,128]{1,0:T(1,128)}, f32[1,128]{1,0:T(1,128)S(1)}, u32[]{:S(2)}) copy-start(f32[1,128]{1,0:T(1,128)S(1)} %collective-permute-done.6.refs_1_) | copy-start | bytes 1540

commit v2 on v0

v2 whole, which is shorter than its diff:
```python
import functools
import math

import jax
import jax.numpy as jnp
from jax import lax
from jax.experimental import pallas as pl
from jax.experimental.pallas import tpu as pltpu
from jax.sharding import PartitionSpec as P


BOX = 256
KX = 129
KY = 128

EPSILON = 1e-06
LANES = 128
UNROLL = 43
SET = 4
F32 = jnp.float32
BF16 = jnp.bfloat16
CONTRACT_LAST = (((1,), (1,)), ((), ()))


def lane(k, width=LANES):
    return pl.ds(pl.multiple_of(k * width, LANES), width)


def iota(shape, axis):
    return lax.broadcasted_iota(jnp.int32, shape, axis)


def row_copies(source, target, sem, start=0):
    return [
        pltpu.make_async_copy(
            source.at[i], target.at[start + 2 * i : start + 2 * i + 2], sem
        )
        for i in range(source.shape[0])
    ]


def weigh_kernel(dims, codes_in, beta_in, groups_in, particles, ctf_in, refs, out, part,
                 codes, beta, groups, ctf, raw, rows_ctf, sem, half_sem, small_sem):
    rows, per_block, n_codes, tiles, sig = dims
    half = part.shape[0]
    small = [
        pltpu.make_async_copy(codes_in, codes, small_sem.at[0]),
        pltpu.make_async_copy(groups_in, groups, small_sem.at[1]),
        pltpu.make_async_copy(ctf_in, ctf, small_sem.at[2]),
        pltpu.make_async_copy(beta_in, beta, small_sem.at[3]),
    ]
    for copy in small:
        copy.start()
    copies = row_copies(particles, raw, sem)
    for copy in copies:
        copy.start()
    half_copy = pltpu.make_async_copy(refs.at[pl.ds(lax.axis_index("dom") * half, half)], part, half_sem)
    half_copy.start()
    shape = (2 * rows, LANES)
    owner = iota(shape, 0) // 2
    column = iota(shape, 1)
    for copy in small:
        copy.wait()
    noise = beta[...].astype(F32)
    noise = jnp.where(iota((2 * rows, rows), 0) // 2 == iota((2 * rows, rows), 1), noise, 0.0)
    extra = jnp.where(column == 1, jnp.sum(noise, axis=1, keepdims=True), 0.0)
    code = jnp.zeros(shape, jnp.int32)
    for p in range(rows):
        mine = owner == p
        code = jnp.where(mine, codes[p], code)
        for s in range(sig):
            group = groups[s, p // per_block].astype(F32)
            extra = jnp.where(mine & (column == 2 + s), group, extra)
    extra = jnp.where(column == 0, code.astype(F32), extra)
    pick = (code[:, :n_codes] == column[:, :n_codes]).astype(BF16)
    rows_ctf[...] = jnp.dot(pick, ctf[...], preferred_element_type=F32)
    for copy in copies:
        copy.wait()

    def step(k, power):
        value = raw[:, lane(k)].astype(F32)
        out[:, lane(k)] = (rows_ctf[:, lane(k)] * value).astype(BF16)
        return power + value * value

    power = lax.fori_loop(0, tiles, step, jnp.zeros(shape, F32), unroll=UNROLL)
    power = jnp.sum(power, axis=1, keepdims=True)
    for s in range(3):
        term = power.astype(BF16).astype(F32)
        extra = jnp.where(column == 2 + sig + s, term, extra)
        power = power - term
    out[:, tiles * LANES :] = extra.astype(BF16)
    half_copy.wait()


def up(value, to):
    return -(-value // to) * to


def prepare_kernel(tiles, images, ctf_in, offsets_in, lhs, cosines, sines, ctf, offsets, sem, small_sem):
    load = pltpu.make_async_copy(ctf_in, ctf, sem)
    load.start()
    small = pltpu.make_async_copy(offsets_in, offsets, small_sem)
    small.start()
    rows, codes = images.shape[0], ctf.shape[0]
    shape = cosines.shape[:1] + (LANES,)
    row, place = iota(shape, 0), iota(shape, 1)
    small.wait()
    step_x = jnp.zeros(shape, jnp.int32)
    step_y = jnp.zeros(shape, jnp.int32)
    for t in range(offsets.shape[1]):
        step_x = jnp.where(row == t, offsets[0, t], step_x)
        step_y = jnp.where(row == t, offsets[1, t], step_y)
    base = step_x * place - step_y * (KY // 2)
    slope = step_y - step_x
    wrapped = step_x * KX - step_y
    load.wait()

    def step(k, carry):
        lhs[:rows, lane(k)] = images[:, lane(k)]
        value = ctf[:, lane(k)].astype(F32)
        square = value * value
        high = square.astype(BF16)
        lhs[rows : rows + codes, lane(k)] = high
        lhs[rows + codes :, lane(k)] = (square - high.astype(F32)).astype(BF16)
        turn = (base + slope * k + jnp.where(place < k, wrapped, 0)) & (BOX - 1)
        quarter = (turn + BOX // 8) >> 6
        x = (turn - (quarter << 6)).astype(F32) * (2.0 * math.pi / BOX)
        x2 = x * x
        sin = x + x * x2 * (
            -1.6666654611e-1 + x2 * (8.3321608736e-3 + x2 * -1.9515295891e-4)
        )
        cos = (1.0 - 0.5 * x2) + x2 * x2 * (
            4.166664568298827e-2 + x2 * (-1.388731625493765e-3 + x2 * 2.443315711809948e-5)
        )
        swap = (quarter & 1) == 1
        first = jnp.where(swap, sin, cos)
        second = jnp.where(swap, cos, sin)
        cosines[:, lane(k)] = jnp.where(((quarter + 1) & 2) == 2, -first, first)
        sines[:, lane(k)] = jnp.where((quarter & 2) == 2, -second, second)
        return carry

    lax.fori_loop(0, tiles, step, 0, unroll=UNROLL)


def shift_rows(raw, cosines, sines, table, shifts, tiles):
    n = raw.shape[0]
    odd = iota((n, LANES), 0) % 2 == 1

    def step(k, carry):
        value = raw[:, lane(k)].astype(F32)
        turned = jnp.where(odd, -pltpu.roll(value, 1, 0), pltpu.roll(value, n - 1, 0))
        parts = [
            value * cosines[t : t + 1, lane(k)] + turned * sines[t : t + 1, lane(k)]
            for t in range(shifts)
        ]
        square = value * value
        high = square.astype(BF16).astype(F32)
        parts += [high, square - high]
        for i in range(0, len(parts), 2):
            both = jnp.concatenate(parts[i : i + 2], axis=0)
            table[n * i : n * i + both.shape[0], lane(k)] = both.astype(BF16)
        return carry

    lax.fori_loop(0, tiles, step, 0, unroll=UNROLL)


def tables_kernel(shifts, tiles, lhs, cosines, sines, *refs):
    pieces = refs[:-4]
    table, product, raw, sem = refs[-4:]
    n = raw.shape[0]
    copies = []
    for i, piece in enumerate(pieces):
        copies += row_copies(piece, raw, sem, i * n // len(pieces))
    for copy in copies:
        copy.start()
    for copy in copies:
        copy.wait()
    shift_rows(raw, cosines, sines, table, shifts, tiles)
    product[...] = lax.dot_general(
        table[...], lhs[...], CONTRACT_LAST, preferred_element_type=F32
    )


def last_kernel(dims, *refs):
    n_img, steps, shifts, tiles, sig, n = dims
    count = len(steps)
    refs = list(refs)
    z, d = lax.axis_index("orient"), lax.axis_index("dom")
    images = [refs.pop(0) for _ in range(n_img)]
    tables = [refs.pop(0) for _ in range(count)]
    products = [refs.pop(0) for _ in range(count)]
    outs = refs
    pixels = tiles * LANES
    rows = images[0].shape[0]
    codes = (products[0].shape[1] - rows) // 2
    total_rows = n_img * rows
    used = up(shifts * n, 16)

    others = []
    if n_img > 1:
        stacked = jnp.concatenate([table[:used, :] for table in tables], axis=0)
    for image in images[1:]:
        others.append(
            lax.dot_general(
                stacked, image[:, :pixels], CONTRACT_LAST, preferred_element_type=F32
            )
        )
    extra = jnp.concatenate([image[:, pixels:] for image in images], axis=0)
    take = (iota((16, LANES), 0) == iota((16, LANES), 1)).astype(BF16)
    turned = lax.dot_general(take, extra, CONTRACT_LAST, preferred_element_type=F32)
    beta = turned[1:2]
    power = turned[2 + sig : 3 + sig] + turned[3 + sig : 4 + sig] + turned[4 + sig : 5 + sig]
    power = power + pltpu.roll(power, total_rows - 1, 1)
    column = iota((total_rows, 6 * codes), 1)
    pick = (extra[:, 0:1].astype(F32).astype(jnp.int32) == column % codes).astype(BF16)
    squares = jnp.concatenate(
        [product[shifts * n : (shifts + 2) * n, rows:] for product in products], axis=0
    )
    terms = []
    for _ in range(3):
        term = squares.astype(BF16)
        terms.append(term)
        squares = squares - term.astype(F32)
    energies = lax.dot_general(
        jnp.concatenate(terms, axis=1), pick, CONTRACT_LAST, preferred_element_type=F32
    )

    even_row = iota((n, total_rows), 0) % 2 == 0
    same = (iota((n, total_rows), 0) % 2) == (iota((n, total_rows), 1) % 2)
    evidence = jnp.zeros((n, total_rows), F32)
    for c in range(count):
        energy = energies[2 * c * n : (2 * c + 1) * n] + energies[(2 * c + 1) * n : (2 * c + 2) * n]
        energy = energy + pltpu.roll(energy, n - 1, 0)
        scale = beta / jnp.sqrt(power * energy + EPSILON)
        cross = [products[c][: shifts * n, :rows]]
        cross += [other[c * used : c * used + shifts * n] for other in others]
        cross = jnp.concatenate(cross, axis=1) if len(cross) > 1 else cross[0]
        total = jnp.zeros((n, total_rows), F32)
        for t in range(shifts):
            value = jnp.where(same, cross[t * n : (t + 1) * n], 0.0)
            value = value + pltpu.roll(value, n - 1, 0)
            value = value + pltpu.roll(value, total_rows - 1, 1)
            total = total + jnp.exp(jnp.where(same & even_row, value * scale, 0.0))
        gid = (z ^ jnp.where(d == 0, *steps[c])).astype(F32)
        named = turned[2:3] == gid
        for s in range(1, sig):
            named = named | (turned[2 + s : 3 + s] == gid)
        evidence = evidence + jnp.where(even_row & named, total, 0.0)
    evidence = jnp.sum(evidence, axis=0, keepdims=True)
    spread = jnp.concatenate(
        [evidence, jnp.zeros((1, LANES - total_rows % LANES), F32)], axis=1
    ) if total_rows % LANES else evidence
    for i in range(n_img):
        here = spread if i == 0 else pltpu.roll(spread, LANES - i * rows, 1)
        outs[i][...] = jnp.where(iota((1, LANES), 1) < rows, here, 1.0)


def finish_kernel(rows, *refs):
    n_cls = len(refs) - 2
    post, log_out = refs[-2:]
    x = lax.axis_index("cls")
    place = iota((1, LANES), 1)
    used = (place % 2 == 0) & (place < 2 * rows)
    found = [jnp.where(used, r[...], 1.0) for r in refs[:n_cls]]
    total = found[0]
    for value in found[1:]:
        total = total + value
    row = iota((n_cls, LANES), 0)
    table = jnp.zeros((n_cls, LANES), F32)
    for k in range(n_cls):
        table = jnp.where(row == (x ^ k), found[k], table)
    squeeze = (iota((LANES, rows), 0) == 2 * iota((LANES, rows), 1)).astype(F32)
    both = jnp.concatenate([table / total, jnp.log(total)], axis=0)
    both = jnp.dot(both, squeeze, precision=lax.Precision.HIGHEST, preferred_element_type=F32)
    post[...] = both[:n_cls]
    log_out[...] = both[n_cls:]


def local(particles, ctf_index, beta, significant, ctf_table, references, offsets):
    groups = lax.axis_size("orient")
    n_cls = lax.axis_size("cls")
    cores = lax.axis_size("dom")
    blocks, sig = significant.shape
    rows, _, pixels = particles.shape
    per_block = rows // blocks
    codes = ctf_table.shape[0]
    oris = references.shape[2]
    shifts = offsets.shape[0]
    tiles = pixels // LANES
    refs_own = references.reshape(oris, 2, pixels)
    steps = list(range(1, groups))
    anywhere = pl.BlockSpec(memory_space=pl.ANY)
    vmem = pl.BlockSpec(memory_space=pltpu.VMEM)
    hbm = pl.BlockSpec(memory_space=pltpu.HBM)
    dma = pltpu.SemaphoreType.DMA

    def in_hbm(values):
        return pltpu.with_memory_space_constraint(values, pltpu.HBM)

    def core_step(first, second):
        pairs = []
        for a in range(groups):
            for core in range(cores):
                step = second if core else first
                pairs.append((a * cores + core, (a ^ step) * cores + core))
        return pairs

    swap = [(c, cores - 1 - c) for c in range(cores)]
    direct, order = [], []
    while len(steps) > 1:
        first, second = steps.pop(0), steps.pop(0)
        direct.append(
            lax.ppermute(refs_own, ("orient", "dom"), core_step(first, second))
        )
        order.append((first, second))
    last = steps.pop(0)

    def across(values, k):
        return lax.ppermute(values, "cls", [(c, c ^ k) for c in range(n_cls)])

    half = oris // 2
    weighted, part = pl.pallas_call(
        functools.partial(weigh_kernel, (rows, per_block, codes, tiles, sig)),
        name="weigh",
        out_shape=[
            jax.ShapeDtypeStruct((2 * rows, pixels + LANES), BF16),
            jax.ShapeDtypeStruct((half, 2, pixels), BF16),
        ],
        in_specs=[hbm, hbm, hbm, hbm, hbm, hbm],
        out_specs=[vmem, vmem],
        scratch_shapes=[
            pltpu.SMEM((rows,), jnp.int32),
            pltpu.VMEM((1, rows), BF16),
            pltpu.SMEM((sig, blocks), jnp.int32),
            pltpu.VMEM((codes, pixels), BF16),
            pltpu.VMEM((2 * rows, pixels), BF16),
            pltpu.VMEM((2 * rows, pixels), F32),
            dma,
            dma,
            dma((4,)),
        ],
        compiler_params=pltpu.CompilerParams(vmem_limit_bytes=16 << 20),
    )(
        in_hbm(ctf_index),
        in_hbm(beta[None]),
        in_hbm(significant.T),
        in_hbm(particles),
        in_hbm(ctf_table),
        in_hbm(refs_own),
    )
    images = [weighted]
    for k in range(1, n_cls):
        images.append(across(weighted, k))
    near_half = lax.ppermute(part, "orient", [(a, a ^ last) for a in range(groups)])
    lhs_rows = 2 * rows + 2 * codes
    phase_shape = jax.ShapeDtypeStruct((up(shifts, 8), pixels), F32)
    lhs, cosines, sines = pl.pallas_call(
        functools.partial(prepare_kernel, tiles),
        name="prepare",
        out_shape=[
            jax.ShapeDtypeStruct((lhs_rows, pixels), BF16),
            phase_shape,
            phase_shape,
        ],
        in_specs=[vmem, hbm, hbm],
        out_specs=[vmem, vmem, vmem],
        scratch_shapes=[
            pltpu.VMEM((codes, pixels), BF16),
            pltpu.SMEM((2, shifts), jnp.int32),
            dma,
            dma,
        ],
        compiler_params=pltpu.CompilerParams(vmem_limit_bytes=16 << 20),
    )(weighted, in_hbm(ctf_table), in_hbm(offsets.T))
    n = 2 * oris
    n_img = len(images)

    used = (shifts + 2) * n

    def make_table(*pieces):
        return pl.pallas_call(
            functools.partial(tables_kernel, shifts, tiles),
            name="tables",
            out_shape=[
                jax.ShapeDtypeStruct((used, pixels), BF16),
                jax.ShapeDtypeStruct((used, lhs_rows), F32),
            ],
            in_specs=[vmem, vmem, vmem] + [anywhere] * len(pieces),
            out_specs=[vmem, vmem],
            scratch_shapes=[pltpu.VMEM((n, pixels), BF16), dma],
            compiler_params=pltpu.CompilerParams(vmem_limit_bytes=12 << 20),
        )(lhs, cosines, sines, *pieces)

    def evaluate(group):
        steps, tables, products = zip(*group)
        return pl.pallas_call(
            functools.partial(last_kernel, (n_img, steps, shifts, tiles, sig, n)),
            name="last",
            out_shape=[jax.ShapeDtypeStruct((1, LANES), F32)] * n_img,
            in_specs=[vmem] * (n_img + 2 * len(group)),
            out_specs=[vmem] * n_img,
            compiler_params=pltpu.CompilerParams(
                vmem_limit_bytes=(12 << 20) if n_img < 4 else (40 << 20)
            ),
        )(*images, *tables, *products)

    made = [((0, 0), *make_table(in_hbm(refs_own)))]
    for (first, second), near in zip(order, direct):
        mate = lax.ppermute(near, "dom", swap)
        made.append(((first, second), *make_table(near)))
        made.append(((second, first), *make_table(mate)))
    far_half = lax.ppermute(near_half, "dom", swap)
    made.append(((last, last), *make_table(near_half, far_half)))
    found = [evaluate(made[i : i + SET]) for i in range(0, len(made), SET)]
    evidence = found[0]
    for more in found[1:]:
        evidence = [a + b for a, b in zip(evidence, more)]
    gathered = [evidence[0]] + [across(evidence[k], k) for k in range(1, n_cls)]
    post, log_total = pl.pallas_call(
        functools.partial(finish_kernel, rows),
        name="finish",
        out_shape=[
            jax.ShapeDtypeStruct((n_cls, rows), F32),
            jax.ShapeDtypeStruct((1, rows), F32),
        ],
        in_specs=[vmem] * n_cls,
        out_specs=[vmem, vmem],
        compiler_params=pltpu.CompilerParams(vmem_limit_bytes=8 << 20),
    )(*gathered)
    return (post.T, log_total.reshape(rows))


def solution(mesh):
    placed = (
        P(("groups", "orient", "cls", "dom"), None, None),
        P(("groups", "orient", "cls", "dom")),
        P(("groups", "orient", "cls", "dom")),
        P(("groups", "orient", "cls", "dom"), None),
        P(),
        P(("groups", "cls"), "orient", None, None, None),
        P("groups", None),
    )

    return jax.shard_map(
        local,
        mesh=mesh,
        in_specs=placed,
        out_specs=(
            P(("groups", "orient", "cls", "dom"), None),
            P(("groups", "orient", "cls", "dom")),
        ),
        check_vma=False,
    )
```

time: 75.5 us -> 34 us (0.45)
  blocking collectives: 16.6 us -> 0 us
  Pallas kernels: 0 us -> 13.5 us
  other arithmetic: 13.5 us -> 0 us
  matrix products: 10.1 us -> 0 us
  waiting for transfers between devices: 16.2 us -> 7.67 us
  local copies, waits for them, and re-layouts: 6.68 us -> 0 us
    all_to_all x2 -> x0, waiting for transfers between devices: 16.2 us -> none  [the longest x1 16.2 us: local(): lax.all_to_all(outgoing[0], 'orient', split_axis=0, concat_axis=0, tiled=...]
    pallas_call x0 -> x8, Pallas kernels: none -> 13.5 us  [the longest x4 6.56 us: make_table(): pl.pallas_call(functools.partial(tables_kernel, shifts, tiles), name='tab...]
    ppermute x0 -> x6, starting transfers between devices: none -> 11.9 us  [the longest x1 4.35 us: local(): mate = lax.ppermute(near, 'dom', swap)]
    all_to_all x2 -> x0, starting transfers between devices: 11.2 us -> none  [the longest x1 6.35 us: local(): lax.all_to_all(outgoing[1], 'orient', split_axis=0, concat_axis=0, tiled=...]
    dot_general x10 -> x0, matrix products: 10.1 us -> none  [the longest x2 4.82 us: class_evidence(): lax.dot_general(weighted, shifted, (((1,), (1,)), ((), ())), preferred_el...]
    all_gather x1 -> x0, blocking collectives: 8.47 us -> none  [local(): every_class = lax.all_gather(references, 'cls', axis=0, tiled=True)]
    all_to_all x1 -> x0, blocking collectives: 8.11 us -> none  [local(): lax.all_to_all(shaped, 'orient', split_axis=0, concat_axis=0, tiled=True)]
    ppermute x0 -> x6, waiting for transfers between devices: none -> 7.67 us  [the longest x1 4.58 us: local(): lax.ppermute(refs_own, ('orient', 'dom'), core_step(first, second))]
  transfers between devices with their start and end apart: 2 -> 6, of which waited for: 1 -> 2; matrix products, arithmetic and copies ran while one was open for 21% -> 0% of each run, Pallas kernels for 0% -> 25%
where the time goes in v2:
time: 34 us; the launch traced here: 33.8 us
  Pallas kernels  13.5 us (40%)
  starting transfers between devices  11.9 us (35%)
  waiting for transfers between devices  7.67 us (23%)
  between operations  0.71 us (2%)
    pallas_call x4, Pallas kernels, make_table(): pl.pallas_call(functools.partial(tables_kernel, shifts, tiles), name='tab...  6.56 us
    ppermute x1, waiting for transfers between devices, local(): lax.ppermute(refs_own, ('orient', 'dom'), core_step(first, second))  4.58 us
    ppermute x1, starting transfers between devices, local(): mate = lax.ppermute(near, 'dom', swap)  4.35 us
    ppermute x2, starting transfers between devices, across(): return lax.ppermute(values, 'cls', [(c, c ^ k) for c in range(n_cls)])  3.52 us
    ppermute x2, waiting for transfers between devices, across(): return lax.ppermute(values, 'cls', [(c, c ^ k) for c in range(n_cls)])  3.08 us
    ppermute x1, starting transfers between devices, local(): lax.ppermute(part, 'orient', [(a, a ^ last) for a in range(groups)])  2.48 us
    pallas_call x1, Pallas kernels, evaluate(): pl.pallas_call(functools.partial(last_kernel, (n_img, steps, shifts, tile...  2.15 us
    pallas_call x1, Pallas kernels, local(): pl.pallas_call(functools.partial(prepare_kernel, tiles), name='prepare',...  2.04 us
  transfers between devices with their start and end apart: 6, of which 2 were waited for; matrix products, arithmetic and copies ran while one was open for 0% of the time, Pallas kernels for 25%

profile of v2, /device:TPU:0, one launch (start us, length us, event | category | flops | bytes accessed | tf_op | source)
XLA Modules:
  0.0 33.8 jit_solution(14726332612188238378)
XLA Ops:
  0.6 2.0 %weigh.1 = (bf16[16,16640]{1,0:T(8,128)(2,1)S(1)}, bf16[2,2,16512]{2,1,0:T(2,128)(2,1)S(1)}) custom-call(s32[8]{0:T(128)} %codes_in.1, bf16[1,8]{1,0:T(2,128)(2,1)} %bitcast.10, s32[1,4]{1,0:T(1,128)} %bitcast.11, bf16[8,2,16512]{2,1,0:T(2,128)(2,1)} %particles.1, bf16[16,16512]{1,0:T(8,128)(2,1)} %ctf_in.3, bf16[4,2,16512]{2,1,0:T(2,128)(2,1)} %bitcast.6), custom_call_target="tpu_custom_call" | custom-call | tf_op jit(solution)/shard_map/weigh/pallas_call | solution.py:322
  2.7 3.0 %collective-permute-start = (bf16[16,16640]{1,0:T(8,128)(2,1)S(1)}, bf16[16,16640]{1,0:T(8,128)(2,1)S(1)}, u32[]{:S(2)}, u32[]{:S(2)}) collective-permute-start(bf16[16,16640]{1,0:T(8,128)(2,1)S(1)} %get-tuple-element.19.images.refs_0_), channel_id=1, source_target_pairs={{0,2},{2,0},{1,3},{3,1},{4,6},{6,4},{5,7},{7,5},{8,10},{10,8},{9,1... | collective-permute-start | bytes 1597448 | tf_op jit(solution)/shard_map/ppermute | solution.py:319
  5.7 1.6 %collective-permute-start.1 = (bf16[4,2,16512]{2,1,0:T(2,128)(2,1)}, bf16[4,2,16512]{2,1,0:T(2,128)(2,1)S(1)}, u32[]{:S(2)}, u32[]{:S(2)}) collective-permute-start(bf16[4,2,16512]{2,1,0:T(2,128)(2,1)} %bitcast.7), channel_id=1, source_target_pairs={{0,4},{1,9},{4,0},{5,13},{8,12},{9,1},{12,8},{13,5},{2,6},{3,11},{... | collective-permute-start | bytes 792584 | tf_op jit(solution)/shard_map/ppermute | solution.py:313
  7.3 2.5 %collective-permute-start.3 = (bf16[2,2,16512]{2,1,0:T(2,128)(2,1)S(1)}, bf16[2,2,16512]{2,1,0:T(2,128)(2,1)S(1)}, u32[]{:S(2)}, u32[]{:S(2)}) collective-permute-start(bf16[2,2,16512]{2,1,0:T(2,128)(2,1)S(1)} %get-tuple-element.26), channel_id=1, source_target_pairs={{0,12},{4,8},{8,4},{12,0},{1,13},{5,9},{9,5},{13,1},{2,14},{6,10},... | collective-permute-start | bytes 396296 | tf_op jit(solution)/shard_map/ppermute | solution.py:354
  9.7 4.6 %collective-permute-done.1.refs_0_ = bf16[4,2,16512]{2,1,0:T(2,128)(2,1)S(1)} collective-permute-done((bf16[4,2,16512]{2,1,0:T(2,128)(2,1)}, bf16[4,2,16512]{2,1,0:T(2,128)(2,1)S(1)}, u32[]{:S(2)}, u32[]{:S(2)}) %collective-permute-start.1) | collective-permute-done | bytes 264224 | tf_op jit(solution)/shard_map/ppermute | solution.py:313
  14.3 4.4 %collective-permute-start.2 = (bf16[4,2,16512]{2,1,0:T(2,128)(2,1)S(1)}, bf16[4,2,16512]{2,1,0:T(2,128)(2,1)S(1)}, u32[]{:S(2)}, u32[]{:S(2)}) collective-permute-start(bf16[4,2,16512]{2,1,0:T(2,128)(2,1)S(1)} %collective-permute-done.1.refs_0_), channel_id=1, source_target_pairs={{0,1},{1,0},{2,3},{3,2},{4,5},{5,4},{6,7},{7,6},{8,9},{9,8},{10,11... | collective-permute-start | bytes 792584 | tf_op jit(solution)/shard_map/ppermute | solution.py:409
  18.7 0.0 collective-permute-done.3.refs_0_
  18.7 0.0 collective-permute-start.4
  18.7 2.0 %prepare.1 = (bf16[48,16512]{1,0:T(8,128)(2,1)S(1)}, f32[8,16512]{1,0:T(8,128)S(1)}, f32[8,16512]{1,0:T(8,128)S(1)}) custom-call(bf16[16,16640]{1,0:T(8,128)(2,1)S(1)} %get-tuple-element.19.images.refs_0_, bf16[16,16512]{1,0:T(8,128)(2,1)} %ctf_in.3, s32[2,5]{1,0:T(2,128)} %bitcast.9), custom_call_target="tpu_custom_call" | custom-call | tf_op jit(solution)/shard_map/prepare/pallas_call | solution.py:357
  20.7 2.2 %tables.4 = (bf16[56,16512]{1,0:T(8,128)(2,1)S(1)}, f32[56,48]{1,0:T(8,128)S(1)}) custom-call(bf16[48,16512]{1,0:T(8,128)(2,1)S(1)} %get-tuple-element.20.lhs, f32[8,16512]{1,0:T(8,128)S(1)} %get-tuple-element.21.cosines, f32[8,16512]{1,0:T(8,128)S(1)} %get-tuple-element.22.sines, bf16[4,2,16512]{2,1,0:T(2,128)(2,1)} %bitcast.8), custom_call_target="tpu_custom_call" | custom-call | tf_op jit(solution)/shard_map/tables/pallas_call | solution.py:381
  23.0 1.4 %tables.5 = (bf16[56,16512]{1,0:T(8,128)(2,1)S(1)}, f32[56,48]{1,0:T(8,128)S(1)}) custom-call(bf16[48,16512]{1,0:T(8,128)(2,1)S(1)} %get-tuple-element.20.lhs, f32[8,16512]{1,0:T(8,128)S(1)} %get-tuple-element.21.cosines, f32[8,16512]{1,0:T(8,128)S(1)} %get-tuple-element.22.sines, bf16[4,2,16512]{2,1,0:T(2,128)(2,1)S(1)} %collective-permute-done.1.refs_0_), custom_call_target="tpu_custom_call" | custom-call | tf_op jit(solution)/shard_map/tables/pallas_call | solution.py:381
  24.4 0.0 collective-permute-done.4.refs_1_
  24.4 1.4 %tables.7 = (bf16[56,16512]{1,0:T(8,128)(2,1)S(1)}, f32[56,48]{1,0:T(8,128)S(1)}) custom-call(bf16[48,16512]{1,0:T(8,128)(2,1)S(1)} %get-tuple-element.20.lhs, f32[8,16512]{1,0:T(8,128)S(1)} %get-tuple-element.21.cosines, f32[8,16512]{1,0:T(8,128)S(1)} %get-tuple-element.22.sines, bf16[2,2,16512]{2,1,0:T(2,128)(2,1)S(1)} %collective-permute-done.3.refs_0_, ...), custom_call_target="tpu_custom_call" | custom-call | tf_op jit(solution)/shard_map/tables/pallas_call | solution.py:381
  25.9 0.0 collective-permute-done.2.refs_0_
  25.9 1.4 %tables.6 = (bf16[56,16512]{1,0:T(8,128)(2,1)S(1)}, f32[56,48]{1,0:T(8,128)S(1)}) custom-call(bf16[48,16512]{1,0:T(8,128)(2,1)S(1)} %get-tuple-element.20.lhs, f32[8,16512]{1,0:T(8,128)S(1)} %get-tuple-element.21.cosines, f32[8,16512]{1,0:T(8,128)S(1)} %get-tuple-element.22.sines, bf16[4,2,16512]{2,1,0:T(2,128)(2,1)S(1)} %collective-permute-done.2.refs_0_), custom_call_target="tpu_custom_call" | custom-call | tf_op jit(solution)/shard_map/tables/pallas_call | solution.py:381
  27.3 0.0 collective-permute-done.refs_1_
  27.3 2.1 %last.1 = (f32[1,128]{1,0:T(1,128)S(1)}, f32[1,128]{1,0:T(1,128)S(1)}) custom-call(bf16[16,16640]{1,0:T(8,128)(2,1)S(1)} %get-tuple-element.19.images.refs_0_, bf16[16,16640]{1,0:T(8,128)(2,1)S(1)} %collective-permute-done.refs_1_, bf16[56,16512]{1,0:T(8,128)(2,1)S(1)} %get-tuple-element.23.refs_2_, bf16[56,16512]{1,0:T(8,128)(2,1)S(1)} %get-tuple-element.24.refs_3_, ...), custom_call_target="tpu_custom_call" | custom-call | tf_op jit(solution)/shard_map/last/pallas_call | solution.py:396
  29.5 0.5 %collective-permute-start.5 = (f32[1,128]{1,0:T(1,128)S(1)}, f32[1,128]{1,0:T(1,128)S(1)}, u32[]{:S(2)}, u32[]{:S(2)}) collective-permute-start(f32[1,128]{1,0:T(1,128)S(1)} %get-tuple-element.33), channel_id=1, source_target_pairs={{0,2},{2,0},{1,3},{3,1},{4,6},{6,4},{5,7},{7,5},{8,10},{10,8},{9,1... | collective-permute-start | bytes 1544 | tf_op jit(solution)/shard_map/ppermute | solution.py:319
  30.0 3.1 %collective-permute-done.5.refs_1_ = f32[1,128]{1,0:T(1,128)S(1)} collective-permute-done((f32[1,128]{1,0:T(1,128)S(1)}, f32[1,128]{1,0:T(1,128)S(1)}, u32[]{:S(2)}, u32[]{:S(2)}) %collective-permute-start.5) | collective-permute-done | bytes 544 | tf_op jit(solution)/shard_map/ppermute | solution.py:319
  33.1 0.7 %finish.1 = (f32[2,8]{1,0:T(2,128)}, f32[1,8]{1,0:T(1,128)}) custom-call(f32[1,128]{1,0:T(1,128)S(1)} %get-tuple-element.32.refs_0_, f32[1,128]{1,0:T(1,128)S(1)} %collective-permute-done.5.refs_1_), custom_call_target="tpu_custom_call" | custom-call | tf_op jit(solution)/shard_map/finish/pallas_call | solution.py:419
Async XLA Ops:
  2.7 24.7 %collective-permute-start = (bf16[16,16640]{1,0:T(8,128)(2,1)S(1)}, bf16[16,16640]{1,0:T(8,128)(2,1)S(1)}, u32[]{:S(2)}, u32[]{:S(2)}) collective-permute-start(bf16[16,16640]{1,0:T(8,128)(2,1)S(1)} %get-tuple-element.19.images.refs_0_), channel_id=1, source_target_pairs={{0,2},{2,0},{1,3},{3,1},{4,6},{6,4},{5,7},{7,5},{8,10},{10,8},{9,1... | collective-permute-start | bytes 1597448 | tf_op jit(solution)/shard_map/ppermute | solution.py:319
  5.7 8.6 %collective-permute-start.1 = (bf16[4,2,16512]{2,1,0:T(2,128)(2,1)}, bf16[4,2,16512]{2,1,0:T(2,128)(2,1)S(1)}, u32[]{:S(2)}, u32[]{:S(2)}) collective-permute-start(bf16[4,2,16512]{2,1,0:T(2,128)(2,1)} %bitcast.7), channel_id=1, source_target_pairs={{0,4},{1,9},{4,0},{5,13},{8,12},{9,1},{12,8},{13,5},{2,6},{3,11},{... | collective-permute-start | bytes 792584 | tf_op jit(solution)/shard_map/ppermute | solution.py:313
  7.3 11.4 %collective-permute-start.3 = (bf16[2,2,16512]{2,1,0:T(2,128)(2,1)S(1)}, bf16[2,2,16512]{2,1,0:T(2,128)(2,1)S(1)}, u32[]{:S(2)}, u32[]{:S(2)}) collective-permute-start(bf16[2,2,16512]{2,1,0:T(2,128)(2,1)S(1)} %get-tuple-element.26), channel_id=1, source_target_pairs={{0,12},{4,8},{8,4},{12,0},{1,13},{5,9},{9,5},{13,1},{2,14},{6,10},... | collective-permute-start | bytes 396296 | tf_op jit(solution)/shard_map/ppermute | solution.py:354
  14.3 11.6 %collective-permute-start.2 = (bf16[4,2,16512]{2,1,0:T(2,128)(2,1)S(1)}, bf16[4,2,16512]{2,1,0:T(2,128)(2,1)S(1)}, u32[]{:S(2)}, u32[]{:S(2)}) collective-permute-start(bf16[4,2,16512]{2,1,0:T(2,128)(2,1)S(1)} %collective-permute-done.1.refs_0_), channel_id=1, source_target_pairs={{0,1},{1,0},{2,3},{3,2},{4,5},{5,4},{6,7},{7,6},{8,9},{9,8},{10,11... | collective-permute-start | bytes 792584 | tf_op jit(solution)/shard_map/ppermute | solution.py:409
  18.7 5.7 %collective-permute-start.4 = (bf16[2,2,16512]{2,1,0:T(2,128)(2,1)S(1)}, bf16[2,2,16512]{2,1,0:T(2,128)(2,1)S(1)}, u32[]{:S(2)}, u32[]{:S(2)}) collective-permute-start(bf16[2,2,16512]{2,1,0:T(2,128)(2,1)S(1)} %collective-permute-done.3.refs_0_), channel_id=1, source_target_pairs={{0,1},{1,0},{2,3},{3,2},{4,5},{5,4},{6,7},{7,6},{8,9},{9,8},{10,11... | collective-permute-start | bytes 396296 | tf_op jit(solution)/shard_map/ppermute | solution.py:412
  29.5 3.6 %collective-permute-start.5 = (f32[1,128]{1,0:T(1,128)S(1)}, f32[1,128]{1,0:T(1,128)S(1)}, u32[]{:S(2)}, u32[]{:S(2)}) collective-permute-start(f32[1,128]{1,0:T(1,128)S(1)} %get-tuple-element.33), channel_id=1, source_target_pairs={{0,2},{2,0},{1,3},{3,1},{4,6},{6,4},{5,7},{7,5},{8,10},{10,8},{9,1... | collective-permute-start | bytes 1544 | tf_op jit(solution)/shard_map/ppermute | solution.py:319

commit v3 on v2

--- a/solution.py
+++ b/solution.py
@@ -39,22 +39,34 @@
     ]
 
 
-def weigh_kernel(dims, codes_in, beta_in, groups_in, particles, ctf_in, refs, out, part,
-                 codes, beta, groups, ctf, raw, rows_ctf, sem, half_sem, small_sem):
-    rows, per_block, n_codes, tiles, sig = dims
+def weigh_kernel(dims, codes_in, beta_in, groups_in, particles, ctf_in, refs, first, rest, part, ctf,
+                 codes, beta, groups, raw, sem, ctf_sem, half_sem, small_sem):
+    rows, per_block, n_codes, sig = dims
     half = part.shape[0]
     small = [
         pltpu.make_async_copy(codes_in, codes, small_sem.at[0]),
         pltpu.make_async_copy(groups_in, groups, small_sem.at[1]),
-        pltpu.make_async_copy(ctf_in, ctf, small_sem.at[2]),
-        pltpu.make_async_copy(beta_in, beta, small_sem.at[3]),
+        pltpu.make_async_copy(beta_in, beta, small_sem.at[2]),
     ]
     for copy in small:
         copy.start()
-    copies = row_copies(particles, raw, sem)
-    for copy in copies:
-        copy.start()
-    half_copy = pltpu.make_async_copy(refs.at[pl.ds(lax.axis_index("dom") * half, half)], part, half_sem)
+    cut, pixels = first.shape[1], raw.shape[1]
+    spans = (slice(0, cut), slice(cut, pixels))
+    loads = []
+    for b, span in enumerate(spans):
+        copies = [pltpu.make_async_copy(ctf_in.at[:, span], ctf.at[:, span], ctf_sem.at[b])]
+        for p in range(rows):
+            copies.append(
+                pltpu.make_async_copy(
+                    particles.at[p, :, span], raw.at[2 * p : 2 * p + 2, span], sem.at[b]
+                )
+            )
+        loads.append(copies)
+        for copy in copies:
+            copy.start()
+    half_copy = pltpu.make_async_copy(
+        refs.at[pl.ds(lax.axis_index("dom") * half, half)], part, half_sem
+    )
     half_copy.start()
     shape = (2 * rows, LANES)
     owner = iota(shape, 0) // 2
@@ -73,22 +85,19 @@
             extra = jnp.where(mine & (column == 2 + s), group, extra)
     extra = jnp.where(column == 0, code.astype(F32), extra)
     pick = (code[:, :n_codes] == column[:, :n_codes]).astype(BF16)
-    rows_ctf[...] = jnp.dot(pick, ctf[...], preferred_element_type=F32)
-    for copy in copies:
-        copy.wait()
-
-    def step(k, power):
-        value = raw[:, lane(k)].astype(F32)
-        out[:, lane(k)] = (rows_ctf[:, lane(k)] * value).astype(BF16)
-        return power + value * value
-
-    power = lax.fori_loop(0, tiles, step, jnp.zeros(shape, F32), unroll=UNROLL)
-    power = jnp.sum(power, axis=1, keepdims=True)
+    power = jnp.zeros((2 * rows, 1), F32)
+    for copies, span, out in zip(loads, spans, (first, rest)):
+        for copy in copies:
+            copy.wait()
+        value = raw[:, span].astype(F32)
+        chosen = jnp.dot(pick, ctf[:, span], preferred_element_type=F32)
+        out[:, : span.stop - span.start] = (chosen * value).astype(BF16)
+        power = power + jnp.sum(value * value, axis=1, keepdims=True)
     for s in range(3):
         term = power.astype(BF16).astype(F32)
         extra = jnp.where(column == 2 + sig + s, term, extra)
         power = power - term
-    out[:, tiles * LANES :] = extra.astype(BF16)
+    rest[:, pixels - cut :] = extra.astype(BF16)
     half_copy.wait()
 
 
@@ -96,12 +105,16 @@
     return -(-value // to) * to
 
 
-def prepare_kernel(tiles, images, ctf_in, offsets_in, lhs, cosines, sines, ctf, offsets, sem, small_sem):
-    load = pltpu.make_async_copy(ctf_in, ctf, sem)
-    load.start()
+def prepare_kernel(tiles, first, rest, ctf, offsets_in, refs, lhs, cosines, sines, table, product, raw, offsets, sem, small_sem):
+    copies = row_copies(refs, raw, sem)
+    for copy in copies:
+        copy.start()
     small = pltpu.make_async_copy(offsets_in, offsets, small_sem)
     small.start()
-    rows, codes = images.shape[0], ctf.shape[0]
+    rows, codes = first.shape[0], ctf.shape[0]
+    cut = first.shape[1]
+    lhs[:rows, :cut] = first[...]
+    lhs[:rows, cut:] = rest[:, : lhs.shape[1] - cut]
     shape = cosines.shape[:1] + (LANES,)
     row, place = iota(shape, 0), iota(shape, 1)
     small.wait()
@@ -113,10 +126,8 @@
     base = step_x * place - step_y * (KY // 2)
     slope = step_y - step_x
     wrapped = step_x * KX - step_y
-    load.wait()
 
     def step(k, carry):
-        lhs[:rows, lane(k)] = images[:, lane(k)]
         value = ctf[:, lane(k)].astype(F32)
         square = value * value
         high = square.astype(BF16)
@@ -140,6 +151,12 @@
         return carry
 
     lax.fori_loop(0, tiles, step, 0, unroll=UNROLL)
+    for copy in copies:
+        copy.wait()
+    shift_rows(raw, cosines, sines, table, offsets.shape[1], tiles)
+    product[...] = lax.dot_general(
+        table[...], lhs[...], CONTRACT_LAST, preferred_element_type=F32
+    )
 
 
 def shift_rows(raw, cosines, sines, table, shifts, tiles):
@@ -181,31 +198,48 @@
     )
 
 
+def against(tables, used, span, images):
+    stacked = jnp.concatenate([table[:used, span] for table in tables], axis=0)
+    found = [
+        lax.dot_general(
+            stacked, image[:, : span.stop - span.start], CONTRACT_LAST, preferred_element_type=F32
+        )
+        for image in images
+    ]
+    return jnp.concatenate(found, axis=1) if len(found) > 1 else found[0]
+
+
+def first_kernel(count, used, *refs):
+    *inputs, out = refs
+    tables, images = inputs[:count], inputs[count:]
+    out[...] = against(tables, used, slice(0, images[0].shape[1]), images)
+
+
 def last_kernel(dims, *refs):
-    n_img, steps, shifts, tiles, sig, n = dims
+    n_img, known, steps, shifts, tiles, sig, n = dims
     count = len(steps)
     refs = list(refs)
     z, d = lax.axis_index("orient"), lax.axis_index("dom")
-    images = [refs.pop(0) for _ in range(n_img)]
+    firsts = [refs.pop(0) for _ in range(n_img - 1)]
+    rests = [refs.pop(0) for _ in range(n_img)]
     tables = [refs.pop(0) for _ in range(count)]
     products = [refs.pop(0) for _ in range(count)]
+    early = refs.pop(0) if known else None
     outs = refs
     pixels = tiles * LANES
-    rows = images[0].shape[0]
+    rows = rests[0].shape[0]
     codes = (products[0].shape[1] - rows) // 2
     total_rows = n_img * rows
-    used = up(shifts * n, 16)
-
-    others = []
-    if n_img > 1:
-        stacked = jnp.concatenate([table[:used, :] for table in tables], axis=0)
-    for image in images[1:]:
-        others.append(
-            lax.dot_general(
-                stacked, image[:, :pixels], CONTRACT_LAST, preferred_element_type=F32
-            )
-        )
-    extra = jnp.concatenate([image[:, pixels:] for image in images], axis=0)
+    used = shifts * n
+    cut = firsts[0].shape[1]
+    beyond = pixels - cut
+
+    crossed = against(tables, used, slice(cut, pixels), rests[1:])
+    starts = [early[...]] if known else []
+    if known < count:
+        starts.append(against(tables[known:], used, slice(0, cut), firsts))
+    crossed = crossed + (jnp.concatenate(starts, axis=0) if len(starts) > 1 else starts[0])
+    extra = jnp.concatenate([rest[:, beyond:] for rest in rests], axis=0)
     take = (iota((16, LANES), 0) == iota((16, LANES), 1)).astype(BF16)
     turned = lax.dot_general(take, extra, CONTRACT_LAST, preferred_element_type=F32)
     beta = turned[1:2]
@@ -232,9 +266,9 @@
         energy = energies[2 * c * n : (2 * c + 1) * n] + energies[(2 * c + 1) * n : (2 * c + 2) * n]
         energy = energy + pltpu.roll(energy, n - 1, 0)
         scale = beta / jnp.sqrt(power * energy + EPSILON)
-        cross = [products[c][: shifts * n, :rows]]
-        cross += [other[c * used : c * used + shifts * n] for other in others]
-        cross = jnp.concatenate(cross, axis=1) if len(cross) > 1 else cross[0]
+        cross = jnp.concatenate(
+            [products[c][:used, :rows], crossed[c * used : (c + 1) * used]], axis=1
+        )
         total = jnp.zeros((n, total_rows), F32)
         for t in range(shifts):
             value = jnp.where(same, cross[t * n : (t + 1) * n], 0.0)
@@ -319,25 +353,27 @@
         return lax.ppermute(values, "cls", [(c, c ^ k) for c in range(n_cls)])
 
     half = oris // 2
-    weighted, part = pl.pallas_call(
-        functools.partial(weigh_kernel, (rows, per_block, codes, tiles, sig)),
+    cut = (tiles + 1) // 2 * LANES
+    first_half, rest_half, part, ctf_near = pl.pallas_call(
+        functools.partial(weigh_kernel, (rows, per_block, codes, sig)),
         name="weigh",
         out_shape=[
-            jax.ShapeDtypeStruct((2 * rows, pixels + LANES), BF16),
+            jax.ShapeDtypeStruct((2 * rows, cut), BF16),
+            jax.ShapeDtypeStruct((2 * rows, pixels - cut + LANES), BF16),
             jax.ShapeDtypeStruct((half, 2, pixels), BF16),
+            jax.ShapeDtypeStruct((codes, pixels), BF16),
         ],
         in_specs=[hbm, hbm, hbm, hbm, hbm, hbm],
-        out_specs=[vmem, vmem],
+        out_specs=[vmem] * 4,
         scratch_shapes=[
             pltpu.SMEM((rows,), jnp.int32),
             pltpu.VMEM((1, rows), BF16),
             pltpu.SMEM((sig, blocks), jnp.int32),
-            pltpu.VMEM((codes, pixels), BF16),
             pltpu.VMEM((2 * rows, pixels), BF16),
-            pltpu.VMEM((2 * rows, pixels), F32),
+            dma((2,)),
+            dma((2,)),
             dma,
-            dma,
-            dma((4,)),
+            dma((3,)),
         ],
         compiler_params=pltpu.CompilerParams(vmem_limit_bytes=16 << 20),
     )(
@@ -348,34 +384,37 @@
         in_hbm(ctf_table),
         in_hbm(refs_own),
     )
-    images = [weighted]
+    firsts, rests = [], [rest_half]
     for k in range(1, n_cls):
-        images.append(across(weighted, k))
+        firsts.append(across(first_half, k))
+        rests.append(across(rest_half, k))
     near_half = lax.ppermute(part, "orient", [(a, a ^ last) for a in range(groups)])
     lhs_rows = 2 * rows + 2 * codes
     phase_shape = jax.ShapeDtypeStruct((up(shifts, 8), pixels), F32)
-    lhs, cosines, sines = pl.pallas_call(
+    n = 2 * oris
+    n_img = n_cls
+
+    used = (shifts + 2) * n
+    lhs, cosines, sines, *own = pl.pallas_call(
         functools.partial(prepare_kernel, tiles),
         name="prepare",
         out_shape=[
             jax.ShapeDtypeStruct((lhs_rows, pixels), BF16),
             phase_shape,
             phase_shape,
+            jax.ShapeDtypeStruct((used, pixels), BF16),
+            jax.ShapeDtypeStruct((used, lhs_rows), F32),
         ],
-        in_specs=[vmem, hbm, hbm],
-        out_specs=[vmem, vmem, vmem],
+        in_specs=[vmem, vmem, vmem, hbm, hbm],
+        out_specs=[vmem] * 5,
         scratch_shapes=[
-            pltpu.VMEM((codes, pixels), BF16),
+            pltpu.VMEM((n, pixels), BF16),
             pltpu.SMEM((2, shifts), jnp.int32),
             dma,
             dma,
         ],
         compiler_params=pltpu.CompilerParams(vmem_limit_bytes=16 << 20),
-    )(weighted, in_hbm(ctf_table), in_hbm(offsets.T))
-    n = 2 * oris
-    n_img = len(images)
-
-    used = (shifts + 2) * n
+    )(first_half, rest_half, ctf_near, in_hbm(offsets.T), in_hbm(refs_own))
 
     def make_table(*pieces):
         return pl.pallas_call(
@@ -391,27 +430,45 @@
             compiler_params=pltpu.CompilerParams(vmem_limit_bytes=12 << 20),
         )(lhs, cosines, sines, *pieces)
 
-    def evaluate(group):
+    def evaluate(group, early=()):
         steps, tables, products = zip(*group)
+        known = early[0].shape[0] // (shifts * n) if early else 0
         return pl.pallas_call(
-            functools.partial(last_kernel, (n_img, steps, shifts, tiles, sig, n)),
+            functools.partial(last_kernel, (n_img, known, steps, shifts, tiles, sig, n)),
             name="last",
             out_shape=[jax.ShapeDtypeStruct((1, LANES), F32)] * n_img,
-            in_specs=[vmem] * (n_img + 2 * len(group)),
+            in_specs=[vmem] * (2 * n_img - 1 + 2 * len(group) + len(early)),
             out_specs=[vmem] * n_img,
             compiler_params=pltpu.CompilerParams(
                 vmem_limit_bytes=(12 << 20) if n_img < 4 else (40 << 20)
             ),
-        )(*images, *tables, *products)
-
-    made = [((0, 0), *make_table(in_hbm(refs_own)))]
+        )(*firsts, *rests, *tables, *products, *early)
+
+    made = [((0, 0), *own)]
     for (first, second), near in zip(order, direct):
         mate = lax.ppermute(near, "dom", swap)
         made.append(((first, second), *make_table(near)))
         made.append(((second, first), *make_table(mate)))
     far_half = lax.ppermute(near_half, "dom", swap)
     made.append(((last, last), *make_table(near_half, far_half)))
-    found = [evaluate(made[i : i + SET]) for i in range(0, len(made), SET)]
+    found = []
+    while len(made) > SET:
+        found.append(evaluate(made[:SET]))
+        made = made[SET:]
+    ready = [table for _, table, _ in made[:-1]]
+    early = pl.pallas_call(
+        functools.partial(first_kernel, len(ready), shifts * n),
+        name="first",
+        out_shape=jax.ShapeDtypeStruct(
+            (len(ready) * shifts * n, (n_img - 1) * 2 * rows), F32
+        ),
+        in_specs=[vmem] * (len(ready) + n_img - 1),
+        out_specs=vmem,
+        compiler_params=pltpu.CompilerParams(
+            vmem_limit_bytes=(12 << 20) if n_img < 4 else (40 << 20)
+        ),
+    )(*ready, *firsts)
+    found.append(evaluate(made, (early,)))
     evidence = found[0]
     for more in found[1:]:
         evidence = [a + b for a, b in zip(evidence, more)]

time: 34 us -> 29.7 us (0.87)
  starting transfers between devices: 11.9 us -> 9.55 us
  Pallas kernels: 13.5 us -> 11.9 us
  waiting for transfers between devices: 7.67 us -> 7.03 us
    ppermute x1, waiting for transfers between devices: 0.01 us -> 4.17 us  [local(): lax.ppermute(part, 'orient', [(a, a ^ last) for a in range(groups)])]
    ppermute x1, starting transfers between devices: 4.35 us -> 0.36 us  [local(): mate = lax.ppermute(near, 'dom', swap)]
    ppermute x1, waiting for transfers between devices: 4.58 us -> 0.77 us  [local(): lax.ppermute(refs_own, ('orient', 'dom'), core_step(first, second))]
    pallas_call x4 -> x3, Pallas kernels: 6.56 us -> 4.3 us  [make_table(): pl.pallas_call(functools.partial(tables_kernel, shifts, tiles), name='tab...]
    ppermute x1, starting transfers between devices: 1.58 us -> 3.12 us  [local(): lax.ppermute(refs_own, ('orient', 'dom'), core_step(first, second))]
    pallas_call x1, Pallas kernels: 2.04 us -> 3.06 us  [local(): pl.pallas_call(functools.partial(prepare_kernel, tiles), name='prepare',...]
    ppermute x2 -> x3, waiting for transfers between devices: 3.08 us -> 2.08 us  [across(): return lax.ppermute(values, 'cls', [(c, c ^ k) for c in range(n_cls)])]
    pallas_call x2 -> x3, Pallas kernels: 4.17 us -> 3.83 us  [the longest x1 1.73 us: local(): pl.pallas_call(functools.partial(weigh_kernel, (rows, per_block, codes, s...]
  transfers between devices with their start and end apart: 6 -> 7, of which waited for: 2 -> 3; matrix products, arithmetic and copies ran while one was open for 0% -> 0% of each run, Pallas kernels for 25% -> 34%
where the time goes in v3:
time: 29.7 us; the launch traced here: 29.2 us
  Pallas kernels  11.9 us (40%)
  starting transfers between devices  9.55 us (32%)
  waiting for transfers between devices  7.03 us (24%)
  between operations  0.72 us (2%)
    pallas_call x3, Pallas kernels, make_table(): pl.pallas_call(functools.partial(tables_kernel, shifts, tiles), name='tab...  4.3 us
    ppermute x1, waiting for transfers between devices, local(): lax.ppermute(part, 'orient', [(a, a ^ last) for a in range(groups)])  4.17 us
    ppermute x3, starting transfers between devices, across(): return lax.ppermute(values, 'cls', [(c, c ^ k) for c in range(n_cls)])  3.59 us
    ppermute x1, starting transfers between devices, local(): lax.ppermute(refs_own, ('orient', 'dom'), core_step(first, second))  3.12 us
    pallas_call x1, Pallas kernels, local(): pl.pallas_call(functools.partial(prepare_kernel, tiles), name='prepare',...  3.06 us
    ppermute x1, starting transfers between devices, local(): lax.ppermute(part, 'orient', [(a, a ^ last) for a in range(groups)])  2.48 us
    ppermute x3, waiting for transfers between devices, across(): return lax.ppermute(values, 'cls', [(c, c ^ k) for c in range(n_cls)])  2.08 us
    pallas_call x1, Pallas kernels, local(): pl.pallas_call(functools.partial(weigh_kernel, (rows, per_block, codes, s...  1.73 us
  transfers between devices with their start and end apart: 7, of which 3 were waited for; matrix products, arithmetic and copies ran while one was open for 0% of the time, Pallas kernels for 34%

profile of v3, /device:TPU:0, one launch (start us, length us, event | category | flops | bytes accessed | tf_op | source)
XLA Modules:
  0.0 29.2 jit_solution(6140936214610403924)
XLA Ops:
  0.6 3.1 %collective-permute-start.2 = (bf16[4,2,16512]{2,1,0:T(2,128)(2,1)}, bf16[4,2,16512]{2,1,0:T(2,128)(2,1)S(1)}, u32[]{:S(2)}, u32[]{:S(2)}) collective-permute-start(bf16[4,2,16512]{2,1,0:T(2,128)(2,1)} %bitcast.6), channel_id=1, source_target_pairs={{0,4},{1,9},{4,0},{5,13},{8,12},{9,1},{12,8},{13,5},{2,6},{3,11},{... | collective-permute-start | bytes 792584 | tf_op jit(solution)/shard_map/ppermute | solution.py:347
  3.7 1.7 %weigh.1 = (bf16[16,8320]{1,0:T(8,128)(2,1)S(1)}, bf16[16,8320]{1,0:T(8,128)(2,1)S(1)}, bf16[2,2,16512]{2,1,0:T(2,128)(2,1)S(1)}, bf16[16,16512]{1,0:T(8,128)(2,1)S(1)}) custom-call(s32[8]{0:T(128)} %codes_in.1, bf16[1,8]{1,0:T(2,128)(2,1)} %bitcast.10, s32[1,4]{1,0:T(1,128)} %bitcast.11, bf16[8,2,16512]{2,1,0:T(2,128)(2,1)} %particles.1, ...), custom_call_target="tpu_custom_call" | custom-call | tf_op jit(solution)/shard_map/weigh/pallas_call | solution.py:357
  5.5 1.6 %collective-permute-start = (bf16[16,8320]{1,0:T(8,128)(2,1)S(1)}, bf16[16,8320]{1,0:T(8,128)(2,1)S(1)}, u32[]{:S(2)}, u32[]{:S(2)}) collective-permute-start(bf16[16,8320]{1,0:T(8,128)(2,1)S(1)} %get-tuple-element.21.first), channel_id=1, source_target_pairs={{0,2},{2,0},{1,3},{3,1},{4,6},{6,4},{5,7},{7,5},{8,10},{10,8},{9,1... | collective-permute-start | bytes 798728 | tf_op jit(solution)/shard_map/ppermute | solution.py:353
  7.0 0.5 %collective-permute-start.1 = (bf16[16,8320]{1,0:T(8,128)(2,1)S(1)}, bf16[16,8320]{1,0:T(8,128)(2,1)S(1)}, u32[]{:S(2)}, u32[]{:S(2)}) collective-permute-start(bf16[16,8320]{1,0:T(8,128)(2,1)S(1)} %get-tuple-element.22.rest.refs_1_), channel_id=1, source_target_pairs={{0,2},{2,0},{1,3},{3,1},{4,6},{6,4},{5,7},{7,5},{8,10},{10,8},{9,1... | collective-permute-start | bytes 798728 | tf_op jit(solution)/shard_map/ppermute | solution.py:353
  7.6 2.5 %collective-permute-start.4 = (bf16[2,2,16512]{2,1,0:T(2,128)(2,1)S(1)}, bf16[2,2,16512]{2,1,0:T(2,128)(2,1)S(1)}, u32[]{:S(2)}, u32[]{:S(2)}) collective-permute-start(bf16[2,2,16512]{2,1,0:T(2,128)(2,1)S(1)} %get-tuple-element.30), channel_id=1, source_target_pairs={{0,12},{4,8},{8,4},{12,0},{1,13},{5,9},{9,5},{13,1},{2,14},{6,10},... | collective-permute-start | bytes 396296 | tf_op jit(solution)/shard_map/ppermute | solution.py:391
  10.1 0.8 %collective-permute-done.2.refs_0_ = bf16[4,2,16512]{2,1,0:T(2,128)(2,1)S(1)} collective-permute-done((bf16[4,2,16512]{2,1,0:T(2,128)(2,1)}, bf16[4,2,16512]{2,1,0:T(2,128)(2,1)S(1)}, u32[]{:S(2)}, u32[]{:S(2)}) %collective-permute-start.2) | collective-permute-done | bytes 264224 | tf_op jit(solution)/shard_map/ppermute | solution.py:347
  10.8 0.4 %collective-permute-start.3 = (bf16[4,2,16512]{2,1,0:T(2,128)(2,1)S(1)}, bf16[4,2,16512]{2,1,0:T(2,128)(2,1)S(1)}, u32[]{:S(2)}, u32[]{:S(2)}) collective-permute-start(bf16[4,2,16512]{2,1,0:T(2,128)(2,1)S(1)} %collective-permute-done.2.refs_0_), channel_id=1, source_target_pairs={{0,1},{1,0},{2,3},{3,2},{4,5},{5,4},{6,7},{7,6},{8,9},{9,8},{10,11... | collective-permute-start | bytes 792584 | tf_op jit(solution)/shard_map/ppermute | solution.py:449
  11.2 4.2 %collective-permute-done.4.refs_0_ = bf16[2,2,16512]{2,1,0:T(2,128)(2,1)S(1)} collective-permute-done((bf16[2,2,16512]{2,1,0:T(2,128)(2,1)S(1)}, bf16[2,2,16512]{2,1,0:T(2,128)(2,1)S(1)}, u32[]{:S(2)}, u32[]{:S(2)}) %collective-permute-start.4) | collective-permute-done | bytes 132128 | tf_op jit(solution)/shard_map/ppermute | solution.py:391
  15.4 0.0 collective-permute-start.5
  15.4 3.1 %prepare.1 = (bf16[48,16512]{1,0:T(8,128)(2,1)S(1)}, f32[8,16512]{1,0:T(8,128)S(1)}, f32[8,16512]{1,0:T(8,128)S(1)}, bf16[56,16512]{1,0:T(8,128)(2,1)S(1)}, f32[56,48]{1,0:T(8,128)S(1)}) custom-call(bf16[16,8320]{1,0:T(8,128)(2,1)S(1)} %get-tuple-element.21.first, bf16[16,8320]{1,0:T(8,128)(2,1)S(1)} %get-tuple-element.22.rest.refs_1_, ...), custom_call_target="tpu_custom_call" | custom-call | tf_op jit(solution)/shard_map/prepare/pallas_call | solution.py:398
  18.4 1.4 %tables.3 = (bf16[56,16512]{1,0:T(8,128)(2,1)S(1)}, f32[56,48]{1,0:T(8,128)S(1)}) custom-call(bf16[48,16512]{1,0:T(8,128)(2,1)S(1)} %get-tuple-element.25.lhs, f32[8,16512]{1,0:T(8,128)S(1)} %get-tuple-element.26.cosines, f32[8,16512]{1,0:T(8,128)S(1)} %get-tuple-element.27.sines, bf16[4,2,16512]{2,1,0:T(2,128)(2,1)S(1)} %collective-permute-done.2.refs_0_), custom_call_target="tpu_custom_call" | custom-call | tf_op jit(solution)/shard_map/tables/pallas_call | solution.py:420
  19.9 0.0 collective-permute-done.5.refs_1_
  19.9 1.4 %tables.5 = (bf16[56,16512]{1,0:T(8,128)(2,1)S(1)}, f32[56,48]{1,0:T(8,128)S(1)}) custom-call(bf16[48,16512]{1,0:T(8,128)(2,1)S(1)} %get-tuple-element.25.lhs, f32[8,16512]{1,0:T(8,128)S(1)} %get-tuple-element.26.cosines, f32[8,16512]{1,0:T(8,128)S(1)} %get-tuple-element.27.sines, bf16[2,2,16512]{2,1,0:T(2,128)(2,1)S(1)} %collective-permute-done.4.refs_0_, ...), custom_call_target="tpu_custom_call" | custom-call | tf_op jit(solution)/shard_map/tables/pallas_call | solution.py:420
  21.3 0.0 collective-permute-done.3.refs_0_
  21.3 1.4 %tables.4 = (bf16[56,16512]{1,0:T(8,128)(2,1)S(1)}, f32[56,48]{1,0:T(8,128)S(1)}) custom-call(bf16[48,16512]{1,0:T(8,128)(2,1)S(1)} %get-tuple-element.25.lhs, f32[8,16512]{1,0:T(8,128)S(1)} %get-tuple-element.26.cosines, f32[8,16512]{1,0:T(8,128)S(1)} %get-tuple-element.27.sines, bf16[4,2,16512]{2,1,0:T(2,128)(2,1)S(1)} %collective-permute-done.3.refs_0_), custom_call_target="tpu_custom_call" | custom-call | tf_op jit(solution)/shard_map/tables/pallas_call | solution.py:420
  22.8 0.0 collective-permute-done.refs_3_.refs_0_
  22.8 0.7 %first.1.refs_11_ = f32[120,16]{1,0:T(8,128)S(1)} custom-call(bf16[56,16512]{1,0:T(8,128)(2,1)S(1)} %get-tuple-element.24.refs_0_.refs_3_, bf16[56,16512]{1,0:T(8,128)(2,1)S(1)} %get-tuple-element.28.refs_1_.refs_4_, bf16[56,16512]{1,0:T(8,128)(2,1)S(1)} %get-tuple-element.29.refs_2_.refs_5_, bf16[16,8320]{1,0:T(8,128)(2,1)S(1)} %collective-permute-done.refs_3_.refs_0_), custom_call_target="tpu_custom_call" | custom-call | tf_op jit(solution)/shard_map/first/pallas_call | solution.py:459
  23.5 0.0 collective-permute-done.1.refs_2_
  23.5 1.4 %last.1 = (f32[1,128]{1,0:T(1,128)S(1)}, f32[1,128]{1,0:T(1,128)S(1)}) custom-call(bf16[16,8320]{1,0:T(8,128)(2,1)S(1)} %collective-permute-done.refs_3_.refs_0_, bf16[16,8320]{1,0:T(8,128)(2,1)S(1)} %get-tuple-element.22.rest.refs_1_, bf16[16,8320]{1,0:T(8,128)(2,1)S(1)} %collective-permute-done.1.refs_2_, ...), custom_call_target="tpu_custom_call" | custom-call | tf_op jit(solution)/shard_map/last/pallas_call | solution.py:436
  24.9 1.5 %collective-permute-start.6 = (f32[1,128]{1,0:T(1,128)S(1)}, f32[1,128]{1,0:T(1,128)S(1)}, u32[]{:S(2)}, u32[]{:S(2)}) collective-permute-start(f32[1,128]{1,0:T(1,128)S(1)} %get-tuple-element.37), channel_id=1, source_target_pairs={{0,2},{2,0},{1,3},{3,1},{4,6},{6,4},{5,7},{7,5},{8,10},{10,8},{9,1... | collective-permute-start | bytes 1544 | tf_op jit(solution)/shard_map/ppermute | solution.py:353
  26.4 2.1 %collective-permute-done.6.refs_1_ = f32[1,128]{1,0:T(1,128)S(1)} collective-permute-done((f32[1,128]{1,0:T(1,128)S(1)}, f32[1,128]{1,0:T(1,128)S(1)}, u32[]{:S(2)}, u32[]{:S(2)}) %collective-permute-start.6) | collective-permute-done | bytes 544 | tf_op jit(solution)/shard_map/ppermute | solution.py:353
  28.5 0.7 %finish.1 = (f32[2,8]{1,0:T(2,128)}, f32[1,8]{1,0:T(1,128)}) custom-call(f32[1,128]{1,0:T(1,128)S(1)} %get-tuple-element.36.refs_0_, f32[1,128]{1,0:T(1,128)S(1)} %collective-permute-done.6.refs_1_), custom_call_target="tpu_custom_call" | custom-call | tf_op jit(solution)/shard_map/finish/pallas_call | solution.py:476
Async XLA Ops:
  0.6 10.2 %collective-permute-start.2 = (bf16[4,2,16512]{2,1,0:T(2,128)(2,1)}, bf16[4,2,16512]{2,1,0:T(2,128)(2,1)S(1)}, u32[]{:S(2)}, u32[]{:S(2)}) collective-permute-start(bf16[4,2,16512]{2,1,0:T(2,128)(2,1)} %bitcast.6), channel_id=1, source_target_pairs={{0,4},{1,9},{4,0},{5,13},{8,12},{9,1},{12,8},{13,5},{2,6},{3,11},{... | collective-permute-start | bytes 792584 | tf_op jit(solution)/shard_map/ppermute | solution.py:347
  5.5 17.3 %collective-permute-start = (bf16[16,8320]{1,0:T(8,128)(2,1)S(1)}, bf16[16,8320]{1,0:T(8,128)(2,1)S(1)}, u32[]{:S(2)}, u32[]{:S(2)}) collective-permute-start(bf16[16,8320]{1,0:T(8,128)(2,1)S(1)} %get-tuple-element.21.first), channel_id=1, source_target_pairs={{0,2},{2,0},{1,3},{3,1},{4,6},{6,4},{5,7},{7,5},{8,10},{10,8},{9,1... | collective-permute-start | bytes 798728 | tf_op jit(solution)/shard_map/ppermute | solution.py:353
  7.0 16.4 %collective-permute-start.1 = (bf16[16,8320]{1,0:T(8,128)(2,1)S(1)}, bf16[16,8320]{1,0:T(8,128)(2,1)S(1)}, u32[]{:S(2)}, u32[]{:S(2)}) collective-permute-start(bf16[16,8320]{1,0:T(8,128)(2,1)S(1)} %get-tuple-element.22.rest.refs_1_), channel_id=1, source_target_pairs={{0,2},{2,0},{1,3},{3,1},{4,6},{6,4},{5,7},{7,5},{8,10},{10,8},{9,1... | collective-permute-start | bytes 798728 | tf_op jit(solution)/shard_map/ppermute | solution.py:353
  7.6 7.8 %collective-permute-start.4 = (bf16[2,2,16512]{2,1,0:T(2,128)(2,1)S(1)}, bf16[2,2,16512]{2,1,0:T(2,128)(2,1)S(1)}, u32[]{:S(2)}, u32[]{:S(2)}) collective-permute-start(bf16[2,2,16512]{2,1,0:T(2,128)(2,1)S(1)} %get-tuple-element.30), channel_id=1, source_target_pairs={{0,12},{4,8},{8,4},{12,0},{1,13},{5,9},{9,5},{13,1},{2,14},{6,10},... | collective-permute-start | bytes 396296 | tf_op jit(solution)/shard_map/ppermute | solution.py:391
  10.8 10.5 %collective-permute-start.3 = (bf16[4,2,16512]{2,1,0:T(2,128)(2,1)S(1)}, bf16[4,2,16512]{2,1,0:T(2,128)(2,1)S(1)}, u32[]{:S(2)}, u32[]{:S(2)}) collective-permute-start(bf16[4,2,16512]{2,1,0:T(2,128)(2,1)S(1)} %collective-permute-done.2.refs_0_), channel_id=1, source_target_pairs={{0,1},{1,0},{2,3},{3,2},{4,5},{5,4},{6,7},{7,6},{8,9},{9,8},{10,11... | collective-permute-start | bytes 792584 | tf_op jit(solution)/shard_map/ppermute | solution.py:449
  15.4 4.5 %collective-permute-start.5 = (bf16[2,2,16512]{2,1,0:T(2,128)(2,1)S(1)}, bf16[2,2,16512]{2,1,0:T(2,128)(2,1)S(1)}, u32[]{:S(2)}, u32[]{:S(2)}) collective-permute-start(bf16[2,2,16512]{2,1,0:T(2,128)(2,1)S(1)} %collective-permute-done.4.refs_0_), channel_id=1, source_target_pairs={{0,1},{1,0},{2,3},{3,2},{4,5},{5,4},{6,7},{7,6},{8,9},{9,8},{10,11... | collective-permute-start | bytes 396296 | tf_op jit(solution)/shard_map/ppermute | solution.py:452
  24.9 3.6 %collective-permute-start.6 = (f32[1,128]{1,0:T(1,128)S(1)}, f32[1,128]{1,0:T(1,128)S(1)}, u32[]{:S(2)}, u32[]{:S(2)}) collective-permute-start(f32[1,128]{1,0:T(1,128)S(1)} %get-tuple-element.37), channel_id=1, source_target_pairs={{0,2},{2,0},{1,3},{3,1},{4,6},{6,4},{5,7},{7,5},{8,10},{10,8},{9,1... | collective-permute-start | bytes 1544 | tf_op jit(solution)/shard_map/ppermute | solution.py:353

commit v4 on v3

--- a/solution.py
+++ b/solution.py
@@ -22,31 +22,35 @@
 CONTRACT_LAST = (((1,), (1,)), ((), ()))
 
 
-def lane(k, width=LANES):
-    return pl.ds(pl.multiple_of(k * width, LANES), width)
+def lane(k, width=1, count=None):
+    return pl.ds(pl.multiple_of(k * width * LANES, LANES), (count or width) * LANES)
 
 
 def iota(shape, axis):
     return lax.broadcasted_iota(jnp.int32, shape, axis)
 
 
-def row_copies(source, target, sem, start=0):
-    return [
-        pltpu.make_async_copy(
-            source.at[i], target.at[start + 2 * i : start + 2 * i + 2], sem
-        )
-        for i in range(source.shape[0])
-    ]
-
-
-def weigh_kernel(dims, codes_in, beta_in, groups_in, particles, ctf_in, refs, first, rest, part, ctf,
-                 codes, beta, groups, raw, sem, ctf_sem, half_sem, small_sem):
+def weighted(pick, ctf, raw, span):
+    value = raw[:, span].astype(F32)
+    chosen = jnp.dot(pick, ctf[:, span], preferred_element_type=F32)
+    return (chosen * value).astype(BF16), jnp.sum(value * value, axis=1, keepdims=True)
+
+
+def picked(code, n_codes):
+    shape = (code.shape[0], n_codes)
+    return (code[:, 0:1] == iota(shape, 1)).astype(BF16)
+
+
+def weigh_kernel(dims, codes_in, beta_in, groups_in, offsets_in, particles, ctf_in, refs,
+                 first, raw, ctf, more, part, turns,
+                 codes, beta, groups, offsets, sem, ctf_sem, half_sem, small_sem):
     rows, per_block, n_codes, sig = dims
     half = part.shape[0]
     small = [
         pltpu.make_async_copy(codes_in, codes, small_sem.at[0]),
         pltpu.make_async_copy(groups_in, groups, small_sem.at[1]),
         pltpu.make_async_copy(beta_in, beta, small_sem.at[2]),
+        pltpu.make_async_copy(offsets_in, offsets, small_sem.at[3]),
     ]
     for copy in small:
         copy.start()
@@ -84,48 +88,106 @@
             group = groups[s, p // per_block].astype(F32)
             extra = jnp.where(mine & (column == 2 + s), group, extra)
     extra = jnp.where(column == 0, code.astype(F32), extra)
-    pick = (code[:, :n_codes] == column[:, :n_codes]).astype(BF16)
-    power = jnp.zeros((2 * rows, 1), F32)
-    for copies, span, out in zip(loads, spans, (first, rest)):
-        for copy in copies:
-            copy.wait()
-        value = raw[:, span].astype(F32)
-        chosen = jnp.dot(pick, ctf[:, span], preferred_element_type=F32)
-        out[:, : span.stop - span.start] = (chosen * value).astype(BF16)
-        power = power + jnp.sum(value * value, axis=1, keepdims=True)
+    pick = picked(code, n_codes)
+    for copy in loads[0]:
+        copy.wait()
+    first[...], power = weighted(pick, ctf, raw, spans[0])
+    more[...] = jnp.where(column == 2 + sig, power, extra)
+    shape = turns.shape[1:]
+    step_x = jnp.zeros(shape, jnp.int32)
+    step_y = jnp.zeros(shape, jnp.int32)
+    for t in range(offsets.shape[1]):
+        step_x = jnp.where(iota(shape, 0) == t, offsets[0, t], step_x)
+        step_y = jnp.where(iota(shape, 0) == t, offsets[1, t], step_y)
+    turns[0] = step_x * iota(shape, 1) - step_y * (KY // 2)
+    turns[1] = step_y - step_x
+    turns[2] = step_x * KX - step_y
+    half_copy.wait()
+    for copy in loads[1]:
+        copy.wait()
+
+
+def rest_kernel(sig, raw, ctf, more, rest):
+    pixels, cut = raw.shape[1], raw.shape[1] + LANES - rest.shape[1]
+    extra = more[...]
+    column = iota(extra.shape, 1)
+    pick = picked(extra.astype(jnp.int32), ctf.shape[0])
+    rest[:, : pixels - cut], power = weighted(pick, ctf, raw, slice(cut, pixels))
+    power = power + extra[:, 2 + sig : 3 + sig]
     for s in range(3):
         term = power.astype(BF16).astype(F32)
         extra = jnp.where(column == 2 + sig + s, term, extra)
         power = power - term
     rest[:, pixels - cut :] = extra.astype(BF16)
-    half_copy.wait()
 
 
 def up(value, to):
     return -(-value // to) * to
 
 
-def prepare_kernel(tiles, first, rest, ctf, offsets_in, refs, lhs, cosines, sines, table, product, raw, offsets, sem, small_sem):
-    copies = row_copies(refs, raw, sem)
-    for copy in copies:
-        copy.start()
-    small = pltpu.make_async_copy(offsets_in, offsets, small_sem)
-    small.start()
+def block_copies(sources, raw, sem, b, width):
+    span = lane(b * width, 1, width)
+    copies, row = [], 0
+    for source in sources:
+        for i in range(source.shape[0]):
+            copies.append(
+                pltpu.make_async_copy(
+                    source.at[i, :, span], raw.at[row : row + 2, span], sem.at[b]
+                )
+            )
+            row += 2
+    return copies
+
+
+def load_blocks(sources, raw, sem):
+    count = sem.shape[0]
+    for b in range(count):
+        for copy in block_copies(sources, raw, sem, b, raw.shape[1] // LANES // count):
+            copy.start()
+
+
+def build_table(sources, raw, sem, cosines, sines, lhs, table, product, shifts):
+    n = raw.shape[0]
+    odd = iota((n, LANES), 0) % 2 == 1
+    count = sem.shape[0]
+    width = raw.shape[1] // LANES // count
+
+    def block(b, carry):
+        for copy in block_copies(sources, raw, sem, b, width):
+            copy.wait()
+
+        def step(k, carry):
+            here = lane(b * width + k)
+            value = raw[:, here].astype(F32)
+            turned = jnp.where(odd, -pltpu.roll(value, 1, 0), pltpu.roll(value, n - 1, 0))
+            parts = [
+                value * cosines[t : t + 1, here] + turned * sines[t : t + 1, here]
+                for t in range(shifts)
+            ]
+            square = value * value
+            high = square.astype(BF16).astype(F32)
+            parts += [high, square - high]
+            for i in range(0, len(parts), 2):
+                both = jnp.concatenate(parts[i : i + 2], axis=0)
+                table[n * i : n * i + both.shape[0], here] = both.astype(BF16)
+            return carry
+
+        return lax.fori_loop(0, width, step, carry, unroll=min(UNROLL, width))
+
+    lax.fori_loop(0, count, block, 0)
+    product[...] = lax.dot_general(
+        table[...], lhs[...], CONTRACT_LAST, preferred_element_type=F32
+    )
+
+
+def prepare_kernel(shifts, first, rest, ctf, turns, refs, lhs, cosines, sines, table, product, raw, sem):
+    load_blocks([refs], raw, sem)
     rows, codes = first.shape[0], ctf.shape[0]
     cut = first.shape[1]
     lhs[:rows, :cut] = first[...]
     lhs[:rows, cut:] = rest[:, : lhs.shape[1] - cut]
-    shape = cosines.shape[:1] + (LANES,)
-    row, place = iota(shape, 0), iota(shape, 1)
-    small.wait()
-    step_x = jnp.zeros(shape, jnp.int32)
-    step_y = jnp.zeros(shape, jnp.int32)
-    for t in range(offsets.shape[1]):
-        step_x = jnp.where(row == t, offsets[0, t], step_x)
-        step_y = jnp.where(row == t, offsets[1, t], step_y)
-    base = step_x * place - step_y * (KY // 2)
-    slope = step_y - step_x
-    wrapped = step_x * KX - step_y
+    place = iota(turns.shape[1:], 1)
+    base, slope, wrapped = turns[0], turns[1], turns[2]
 
     def step(k, carry):
         value = ctf[:, lane(k)].astype(F32)
@@ -144,58 +206,20 @@
             4.166664568298827e-2 + x2 * (-1.388731625493765e-3 + x2 * 2.443315711809948e-5)
         )
         swap = (quarter & 1) == 1
-        first = jnp.where(swap, sin, cos)
-        second = jnp.where(swap, cos, sin)
-        cosines[:, lane(k)] = jnp.where(((quarter + 1) & 2) == 2, -first, first)
-        sines[:, lane(k)] = jnp.where((quarter & 2) == 2, -second, second)
+        near = jnp.where(swap, sin, cos)
+        other = jnp.where(swap, cos, sin)
+        cosines[:, lane(k)] = jnp.where(((quarter + 1) & 2) == 2, -near, near)
+        sines[:, lane(k)] = jnp.where((quarter & 2) == 2, -other, other)
         return carry
 
-    lax.fori_loop(0, tiles, step, 0, unroll=UNROLL)
-    for copy in copies:
-        copy.wait()
-    shift_rows(raw, cosines, sines, table, offsets.shape[1], tiles)
-    product[...] = lax.dot_general(
-        table[...], lhs[...], CONTRACT_LAST, preferred_element_type=F32
-    )
-
-
-def shift_rows(raw, cosines, sines, table, shifts, tiles):
-    n = raw.shape[0]
-    odd = iota((n, LANES), 0) % 2 == 1
-
-    def step(k, carry):
-        value = raw[:, lane(k)].astype(F32)
-        turned = jnp.where(odd, -pltpu.roll(value, 1, 0), pltpu.roll(value, n - 1, 0))
-        parts = [
-            value * cosines[t : t + 1, lane(k)] + turned * sines[t : t + 1, lane(k)]
-            for t in range(shifts)
-        ]
-        square = value * value
-        high = square.astype(BF16).astype(F32)
-        parts += [high, square - high]
-        for i in range(0, len(parts), 2):
-            both = jnp.concatenate(parts[i : i + 2], axis=0)
-            table[n * i : n * i + both.shape[0], lane(k)] = both.astype(BF16)
-        return carry
-
-    lax.fori_loop(0, tiles, step, 0, unroll=UNROLL)
-
-
-def tables_kernel(shifts, tiles, lhs, cosines, sines, *refs):
-    pieces = refs[:-4]
+    lax.fori_loop(0, lhs.shape[1] // LANES, step, 0, unroll=UNROLL)
+    build_table([refs], raw, sem, cosines, sines, lhs, table, product, shifts)
+
+
+def tables_kernel(shifts, lhs, cosines, sines, *refs):
     table, product, raw, sem = refs[-4:]
-    n = raw.shape[0]
-    copies = []
-    for i, piece in enumerate(pieces):
-        copies += row_copies(piece, raw, sem, i * n // len(pieces))
-    for copy in copies:
-        copy.start()
-    for copy in copies:
-        copy.wait()
-    shift_rows(raw, cosines, sines, table, shifts, tiles)
-    product[...] = lax.dot_general(
-        table[...], lhs[...], CONTRACT_LAST, preferred_element_type=F32
-    )
+    load_blocks(refs[:-4], raw, sem)
+    build_table(refs[:-4], raw, sem, cosines, sines, lhs, table, product, shifts)
 
 
 def against(tables, used, span, images):
@@ -231,13 +255,12 @@
     codes = (products[0].shape[1] - rows) // 2
     total_rows = n_img * rows
     used = shifts * n
-    cut = firsts[0].shape[1]
-    beyond = pixels - cut
-
-    crossed = against(tables, used, slice(cut, pixels), rests[1:])
+    beyond = rests[0].shape[1] - LANES
+
+    crossed = against(tables, used, slice(pixels - beyond, pixels), rests[1:])
     starts = [early[...]] if known else []
     if known < count:
-        starts.append(against(tables[known:], used, slice(0, cut), firsts))
+        starts.append(against(tables[known:], used, slice(0, pixels - beyond), firsts))
     crossed = crossed + (jnp.concatenate(starts, axis=0) if len(starts) > 1 else starts[0])
     extra = jnp.concatenate([rest[:, beyond:] for rest in rests], axis=0)
     take = (iota((16, LANES), 0) == iota((16, LANES), 1)).astype(BF16)
@@ -314,15 +337,15 @@
     groups = lax.axis_size("orient")
     n_cls = lax.axis_size("cls")
     cores = lax.axis_size("dom")
-    blocks, sig = significant.shape
+    blocks_here, sig = significant.shape
     rows, _, pixels = particles.shape
-    per_block = rows // blocks
+    per_block = rows // blocks_here
     codes = ctf_table.shape[0]
     oris = references.shape[2]
     shifts = offsets.shape[0]
     tiles = pixels // LANES
     refs_own = references.reshape(oris, 2, pixels)
-    steps = list(range(1, groups))
+    steps = [k for k in range(1, groups) if k != groups // 2] + [groups // 2]
     anywhere = pl.BlockSpec(memory_space=pl.ANY)
     vmem = pl.BlockSpec(memory_space=pltpu.VMEM)
     hbm = pl.BlockSpec(memory_space=pltpu.HBM)
@@ -342,61 +365,71 @@
     swap = [(c, cores - 1 - c) for c in range(cores)]
     direct, order = [], []
     while len(steps) > 1:
-        first, second = steps.pop(0), steps.pop(0)
-        direct.append(
-            lax.ppermute(refs_own, ("orient", "dom"), core_step(first, second))
-        )
-        order.append((first, second))
+        low, high = steps.pop(0), steps.pop(0)
+        direct.append(lax.ppermute(refs_own, ("orient", "dom"), core_step(low, high)))
+        order.append((low, high))
     last = steps.pop(0)
 
     def across(values, k):
         return lax.ppermute(values, "cls", [(c, c ^ k) for c in range(n_cls)])
 
     half = oris // 2
-    cut = (tiles + 1) // 2 * LANES
-    first_half, rest_half, part, ctf_near = pl.pallas_call(
+    cut = tiles * 3 // 4 * LANES
+    first, raw_rows, ctf_near, more, part, turns = pl.pallas_call(
         functools.partial(weigh_kernel, (rows, per_block, codes, sig)),
         name="weigh",
         out_shape=[
             jax.ShapeDtypeStruct((2 * rows, cut), BF16),
-            jax.ShapeDtypeStruct((2 * rows, pixels - cut + LANES), BF16),
+            jax.ShapeDtypeStruct((2 * rows, pixels), BF16),
+            jax.ShapeDtypeStruct((codes, pixels), BF16),
+            jax.ShapeDtypeStruct((2 * rows, LANES), F32),
             jax.ShapeDtypeStruct((half, 2, pixels), BF16),
-            jax.ShapeDtypeStruct((codes, pixels), BF16),
+            jax.ShapeDtypeStruct((3, up(shifts, 8), LANES), jnp.int32),
         ],
-        in_specs=[hbm, hbm, hbm, hbm, hbm, hbm],
-        out_specs=[vmem] * 4,
+        in_specs=[hbm] * 7,
+        out_specs=[vmem] * 6,
         scratch_shapes=[
             pltpu.SMEM((rows,), jnp.int32),
             pltpu.VMEM((1, rows), BF16),
-            pltpu.SMEM((sig, blocks), jnp.int32),
-            pltpu.VMEM((2 * rows, pixels), BF16),
+            pltpu.SMEM((sig, blocks_here), jnp.int32),
+            pltpu.SMEM((2, shifts), jnp.int32),
             dma((2,)),
             dma((2,)),
             dma,
-            dma((3,)),
+            dma((4,)),
         ],
         compiler_params=pltpu.CompilerParams(vmem_limit_bytes=16 << 20),
     )(
         in_hbm(ctf_index),
         in_hbm(beta[None]),
         in_hbm(significant.T),
+        in_hbm(offsets.T),
         in_hbm(particles),
         in_hbm(ctf_table),
         in_hbm(refs_own),
     )
-    firsts, rests = [], [rest_half]
+    rest = pl.pallas_call(
+        functools.partial(rest_kernel, sig),
+        name="rest",
+        out_shape=jax.ShapeDtypeStruct((2 * rows, pixels - cut + LANES), BF16),
+        in_specs=[vmem] * 3,
+        out_specs=vmem,
+        compiler_params=pltpu.CompilerParams(vmem_limit_bytes=12 << 20),
+    )(raw_rows, ctf_near, more)
+    firsts, rests = [], [rest]
     for k in range(1, n_cls):
-        firsts.append(across(first_half, k))
-        rests.append(across(rest_half, k))
+        firsts.append(across(first, k))
+        rests.append(across(rest, k))
     near_half = lax.ppermute(part, "orient", [(a, a ^ last) for a in range(groups)])
     lhs_rows = 2 * rows + 2 * codes
     phase_shape = jax.ShapeDtypeStruct((up(shifts, 8), pixels), F32)
     n = 2 * oris
     n_img = n_cls
+    n_blocks = 3 if tiles % 3 == 0 else 1
 
     used = (shifts + 2) * n
     lhs, cosines, sines, *own = pl.pallas_call(
-        functools.partial(prepare_kernel, tiles),
+        functools.partial(prepare_kernel, shifts),
         name="prepare",
         out_shape=[
             jax.ShapeDtypeStruct((lhs_rows, pixels), BF16),
@@ -405,20 +438,15 @@
             jax.ShapeDtypeStruct((used, pixels), BF16),
             jax.ShapeDtypeStruct((used, lhs_rows), F32),
         ],
-        in_specs=[vmem, vmem, vmem, hbm, hbm],
+        in_specs=[vmem] * 4 + [hbm],
         out_specs=[vmem] * 5,
-        scratch_shapes=[
-            pltpu.VMEM((n, pixels), BF16),
-            pltpu.SMEM((2, shifts), jnp.int32),
-            dma,
-            dma,
-        ],
+        scratch_shapes=[pltpu.VMEM((n, pixels), BF16), dma((n_blocks,))],
         compiler_params=pltpu.CompilerParams(vmem_limit_bytes=16 << 20),
-    )(first_half, rest_half, ctf_near, in_hbm(offsets.T), in_hbm(refs_own))
+    )(first, rest, ctf_near, turns, in_hbm(refs_own))
 
     def make_table(*pieces):
         return pl.pallas_call(
-            functools.partial(tables_kernel, shifts, tiles),
+            functools.partial(tables_kernel, shifts),
             name="tables",
             out_shape=[
                 jax.ShapeDtypeStruct((used, pixels), BF16),
@@ -426,7 +454,7 @@
             ],
             in_specs=[vmem, vmem, vmem] + [anywhere] * len(pieces),
             out_specs=[vmem, vmem],
-            scratch_shapes=[pltpu.VMEM((n, pixels), BF16), dma],
+            scratch_shapes=[pltpu.VMEM((n, pixels), BF16), dma((n_blocks,))],
             compiler_params=pltpu.CompilerParams(vmem_limit_bytes=12 << 20),
         )(lhs, cosines, sines, *pieces)
 
@@ -445,10 +473,10 @@
         )(*firsts, *rests, *tables, *products, *early)
 
     made = [((0, 0), *own)]
-    for (first, second), near in zip(order, direct):
+    for (low, high), near in zip(order, direct):
         mate = lax.ppermute(near, "dom", swap)
-        made.append(((first, second), *make_table(near)))
-        made.append(((second, first), *make_table(mate)))
+        made.append(((low, high), *make_table(near)))
+        made.append(((high, low), *make_table(mate)))
     far_half = lax.ppermute(near_half, "dom", swap)
     made.append(((last, last), *make_table(near_half, far_half)))
     found = []

time: 29.7 us -> 30.3 us (1.020); the launches traced: 29.2 us -> 30.2 us
  starting transfers between devices: 9.55 us -> 11.2 us
  Pallas kernels: 11.9 us -> 11.3 us
    ppermute x3, starting transfers between devices: 3.59 us -> 5.38 us  [across(): return lax.ppermute(values, 'cls', [(c, c ^ k) for c in range(n_cls)])]
    ppermute x1, waiting for transfers between devices: 4.17 us -> 3.1 us  [local(): lax.ppermute(part, 'orient', [(a, a ^ last) for a in range(groups)])]
    ppermute x1, waiting for transfers between devices: 0.77 us -> 1.67 us  [local(): lax.ppermute(refs_own, ('orient', 'dom'), core_step(low, high))]
    pallas_call x4 -> x5, Pallas kernels: 7.36 us -> 6.88 us  [the longest x3 4.37 us: make_table(): pl.pallas_call(functools.partial(tables_kernel, shifts), name='tables', o...]
    ppermute x1, starting transfers between devices: 0.36 us -> 0.01 us  [local(): mate = lax.ppermute(near, 'dom', swap)]
  transfers between devices with their start and end apart: 7 -> 7, of which waited for: 3 -> 3; matrix products, arithmetic and copies ran while one was open for 0% -> 0% of each run, Pallas kernels for 34% -> 31%
where the time goes in v4:
time: 30.3 us; the launch traced here: 30.2 us
  Pallas kernels  11.3 us (37%)
  starting transfers between devices  11.2 us (37%)
  waiting for transfers between devices  6.92 us (23%)
  between operations  0.72 us (2%)
    ppermute x3, starting transfers between devices, across(): return lax.ppermute(values, 'cls', [(c, c ^ k) for c in range(n_cls)])  5.38 us
    pallas_call x3, Pallas kernels, make_table(): pl.pallas_call(functools.partial(tables_kernel, shifts), name='tables', o...  4.37 us
    ppermute x1, starting transfers between devices, local(): lax.ppermute(refs_own, ('orient', 'dom'), core_step(low, high))  3.12 us
    ppermute x1, waiting for transfers between devices, local(): lax.ppermute(part, 'orient', [(a, a ^ last) for a in range(groups)])  3.1 us
    ppermute x1, starting transfers between devices, local(): lax.ppermute(part, 'orient', [(a, a ^ last) for a in range(groups)])  2.59 us
    pallas_call x1, Pallas kernels, local(): pl.pallas_call(functools.partial(prepare_kernel, shifts), name='prepare',...  2.28 us
    ppermute x3, waiting for transfers between devices, across(): return lax.ppermute(values, 'cls', [(c, c ^ k) for c in range(n_cls)])  2.15 us
    ppermute x1, waiting for transfers between devices, local(): lax.ppermute(refs_own, ('orient', 'dom'), core_step(low, high))  1.67 us
  transfers between devices with their start and end apart: 7, of which 3 were waited for; matrix products, arithmetic and copies ran while one was open for 0% of the time, Pallas kernels for 31%

profile of v4, /device:TPU:0, one launch (start us, length us, event | category | flops | bytes accessed | tf_op | source)
XLA Modules:
  0.0 30.2 jit_solution(6376828184036226034)
XLA Ops:
  0.6 3.1 %collective-permute-start.2 = (bf16[4,2,16512]{2,1,0:T(2,128)(2,1)}, bf16[4,2,16512]{2,1,0:T(2,128)(2,1)S(1)}, u32[]{:S(2)}, u32[]{:S(2)}) collective-permute-start(bf16[4,2,16512]{2,1,0:T(2,128)(2,1)} %bitcast.6), channel_id=1, source_target_pairs={{0,4},{1,13},{4,0},{5,9},{8,12},{9,5},{12,8},{13,1},{2,6},{3,15},{... | collective-permute-start | bytes 792584 | tf_op jit(solution)/shard_map/ppermute | solution.py:369
  3.7 1.6 %weigh.1 = (bf16[16,12288]{1,0:T(8,128)(2,1)S(1)}, bf16[16,16512]{1,0:T(8,128)(2,1)S(1)}, bf16[16,16512]{1,0:T(8,128)(2,1)S(1)}, f32[16,128]{1,0:T(8,128)S(1)}, ...) custom-call(s32[8]{0:T(128)} %codes_in.1, bf16[1,8]{1,0:T(2,128)(2,1)} %bitcast.10, s32[1,4]{1,0:T(1,128)} %bitcast.11, ...), custom_call_target="tpu_custom_call" | custom-call | tf_op jit(solution)/shard_map/weigh/pallas_call | solution.py:378
  5.4 1.6 %collective-permute-start = (bf16[16,12288]{1,0:T(8,128)(2,1)S(1)}, bf16[16,12288]{1,0:T(8,128)(2,1)S(1)}, u32[]{:S(2)}, u32[]{:S(2)}) collective-permute-start(bf16[16,12288]{1,0:T(8,128)(2,1)S(1)} %get-tuple-element.23.first), channel_id=1, source_target_pairs={{0,2},{2,0},{1,3},{3,1},{4,6},{6,4},{5,7},{7,5},{8,10},{10,8},{9,1... | collective-permute-start | bytes 1179656 | tf_op jit(solution)/shard_map/ppermute | solution.py:374
  6.9 2.6 %collective-permute-start.4 = (bf16[2,2,16512]{2,1,0:T(2,128)(2,1)S(1)}, bf16[2,2,16512]{2,1,0:T(2,128)(2,1)S(1)}, u32[]{:S(2)}, u32[]{:S(2)}) collective-permute-start(bf16[2,2,16512]{2,1,0:T(2,128)(2,1)S(1)} %get-tuple-element.34), channel_id=1, source_target_pairs={{0,8},{4,12},{8,0},{12,4},{1,9},{5,13},{9,1},{13,5},{2,10},{6,14},... | collective-permute-start | bytes 396296 | tf_op jit(solution)/shard_map/ppermute | solution.py:423
  9.5 1.7 %collective-permute-done.2.refs_0_ = bf16[4,2,16512]{2,1,0:T(2,128)(2,1)S(1)} collective-permute-done((bf16[4,2,16512]{2,1,0:T(2,128)(2,1)}, bf16[4,2,16512]{2,1,0:T(2,128)(2,1)S(1)}, u32[]{:S(2)}, u32[]{:S(2)}) %collective-permute-start.2) | collective-permute-done | bytes 264224 | tf_op jit(solution)/shard_map/ppermute | solution.py:369
  11.2 0.0 collective-permute-start.3
  11.2 0.2 rest.1.refs_1_
  11.4 2.4 %collective-permute-start.1 = (bf16[16,4352]{1,0:T(8,128)(2,1)S(1)}, bf16[16,4352]{1,0:T(8,128)(2,1)S(1)}, u32[]{:S(2)}, u32[]{:S(2)}) collective-permute-start(bf16[16,4352]{1,0:T(8,128)(2,1)S(1)} %rest.1.refs_1_), channel_id=1, source_target_pairs={{0,2},{2,0},{1,3},{3,1},{4,6},{6,4},{5,7},{7,5},{8,10},{10,8},{9,1... | collective-permute-start | bytes 417800 | tf_op jit(solution)/shard_map/ppermute | solution.py:374
  13.8 3.1 %collective-permute-done.4.refs_0_ = bf16[2,2,16512]{2,1,0:T(2,128)(2,1)S(1)} collective-permute-done((bf16[2,2,16512]{2,1,0:T(2,128)(2,1)S(1)}, bf16[2,2,16512]{2,1,0:T(2,128)(2,1)S(1)}, u32[]{:S(2)}, u32[]{:S(2)}) %collective-permute-start.4) | collective-permute-done | bytes 132128 | tf_op jit(solution)/shard_map/ppermute | solution.py:423
  16.9 0.1 collective-permute-start.5
  17.0 2.3 %prepare.1 = (bf16[48,16512]{1,0:T(8,128)(2,1)S(1)}, f32[8,16512]{1,0:T(8,128)S(1)}, f32[8,16512]{1,0:T(8,128)S(1)}, bf16[56,16512]{1,0:T(8,128)(2,1)S(1)}, f32[56,48]{1,0:T(8,128)S(1)}) custom-call(bf16[16,12288]{1,0:T(8,128)(2,1)S(1)} %get-tuple-element.23.first, bf16[16,4352]{1,0:T(8,128)(2,1)S(1)} %rest.1.refs_1_, ...), custom_call_target="tpu_custom_call" | custom-call | tf_op jit(solution)/shard_map/prepare/pallas_call | solution.py:431
  19.3 1.5 %tables.3 = (bf16[56,16512]{1,0:T(8,128)(2,1)S(1)}, f32[56,48]{1,0:T(8,128)S(1)}) custom-call(bf16[48,16512]{1,0:T(8,128)(2,1)S(1)} %get-tuple-element.29.lhs, f32[8,16512]{1,0:T(8,128)S(1)} %get-tuple-element.30.cosines, f32[8,16512]{1,0:T(8,128)S(1)} %get-tuple-element.31.sines, bf16[4,2,16512]{2,1,0:T(2,128)(2,1)S(1)} %collective-permute-done.2.refs_0_), custom_call_target="tpu_custom_call" | custom-call | tf_op jit(solution)/shard_map/tables/pallas_call | solution.py:448
  20.8 0.0 collective-permute-done.5.refs_1_
  20.8 1.5 %tables.5 = (bf16[56,16512]{1,0:T(8,128)(2,1)S(1)}, f32[56,48]{1,0:T(8,128)S(1)}) custom-call(bf16[48,16512]{1,0:T(8,128)(2,1)S(1)} %get-tuple-element.29.lhs, f32[8,16512]{1,0:T(8,128)S(1)} %get-tuple-element.30.cosines, f32[8,16512]{1,0:T(8,128)S(1)} %get-tuple-element.31.sines, bf16[2,2,16512]{2,1,0:T(2,128)(2,1)S(1)} %collective-permute-done.4.refs_0_, ...), custom_call_target="tpu_custom_call" | custom-call | tf_op jit(solution)/shard_map/tables/pallas_call | solution.py:448
  22.2 0.0 collective-permute-done.3.refs_0_
  22.3 1.5 %tables.4 = (bf16[56,16512]{1,0:T(8,128)(2,1)S(1)}, f32[56,48]{1,0:T(8,128)S(1)}) custom-call(bf16[48,16512]{1,0:T(8,128)(2,1)S(1)} %get-tuple-element.29.lhs, f32[8,16512]{1,0:T(8,128)S(1)} %get-tuple-element.30.cosines, f32[8,16512]{1,0:T(8,128)S(1)} %get-tuple-element.31.sines, bf16[4,2,16512]{2,1,0:T(2,128)(2,1)S(1)} %collective-permute-done.3.refs_0_), custom_call_target="tpu_custom_call" | custom-call | tf_op jit(solution)/shard_map/tables/pallas_call | solution.py:448
  23.7 0.0 collective-permute-done.refs_3_.refs_0_
  23.7 0.9 %first.1.refs_11_ = f32[120,16]{1,0:T(8,128)S(1)} custom-call(bf16[56,16512]{1,0:T(8,128)(2,1)S(1)} %get-tuple-element.28.refs_0_.refs_3_, bf16[56,16512]{1,0:T(8,128)(2,1)S(1)} %get-tuple-element.32.refs_1_.refs_4_, bf16[56,16512]{1,0:T(8,128)(2,1)S(1)} %get-tuple-element.33.refs_2_.refs_5_, bf16[16,12288]{1,0:T(8,128)(2,1)S(1)} %collective-permute-done.refs_3_.refs_0_), custom_call_target="tpu_custom_call" | custom-call | tf_op jit(solution)/shard_map/first/pallas_call | solution.py:487
  24.7 0.0 collective-permute-done.1.refs_2_
  24.7 1.2 %last.1 = (f32[1,128]{1,0:T(1,128)S(1)}, f32[1,128]{1,0:T(1,128)S(1)}) custom-call(bf16[16,12288]{1,0:T(8,128)(2,1)S(1)} %collective-permute-done.refs_3_.refs_0_, bf16[16,4352]{1,0:T(8,128)(2,1)S(1)} %rest.1.refs_1_, bf16[16,4352]{1,0:T(8,128)(2,1)S(1)} %collective-permute-done.1.refs_2_, bf16[56,16512]{1,0:T(8,128)(2,1)S(1)} %get-tuple-element.28.refs_0_.refs_3_, ...), custom_call_target="tpu_custom_call" | custom-call | tf_op jit(solution)/shard_map/last/pallas_call | solution.py:464
  25.9 1.4 %collective-permute-start.6 = (f32[1,128]{1,0:T(1,128)S(1)}, f32[1,128]{1,0:T(1,128)S(1)}, u32[]{:S(2)}, u32[]{:S(2)}) collective-permute-start(f32[1,128]{1,0:T(1,128)S(1)} %get-tuple-element.41), channel_id=1, source_target_pairs={{0,2},{2,0},{1,3},{3,1},{4,6},{6,4},{5,7},{7,5},{8,10},{10,8},{9,1... | collective-permute-start | bytes 1544 | tf_op jit(solution)/shard_map/ppermute | solution.py:374
  27.3 2.1 %collective-permute-done.6.refs_1_ = f32[1,128]{1,0:T(1,128)S(1)} collective-permute-done((f32[1,128]{1,0:T(1,128)S(1)}, f32[1,128]{1,0:T(1,128)S(1)}, u32[]{:S(2)}, u32[]{:S(2)}) %collective-permute-start.6) | collective-permute-done | bytes 544 | tf_op jit(solution)/shard_map/ppermute | solution.py:374
  29.4 0.7 %finish.1 = (f32[2,8]{1,0:T(2,128)}, f32[1,8]{1,0:T(1,128)}) custom-call(f32[1,128]{1,0:T(1,128)S(1)} %get-tuple-element.40.refs_0_, f32[1,128]{1,0:T(1,128)S(1)} %collective-permute-done.6.refs_1_), custom_call_target="tpu_custom_call" | custom-call | tf_op jit(solution)/shard_map/finish/pallas_call | solution.py:504
Async XLA Ops:
  0.6 10.5 %collective-permute-start.2 = (bf16[4,2,16512]{2,1,0:T(2,128)(2,1)}, bf16[4,2,16512]{2,1,0:T(2,128)(2,1)S(1)}, u32[]{:S(2)}, u32[]{:S(2)}) collective-permute-start(bf16[4,2,16512]{2,1,0:T(2,128)(2,1)} %bitcast.6), channel_id=1, source_target_pairs={{0,4},{1,13},{4,0},{5,9},{8,12},{9,5},{12,8},{13,1},{2,6},{3,15},{... | collective-permute-start | bytes 792584 | tf_op jit(solution)/shard_map/ppermute | solution.py:369
  5.4 18.4 %collective-permute-start = (bf16[16,12288]{1,0:T(8,128)(2,1)S(1)}, bf16[16,12288]{1,0:T(8,128)(2,1)S(1)}, u32[]{:S(2)}, u32[]{:S(2)}) collective-permute-start(bf16[16,12288]{1,0:T(8,128)(2,1)S(1)} %get-tuple-element.23.first), channel_id=1, source_target_pairs={{0,2},{2,0},{1,3},{3,1},{4,6},{6,4},{5,7},{7,5},{8,10},{10,8},{9,1... | collective-permute-start | bytes 1179656 | tf_op jit(solution)/shard_map/ppermute | solution.py:374
  6.9 10.0 %collective-permute-start.4 = (bf16[2,2,16512]{2,1,0:T(2,128)(2,1)S(1)}, bf16[2,2,16512]{2,1,0:T(2,128)(2,1)S(1)}, u32[]{:S(2)}, u32[]{:S(2)}) collective-permute-start(bf16[2,2,16512]{2,1,0:T(2,128)(2,1)S(1)} %get-tuple-element.34), channel_id=1, source_target_pairs={{0,8},{4,12},{8,0},{12,4},{1,9},{5,13},{9,1},{13,5},{2,10},{6,14},... | collective-permute-start | bytes 396296 | tf_op jit(solution)/shard_map/ppermute | solution.py:423
  11.2 11.1 %collective-permute-start.3 = (bf16[4,2,16512]{2,1,0:T(2,128)(2,1)S(1)}, bf16[4,2,16512]{2,1,0:T(2,128)(2,1)S(1)}, u32[]{:S(2)}, u32[]{:S(2)}) collective-permute-start(bf16[4,2,16512]{2,1,0:T(2,128)(2,1)S(1)} %collective-permute-done.2.refs_0_), channel_id=1, source_target_pairs={{0,1},{1,0},{2,3},{3,2},{4,5},{5,4},{6,7},{7,6},{8,9},{9,8},{10,11... | collective-permute-start | bytes 792584 | tf_op jit(solution)/shard_map/ppermute | solution.py:477
  11.4 13.3 %collective-permute-start.1 = (bf16[16,4352]{1,0:T(8,128)(2,1)S(1)}, bf16[16,4352]{1,0:T(8,128)(2,1)S(1)}, u32[]{:S(2)}, u32[]{:S(2)}) collective-permute-start(bf16[16,4352]{1,0:T(8,128)(2,1)S(1)} %rest.1.refs_1_), channel_id=1, source_target_pairs={{0,2},{2,0},{1,3},{3,1},{4,6},{6,4},{5,7},{7,5},{8,10},{10,8},{9,1... | collective-permute-start | bytes 417800 | tf_op jit(solution)/shard_map/ppermute | solution.py:374
  16.9 3.9 %collective-permute-start.5 = (bf16[2,2,16512]{2,1,0:T(2,128)(2,1)S(1)}, bf16[2,2,16512]{2,1,0:T(2,128)(2,1)S(1)}, u32[]{:S(2)}, u32[]{:S(2)}) collective-permute-start(bf16[2,2,16512]{2,1,0:T(2,128)(2,1)S(1)} %collective-permute-done.4.refs_0_), channel_id=1, source_target_pairs={{0,1},{1,0},{2,3},{3,2},{4,5},{5,4},{6,7},{7,6},{8,9},{9,8},{10,11... | collective-permute-start | bytes 396296 | tf_op jit(solution)/shard_map/ppermute | solution.py:480
  25.9 3.6 %collective-permute-start.6 = (f32[1,128]{1,0:T(1,128)S(1)}, f32[1,128]{1,0:T(1,128)S(1)}, u32[]{:S(2)}, u32[]{:S(2)}) collective-permute-start(f32[1,128]{1,0:T(1,128)S(1)} %get-tuple-element.41), channel_id=1, source_target_pairs={{0,2},{2,0},{1,3},{3,1},{4,6},{6,4},{5,7},{7,5},{8,10},{10,8},{9,1... | collective-permute-start | bytes 1544 | tf_op jit(solution)/shard_map/ppermute | solution.py:374

commit v5 on v4

--- a/solution.py
+++ b/solution.py
@@ -52,8 +52,6 @@
         pltpu.make_async_copy(beta_in, beta, small_sem.at[2]),
         pltpu.make_async_copy(offsets_in, offsets, small_sem.at[3]),
     ]
-    for copy in small:
-        copy.start()
     cut, pixels = first.shape[1], raw.shape[1]
     spans = (slice(0, cut), slice(cut, pixels))
     loads = []
@@ -68,6 +66,9 @@
         loads.append(copies)
         for copy in copies:
             copy.start()
+        if b == 0:
+            for copy in small:
+                copy.start()
     half_copy = pltpu.make_async_copy(
         refs.at[pl.ds(lax.axis_index("dom") * half, half)], part, half_sem
     )
@@ -88,20 +89,20 @@
             group = groups[s, p // per_block].astype(F32)
             extra = jnp.where(mine & (column == 2 + s), group, extra)
     extra = jnp.where(column == 0, code.astype(F32), extra)
+    phases = turns.shape[1:]
+    step_x = jnp.zeros(phases, jnp.int32)
+    step_y = jnp.zeros(phases, jnp.int32)
+    for t in range(offsets.shape[1]):
+        step_x = jnp.where(iota(phases, 0) == t, offsets[0, t], step_x)
+        step_y = jnp.where(iota(phases, 0) == t, offsets[1, t], step_y)
+    turns[0] = step_x * iota(phases, 1) - step_y * (KY // 2)
+    turns[1] = step_y - step_x
+    turns[2] = step_x * KX - step_y
     pick = picked(code, n_codes)
     for copy in loads[0]:
         copy.wait()
     first[...], power = weighted(pick, ctf, raw, spans[0])
     more[...] = jnp.where(column == 2 + sig, power, extra)
-    shape = turns.shape[1:]
-    step_x = jnp.zeros(shape, jnp.int32)
-    step_y = jnp.zeros(shape, jnp.int32)
-    for t in range(offsets.shape[1]):
-        step_x = jnp.where(iota(shape, 0) == t, offsets[0, t], step_x)
-        step_y = jnp.where(iota(shape, 0) == t, offsets[1, t], step_y)
-    turns[0] = step_x * iota(shape, 1) - step_y * (KY // 2)
-    turns[1] = step_y - step_x
-    turns[2] = step_x * KX - step_y
     half_copy.wait()
     for copy in loads[1]:
         copy.wait()
@@ -146,7 +147,7 @@
             copy.start()
 
 
-def build_table(sources, raw, sem, cosines, sines, lhs, table, product, shifts):
+def build_table(sources, raw, sem, cosines, sines, lhs, table, product, shifts, images=(), cross=None):
     n = raw.shape[0]
     odd = iota((n, LANES), 0) % 2 == 1
     count = sem.shape[0]
@@ -175,9 +176,20 @@
         return lax.fori_loop(0, width, step, carry, unroll=min(UNROLL, width))
 
     lax.fori_loop(0, count, block, 0)
-    product[...] = lax.dot_general(
-        table[...], lhs[...], CONTRACT_LAST, preferred_element_type=F32
-    )
+    if not images:
+        product[...] = lax.dot_general(
+            table[...], lhs[...], CONTRACT_LAST, preferred_element_type=F32
+        )
+        return
+    cut, width = images[0].shape[1], lhs.shape[0]
+    right = jnp.concatenate([lhs[:, :cut]] + [image[...] for image in images], axis=0)
+    both = lax.dot_general(
+        table[:, :cut], right, CONTRACT_LAST, preferred_element_type=F32
+    )
+    product[...] = both[:, :width] + lax.dot_general(
+        table[:, cut:], lhs[:, cut:], CONTRACT_LAST, preferred_element_type=F32
+    )
+    cross[...] = both[: cross.shape[0], width:]
 
 
 def prepare_kernel(shifts, first, rest, ctf, turns, refs, lhs, cosines, sines, table, product, raw, sem):
@@ -216,10 +228,13 @@
     build_table([refs], raw, sem, cosines, sines, lhs, table, product, shifts)
 
 
-def tables_kernel(shifts, lhs, cosines, sines, *refs):
-    table, product, raw, sem = refs[-4:]
-    load_blocks(refs[:-4], raw, sem)
-    build_table(refs[:-4], raw, sem, cosines, sines, lhs, table, product, shifts)
+def tables_kernel(shifts, n_other, lhs, cosines, sines, *refs):
+    images, refs = refs[:n_other], refs[n_other:]
+    raw, sem = refs[-2:]
+    n_out = 3 if images else 2
+    pieces, outs = refs[: -2 - n_out], refs[-2 - n_out : -2]
+    load_blocks(pieces, raw, sem)
+    build_table(pieces, raw, sem, cosines, sines, lhs, outs[0], outs[1], shifts, images, outs[-1])
 
 
 def against(tables, used, span, images):
@@ -240,7 +255,7 @@
 
 
 def last_kernel(dims, *refs):
-    n_img, known, steps, shifts, tiles, sig, n = dims
+    n_img, n_early, steps, shifts, tiles, sig, n = dims
     count = len(steps)
     refs = list(refs)
     z, d = lax.axis_index("orient"), lax.axis_index("dom")
@@ -248,7 +263,7 @@
     rests = [refs.pop(0) for _ in range(n_img)]
     tables = [refs.pop(0) for _ in range(count)]
     products = [refs.pop(0) for _ in range(count)]
-    early = refs.pop(0) if known else None
+    starts = [refs.pop(0)[...] for _ in range(n_early)]
     outs = refs
     pixels = tiles * LANES
     rows = rests[0].shape[0]
@@ -258,9 +273,8 @@
     beyond = rests[0].shape[1] - LANES
 
     crossed = against(tables, used, slice(pixels - beyond, pixels), rests[1:])
-    starts = [early[...]] if known else []
-    if known < count:
-        starts.append(against(tables[known:], used, slice(0, pixels - beyond), firsts))
+    if not starts:
+        starts = [against(tables, used, slice(0, pixels - beyond), firsts)]
     crossed = crossed + (jnp.concatenate(starts, axis=0) if len(starts) > 1 else starts[0])
     extra = jnp.concatenate([rest[:, beyond:] for rest in rests], axis=0)
     take = (iota((16, LANES), 0) == iota((16, LANES), 1)).astype(BF16)
@@ -444,25 +458,31 @@
         compiler_params=pltpu.CompilerParams(vmem_limit_bytes=16 << 20),
     )(first, rest, ctf_near, turns, in_hbm(refs_own))
 
-    def make_table(*pieces):
+    def make_table(*pieces, images=()):
+        outs = [
+            jax.ShapeDtypeStruct((used, pixels), BF16),
+            jax.ShapeDtypeStruct((used, lhs_rows), F32),
+        ]
+        if images:
+            outs.append(
+                jax.ShapeDtypeStruct((shifts * n, len(images) * 2 * rows), F32)
+            )
         return pl.pallas_call(
-            functools.partial(tables_kernel, shifts),
+            functools.partial(tables_kernel, shifts, len(images)),
             name="tables",
-            out_shape=[
-                jax.ShapeDtypeStruct((used, pixels), BF16),
-                jax.ShapeDtypeStruct((used, lhs_rows), F32),
-            ],
-            in_specs=[vmem, vmem, vmem] + [anywhere] * len(pieces),
-            out_specs=[vmem, vmem],
-            scratch_shapes=[pltpu.VMEM((n, pixels), BF16), dma((n_blocks,))],
+            out_shape=outs,
+            in_specs=[vmem] * (3 + len(images)) + [anywhere] * len(pieces),
+            out_specs=[vmem] * len(outs),
+            scratch_shapes=[pltpu.VMEM((n, pixels), BF16), dma((1,))],
             compiler_params=pltpu.CompilerParams(vmem_limit_bytes=12 << 20),
-        )(lhs, cosines, sines, *pieces)
+        )(lhs, cosines, sines, *images, *pieces)
 
     def evaluate(group, early=()):
         steps, tables, products = zip(*group)
-        known = early[0].shape[0] // (shifts * n) if early else 0
         return pl.pallas_call(
-            functools.partial(last_kernel, (n_img, known, steps, shifts, tiles, sig, n)),
+            functools.partial(
+                last_kernel, (n_img, len(early), steps, shifts, tiles, sig, n)
+            ),
             name="last",
             out_shape=[jax.ShapeDtypeStruct((1, LANES), F32)] * n_img,
             in_specs=[vmem] * (2 * n_img - 1 + 2 * len(group) + len(early)),
@@ -478,7 +498,10 @@
         made.append(((low, high), *make_table(near)))
         made.append(((high, low), *make_table(mate)))
     far_half = lax.ppermute(near_half, "dom", swap)
-    made.append(((last, last), *make_table(near_half, far_half)))
+    late_table, late_product, late_cross = make_table(
+        near_half, far_half, images=firsts
+    )
+    made.append(((last, last), late_table, late_product))
     found = []
     while len(made) > SET:
         found.append(evaluate(made[:SET]))
@@ -496,7 +519,7 @@
             vmem_limit_bytes=(12 << 20) if n_img < 4 else (40 << 20)
         ),
     )(*ready, *firsts)
-    found.append(evaluate(made, (early,)))
+    found.append(evaluate(made, (early, late_cross)))
     evidence = found[0]
     for more in found[1:]:
         evidence = [a + b for a, b in zip(evidence, more)]

time: 30.3 us -> 30 us (0.990)
    pallas_call x4, Pallas kernels: 5.53 us -> 5.22 us  [the longest x3 4.36 us: make_table(): pl.pallas_call(functools.partial(tables_kernel, shifts, len(images)), nam...]
where the time goes in v5:
time: 30 us; the launch traced here: 29.9 us
  starting transfers between devices  11.2 us (37%)
  Pallas kernels  11 us (37%)
  waiting for transfers between devices  6.92 us (23%)
  between operations  0.72 us (2%)
    ppermute x3, starting transfers between devices, across(): return lax.ppermute(values, 'cls', [(c, c ^ k) for c in range(n_cls)])  5.39 us
    pallas_call x3, Pallas kernels, make_table(): pl.pallas_call(functools.partial(tables_kernel, shifts, len(images)), nam...  4.36 us
    ppermute x1, starting transfers between devices, local(): lax.ppermute(refs_own, ('orient', 'dom'), core_step(low, high))  3.12 us
    ppermute x1, waiting for transfers between devices, local(): lax.ppermute(part, 'orient', [(a, a ^ last) for a in range(groups)])  3.11 us
    ppermute x1, starting transfers between devices, local(): lax.ppermute(part, 'orient', [(a, a ^ last) for a in range(groups)])  2.59 us
    pallas_call x1, Pallas kernels, local(): pl.pallas_call(functools.partial(prepare_kernel, shifts), name='prepare',...  2.28 us
    ppermute x3, waiting for transfers between devices, across(): return lax.ppermute(values, 'cls', [(c, c ^ k) for c in range(n_cls)])  2.14 us
    ppermute x1, waiting for transfers between devices, local(): lax.ppermute(refs_own, ('orient', 'dom'), core_step(low, high))  1.67 us
  transfers between devices with their start and end apart: 7, of which 3 were waited for; matrix products, arithmetic and copies ran while one was open for 0% of the time, Pallas kernels for 31%

profile of v5, /device:TPU:0, one launch (start us, length us, event | category | flops | bytes accessed | tf_op | source)
XLA Modules:
  0.0 29.9 jit_solution(17767145681720619193)
XLA Ops:
  0.6 3.1 %collective-permute-start.2 = (bf16[4,2,16512]{2,1,0:T(2,128)(2,1)}, bf16[4,2,16512]{2,1,0:T(2,128)(2,1)S(1)}, u32[]{:S(2)}, u32[]{:S(2)}) collective-permute-start(bf16[4,2,16512]{2,1,0:T(2,128)(2,1)} %bitcast.6), channel_id=1, source_target_pairs={{0,4},{1,13},{4,0},{5,9},{8,12},{9,5},{12,8},{13,1},{2,6},{3,15},{... | collective-permute-start | bytes 792584 | tf_op jit(solution)/shard_map/ppermute | solution.py:383
  3.7 1.6 %weigh.1 = (bf16[16,12288]{1,0:T(8,128)(2,1)S(1)}, bf16[16,16512]{1,0:T(8,128)(2,1)S(1)}, bf16[16,16512]{1,0:T(8,128)(2,1)S(1)}, f32[16,128]{1,0:T(8,128)S(1)}, ...) custom-call(s32[8]{0:T(128)} %codes_in.1, bf16[1,8]{1,0:T(2,128)(2,1)} %bitcast.10, s32[1,4]{1,0:T(1,128)} %bitcast.11, ...), custom_call_target="tpu_custom_call" | custom-call | tf_op jit(solution)/shard_map/weigh/pallas_call | solution.py:392
  5.3 1.6 %collective-permute-start = (bf16[16,12288]{1,0:T(8,128)(2,1)S(1)}, bf16[16,12288]{1,0:T(8,128)(2,1)S(1)}, u32[]{:S(2)}, u32[]{:S(2)}) collective-permute-start(bf16[16,12288]{1,0:T(8,128)(2,1)S(1)} %get-tuple-element.24.first), channel_id=1, source_target_pairs={{0,2},{2,0},{1,3},{3,1},{4,6},{6,4},{5,7},{7,5},{8,10},{10,8},{9,1... | collective-permute-start | bytes 1179656 | tf_op jit(solution)/shard_map/ppermute | solution.py:388
  6.9 2.6 %collective-permute-start.4 = (bf16[2,2,16512]{2,1,0:T(2,128)(2,1)S(1)}, bf16[2,2,16512]{2,1,0:T(2,128)(2,1)S(1)}, u32[]{:S(2)}, u32[]{:S(2)}) collective-permute-start(bf16[2,2,16512]{2,1,0:T(2,128)(2,1)S(1)} %get-tuple-element.35), channel_id=1, source_target_pairs={{0,8},{4,12},{8,0},{12,4},{1,9},{5,13},{9,1},{13,5},{2,10},{6,14},... | collective-permute-start | bytes 396296 | tf_op jit(solution)/shard_map/ppermute | solution.py:437
  9.5 1.7 %collective-permute-done.2.refs_0_ = bf16[4,2,16512]{2,1,0:T(2,128)(2,1)S(1)} collective-permute-done((bf16[4,2,16512]{2,1,0:T(2,128)(2,1)}, bf16[4,2,16512]{2,1,0:T(2,128)(2,1)S(1)}, u32[]{:S(2)}, u32[]{:S(2)}) %collective-permute-start.2) | collective-permute-done | bytes 264224 | tf_op jit(solution)/shard_map/ppermute | solution.py:383
  11.2 0.0 collective-permute-start.3
  11.2 0.2 rest.1.refs_1_
  11.4 2.4 %collective-permute-start.1 = (bf16[16,4352]{1,0:T(8,128)(2,1)S(1)}, bf16[16,4352]{1,0:T(8,128)(2,1)S(1)}, u32[]{:S(2)}, u32[]{:S(2)}) collective-permute-start(bf16[16,4352]{1,0:T(8,128)(2,1)S(1)} %rest.1.refs_1_), channel_id=1, source_target_pairs={{0,2},{2,0},{1,3},{3,1},{4,6},{6,4},{5,7},{7,5},{8,10},{10,8},{9,1... | collective-permute-start | bytes 417800 | tf_op jit(solution)/shard_map/ppermute | solution.py:388
  13.8 3.1 %collective-permute-done.4.refs_1_ = bf16[2,2,16512]{2,1,0:T(2,128)(2,1)S(1)} collective-permute-done((bf16[2,2,16512]{2,1,0:T(2,128)(2,1)S(1)}, bf16[2,2,16512]{2,1,0:T(2,128)(2,1)S(1)}, u32[]{:S(2)}, u32[]{:S(2)}) %collective-permute-start.4) | collective-permute-done | bytes 132128 | tf_op jit(solution)/shard_map/ppermute | solution.py:437
  16.9 0.1 collective-permute-start.5
  17.0 2.3 %prepare.1 = (bf16[48,16512]{1,0:T(8,128)(2,1)S(1)}, f32[8,16512]{1,0:T(8,128)S(1)}, f32[8,16512]{1,0:T(8,128)S(1)}, bf16[56,16512]{1,0:T(8,128)(2,1)S(1)}, f32[56,48]{1,0:T(8,128)S(1)}) custom-call(bf16[16,12288]{1,0:T(8,128)(2,1)S(1)} %get-tuple-element.24.first, bf16[16,4352]{1,0:T(8,128)(2,1)S(1)} %rest.1.refs_1_, ...), custom_call_target="tpu_custom_call" | custom-call | tf_op jit(solution)/shard_map/prepare/pallas_call | solution.py:445
  19.3 1.4 %tables.3 = (bf16[56,16512]{1,0:T(8,128)(2,1)S(1)}, f32[56,48]{1,0:T(8,128)S(1)}) custom-call(bf16[48,16512]{1,0:T(8,128)(2,1)S(1)} %get-tuple-element.30.lhs, f32[8,16512]{1,0:T(8,128)S(1)} %get-tuple-element.31.cosines, f32[8,16512]{1,0:T(8,128)S(1)} %get-tuple-element.32.sines, bf16[4,2,16512]{2,1,0:T(2,128)(2,1)S(1)} %collective-permute-done.2.refs_0_), custom_call_target="tpu_custom_call" | custom-call | tf_op jit(solution)/shard_map/tables/pallas_call | solution.py:470
  20.7 0.0 collective-permute-done.5.refs_2_
  20.8 0.0 collective-permute-done.refs_0_.refs_3_
  20.8 1.5 %tables.5 = (bf16[56,16512]{1,0:T(8,128)(2,1)S(1)}, f32[56,48]{1,0:T(8,128)S(1)}, f32[40,16]{1,0:T(8,128)S(1)}) custom-call(bf16[48,16512]{1,0:T(8,128)(2,1)S(1)} %get-tuple-element.30.lhs, f32[8,16512]{1,0:T(8,128)S(1)} %get-tuple-element.31.cosines, f32[8,16512]{1,0:T(8,128)S(1)} %get-tuple-element.32.sines, ...), custom_call_target="tpu_custom_call" | custom-call | tf_op jit(solution)/shard_map/tables/pallas_call | solution.py:470
  22.3 0.0 collective-permute-done.3.refs_0_
  22.3 1.4 %tables.4 = (bf16[56,16512]{1,0:T(8,128)(2,1)S(1)}, f32[56,48]{1,0:T(8,128)S(1)}) custom-call(bf16[48,16512]{1,0:T(8,128)(2,1)S(1)} %get-tuple-element.30.lhs, f32[8,16512]{1,0:T(8,128)S(1)} %get-tuple-element.31.cosines, f32[8,16512]{1,0:T(8,128)S(1)} %get-tuple-element.32.sines, bf16[4,2,16512]{2,1,0:T(2,128)(2,1)S(1)} %collective-permute-done.3.refs_0_), custom_call_target="tpu_custom_call" | custom-call | tf_op jit(solution)/shard_map/tables/pallas_call | solution.py:470
  23.7 0.9 %first.1.refs_11_ = f32[120,16]{1,0:T(8,128)S(1)} custom-call(bf16[56,16512]{1,0:T(8,128)(2,1)S(1)} %get-tuple-element.29.refs_0_.refs_3_, bf16[56,16512]{1,0:T(8,128)(2,1)S(1)} %get-tuple-element.33.refs_1_.refs_4_, bf16[56,16512]{1,0:T(8,128)(2,1)S(1)} %get-tuple-element.34.refs_2_.refs_5_, bf16[16,12288]{1,0:T(8,128)(2,1)S(1)} %collective-permute-done.refs_0_.refs_3_), custom_call_target="tpu_custom_call" | custom-call | tf_op jit(solution)/shard_map/first/pallas_call | solution.py:510
  24.7 0.0 collective-permute-done.1.refs_2_
  24.7 0.9 %last.1 = (f32[1,128]{1,0:T(1,128)S(1)}, f32[1,128]{1,0:T(1,128)S(1)}) custom-call(bf16[16,12288]{1,0:T(8,128)(2,1)S(1)} %collective-permute-done.refs_0_.refs_3_, bf16[16,4352]{1,0:T(8,128)(2,1)S(1)} %rest.1.refs_1_, bf16[16,4352]{1,0:T(8,128)(2,1)S(1)} %collective-permute-done.1.refs_2_, bf16[56,16512]{1,0:T(8,128)(2,1)S(1)} %get-tuple-element.29.refs_0_.refs_3_, ...), custom_call_target="tpu_custom_call" | custom-call | tf_op jit(solution)/shard_map/last/pallas_call | solution.py:482
  25.5 1.4 %collective-permute-start.6 = (f32[1,128]{1,0:T(1,128)S(1)}, f32[1,128]{1,0:T(1,128)S(1)}, u32[]{:S(2)}, u32[]{:S(2)}) collective-permute-start(f32[1,128]{1,0:T(1,128)S(1)} %get-tuple-element.43), channel_id=1, source_target_pairs={{0,2},{2,0},{1,3},{3,1},{4,6},{6,4},{5,7},{7,5},{8,10},{10,8},{9,1... | collective-permute-start | bytes 1544 | tf_op jit(solution)/shard_map/ppermute | solution.py:388
  27.0 2.1 %collective-permute-done.6.refs_1_ = f32[1,128]{1,0:T(1,128)S(1)} collective-permute-done((f32[1,128]{1,0:T(1,128)S(1)}, f32[1,128]{1,0:T(1,128)S(1)}, u32[]{:S(2)}, u32[]{:S(2)}) %collective-permute-start.6) | collective-permute-done | bytes 544 | tf_op jit(solution)/shard_map/ppermute | solution.py:388
  29.1 0.7 %finish.1 = (f32[2,8]{1,0:T(2,128)}, f32[1,8]{1,0:T(1,128)}) custom-call(f32[1,128]{1,0:T(1,128)S(1)} %get-tuple-element.42.refs_0_, f32[1,128]{1,0:T(1,128)S(1)} %collective-permute-done.6.refs_1_), custom_call_target="tpu_custom_call" | custom-call | tf_op jit(solution)/shard_map/finish/pallas_call | solution.py:527
Async XLA Ops:
  0.6 10.5 %collective-permute-start.2 = (bf16[4,2,16512]{2,1,0:T(2,128)(2,1)}, bf16[4,2,16512]{2,1,0:T(2,128)(2,1)S(1)}, u32[]{:S(2)}, u32[]{:S(2)}) collective-permute-start(bf16[4,2,16512]{2,1,0:T(2,128)(2,1)} %bitcast.6), channel_id=1, source_target_pairs={{0,4},{1,13},{4,0},{5,9},{8,12},{9,5},{12,8},{13,1},{2,6},{3,15},{... | collective-permute-start | bytes 792584 | tf_op jit(solution)/shard_map/ppermute | solution.py:383
  5.3 15.4 %collective-permute-start = (bf16[16,12288]{1,0:T(8,128)(2,1)S(1)}, bf16[16,12288]{1,0:T(8,128)(2,1)S(1)}, u32[]{:S(2)}, u32[]{:S(2)}) collective-permute-start(bf16[16,12288]{1,0:T(8,128)(2,1)S(1)} %get-tuple-element.24.first), channel_id=1, source_target_pairs={{0,2},{2,0},{1,3},{3,1},{4,6},{6,4},{5,7},{7,5},{8,10},{10,8},{9,1... | collective-permute-start | bytes 1179656 | tf_op jit(solution)/shard_map/ppermute | solution.py:388
  6.9 10.0 %collective-permute-start.4 = (bf16[2,2,16512]{2,1,0:T(2,128)(2,1)S(1)}, bf16[2,2,16512]{2,1,0:T(2,128)(2,1)S(1)}, u32[]{:S(2)}, u32[]{:S(2)}) collective-permute-start(bf16[2,2,16512]{2,1,0:T(2,128)(2,1)S(1)} %get-tuple-element.35), channel_id=1, source_target_pairs={{0,8},{4,12},{8,0},{12,4},{1,9},{5,13},{9,1},{13,5},{2,10},{6,14},... | collective-permute-start | bytes 396296 | tf_op jit(solution)/shard_map/ppermute | solution.py:437
  11.2 11.1 %collective-permute-start.3 = (bf16[4,2,16512]{2,1,0:T(2,128)(2,1)S(1)}, bf16[4,2,16512]{2,1,0:T(2,128)(2,1)S(1)}, u32[]{:S(2)}, u32[]{:S(2)}) collective-permute-start(bf16[4,2,16512]{2,1,0:T(2,128)(2,1)S(1)} %collective-permute-done.2.refs_0_), channel_id=1, source_target_pairs={{0,1},{1,0},{2,3},{3,2},{4,5},{5,4},{6,7},{7,6},{8,9},{9,8},{10,11... | collective-permute-start | bytes 792584 | tf_op jit(solution)/shard_map/ppermute | solution.py:497
  11.4 13.3 %collective-permute-start.1 = (bf16[16,4352]{1,0:T(8,128)(2,1)S(1)}, bf16[16,4352]{1,0:T(8,128)(2,1)S(1)}, u32[]{:S(2)}, u32[]{:S(2)}) collective-permute-start(bf16[16,4352]{1,0:T(8,128)(2,1)S(1)} %rest.1.refs_1_), channel_id=1, source_target_pairs={{0,2},{2,0},{1,3},{3,1},{4,6},{6,4},{5,7},{7,5},{8,10},{10,8},{9,1... | collective-permute-start | bytes 417800 | tf_op jit(solution)/shard_map/ppermute | solution.py:388
  16.9 3.8 %collective-permute-start.5 = (bf16[2,2,16512]{2,1,0:T(2,128)(2,1)S(1)}, bf16[2,2,16512]{2,1,0:T(2,128)(2,1)S(1)}, u32[]{:S(2)}, u32[]{:S(2)}) collective-permute-start(bf16[2,2,16512]{2,1,0:T(2,128)(2,1)S(1)} %collective-permute-done.4.refs_1_), channel_id=1, source_target_pairs={{0,1},{1,0},{2,3},{3,2},{4,5},{5,4},{6,7},{7,6},{8,9},{9,8},{10,11... | collective-permute-start | bytes 396296 | tf_op jit(solution)/shard_map/ppermute | solution.py:500
  25.5 3.6 %collective-permute-start.6 = (f32[1,128]{1,0:T(1,128)S(1)}, f32[1,128]{1,0:T(1,128)S(1)}, u32[]{:S(2)}, u32[]{:S(2)}) collective-permute-start(f32[1,128]{1,0:T(1,128)S(1)} %get-tuple-element.43), channel_id=1, source_target_pairs={{0,2},{2,0},{1,3},{3,1},{4,6},{6,4},{5,7},{7,5},{8,10},{10,8},{9,1... | collective-permute-start | bytes 1544 | tf_op jit(solution)/shard_map/ppermute | solution.py:388

commit v6 on v5

--- a/solution.py
+++ b/solution.py
@@ -52,6 +52,8 @@
         pltpu.make_async_copy(beta_in, beta, small_sem.at[2]),
         pltpu.make_async_copy(offsets_in, offsets, small_sem.at[3]),
     ]
+    for copy in small:
+        copy.start()
     cut, pixels = first.shape[1], raw.shape[1]
     spans = (slice(0, cut), slice(cut, pixels))
     loads = []
@@ -66,9 +68,6 @@
         loads.append(copies)
         for copy in copies:
             copy.start()
-        if b == 0:
-            for copy in small:
-                copy.start()
     half_copy = pltpu.make_async_copy(
         refs.at[pl.ds(lax.axis_index("dom") * half, half)], part, half_sem
     )
@@ -89,20 +88,20 @@
             group = groups[s, p // per_block].astype(F32)
             extra = jnp.where(mine & (column == 2 + s), group, extra)
     extra = jnp.where(column == 0, code.astype(F32), extra)
-    phases = turns.shape[1:]
-    step_x = jnp.zeros(phases, jnp.int32)
-    step_y = jnp.zeros(phases, jnp.int32)
-    for t in range(offsets.shape[1]):
-        step_x = jnp.where(iota(phases, 0) == t, offsets[0, t], step_x)
-        step_y = jnp.where(iota(phases, 0) == t, offsets[1, t], step_y)
-    turns[0] = step_x * iota(phases, 1) - step_y * (KY // 2)
-    turns[1] = step_y - step_x
-    turns[2] = step_x * KX - step_y
     pick = picked(code, n_codes)
     for copy in loads[0]:
         copy.wait()
     first[...], power = weighted(pick, ctf, raw, spans[0])
     more[...] = jnp.where(column == 2 + sig, power, extra)
+    shape = turns.shape[1:]
+    step_x = jnp.zeros(shape, jnp.int32)
+    step_y = jnp.zeros(shape, jnp.int32)
+    for t in range(offsets.shape[1]):
+        step_x = jnp.where(iota(shape, 0) == t, offsets[0, t], step_x)
+        step_y = jnp.where(iota(shape, 0) == t, offsets[1, t], step_y)
+    turns[0] = step_x * iota(shape, 1) - step_y * (KY // 2)
+    turns[1] = step_y - step_x
+    turns[2] = step_x * KX - step_y
     half_copy.wait()
     for copy in loads[1]:
         copy.wait()
@@ -302,7 +301,7 @@
     for c in range(count):
         energy = energies[2 * c * n : (2 * c + 1) * n] + energies[(2 * c + 1) * n : (2 * c + 2) * n]
         energy = energy + pltpu.roll(energy, n - 1, 0)
-        scale = beta / jnp.sqrt(power * energy + EPSILON)
+        scale = beta * lax.rsqrt(power * energy + EPSILON)
         cross = jnp.concatenate(
             [products[c][:used, :rows], crossed[c * used : (c + 1) * used]], axis=1
         )
@@ -473,7 +472,7 @@
             out_shape=outs,
             in_specs=[vmem] * (3 + len(images)) + [anywhere] * len(pieces),
             out_specs=[vmem] * len(outs),
-            scratch_shapes=[pltpu.VMEM((n, pixels), BF16), dma((1,))],
+            scratch_shapes=[pltpu.VMEM((n, pixels), BF16), dma((n_blocks,))],
             compiler_params=pltpu.CompilerParams(vmem_limit_bytes=12 << 20),
         )(lhs, cosines, sines, *images, *pieces)
 

time: 30 us -> 30.1 us (level)
  transfers between devices with their start and end apart: 7 -> 7, of which waited for: 3 -> 3; matrix products, arithmetic and copies ran while one was open for 0% -> 0% of each run, Pallas kernels for 31% -> 32%
where the time goes in v6:
time: 30.1 us; the launch traced here: 29.9 us
  starting transfers between devices  11.2 us (37%)
  Pallas kernels  11.1 us (37%)
  waiting for transfers between devices  6.92 us (23%)
  between operations  0.72 us (2%)
    ppermute x3, starting transfers between devices, across(): return lax.ppermute(values, 'cls', [(c, c ^ k) for c in range(n_cls)])  5.37 us
    pallas_call x3, Pallas kernels, make_table(): pl.pallas_call(functools.partial(tables_kernel, shifts, len(images)), nam...  4.43 us
    ppermute x1, starting transfers between devices, local(): lax.ppermute(refs_own, ('orient', 'dom'), core_step(low, high))  3.12 us
    ppermute x1, waiting for transfers between devices, local(): lax.ppermute(part, 'orient', [(a, a ^ last) for a in range(groups)])  3.11 us
    ppermute x1, starting transfers between devices, local(): lax.ppermute(part, 'orient', [(a, a ^ last) for a in range(groups)])  2.6 us
    pallas_call x1, Pallas kernels, local(): pl.pallas_call(functools.partial(prepare_kernel, shifts), name='prepare',...  2.28 us
    ppermute x3, waiting for transfers between devices, across(): return lax.ppermute(values, 'cls', [(c, c ^ k) for c in range(n_cls)])  2.14 us
    ppermute x1, waiting for transfers between devices, local(): lax.ppermute(refs_own, ('orient', 'dom'), core_step(low, high))  1.66 us
  transfers between devices with their start and end apart: 7, of which 3 were waited for; matrix products, arithmetic and copies ran while one was open for 0% of the time, Pallas kernels for 32%

profile of v6, /device:TPU:0, one launch (start us, length us, event | category | flops | bytes accessed | tf_op | source)
XLA Modules:
  0.0 29.9 jit_solution(1027247460323531834)
XLA Ops:
  0.6 3.1 %collective-permute-start.2 = (bf16[4,2,16512]{2,1,0:T(2,128)(2,1)}, bf16[4,2,16512]{2,1,0:T(2,128)(2,1)S(1)}, u32[]{:S(2)}, u32[]{:S(2)}) collective-permute-start(bf16[4,2,16512]{2,1,0:T(2,128)(2,1)} %bitcast.6), channel_id=1, source_target_pairs={{0,4},{1,13},{4,0},{5,9},{8,12},{9,5},{12,8},{13,1},{2,6},{3,15},{... | collective-permute-start | bytes 792584 | tf_op jit(solution)/shard_map/ppermute | solution.py:382
  3.7 1.6 %weigh.1 = (bf16[16,12288]{1,0:T(8,128)(2,1)S(1)}, bf16[16,16512]{1,0:T(8,128)(2,1)S(1)}, bf16[16,16512]{1,0:T(8,128)(2,1)S(1)}, f32[16,128]{1,0:T(8,128)S(1)}, ...) custom-call(s32[8]{0:T(128)} %codes_in.1, bf16[1,8]{1,0:T(2,128)(2,1)} %bitcast.10, s32[1,4]{1,0:T(1,128)} %bitcast.11, ...), custom_call_target="tpu_custom_call" | custom-call | tf_op jit(solution)/shard_map/weigh/pallas_call | solution.py:391
  5.4 1.5 %collective-permute-start = (bf16[16,12288]{1,0:T(8,128)(2,1)S(1)}, bf16[16,12288]{1,0:T(8,128)(2,1)S(1)}, u32[]{:S(2)}, u32[]{:S(2)}) collective-permute-start(bf16[16,12288]{1,0:T(8,128)(2,1)S(1)} %get-tuple-element.24.first), channel_id=1, source_target_pairs={{0,2},{2,0},{1,3},{3,1},{4,6},{6,4},{5,7},{7,5},{8,10},{10,8},{9,1... | collective-permute-start | bytes 1179656 | tf_op jit(solution)/shard_map/ppermute | solution.py:387
  6.9 2.6 %collective-permute-start.4 = (bf16[2,2,16512]{2,1,0:T(2,128)(2,1)S(1)}, bf16[2,2,16512]{2,1,0:T(2,128)(2,1)S(1)}, u32[]{:S(2)}, u32[]{:S(2)}) collective-permute-start(bf16[2,2,16512]{2,1,0:T(2,128)(2,1)S(1)} %get-tuple-element.35), channel_id=1, source_target_pairs={{0,8},{4,12},{8,0},{12,4},{1,9},{5,13},{9,1},{13,5},{2,10},{6,14},... | collective-permute-start | bytes 396296 | tf_op jit(solution)/shard_map/ppermute | solution.py:436
  9.5 1.7 %collective-permute-done.2.refs_0_ = bf16[4,2,16512]{2,1,0:T(2,128)(2,1)S(1)} collective-permute-done((bf16[4,2,16512]{2,1,0:T(2,128)(2,1)}, bf16[4,2,16512]{2,1,0:T(2,128)(2,1)S(1)}, u32[]{:S(2)}, u32[]{:S(2)}) %collective-permute-start.2) | collective-permute-done | bytes 264224 | tf_op jit(solution)/shard_map/ppermute | solution.py:382
  11.2 0.0 collective-permute-start.3
  11.2 0.2 rest.1.refs_1_
  11.4 2.4 %collective-permute-start.1 = (bf16[16,4352]{1,0:T(8,128)(2,1)S(1)}, bf16[16,4352]{1,0:T(8,128)(2,1)S(1)}, u32[]{:S(2)}, u32[]{:S(2)}) collective-permute-start(bf16[16,4352]{1,0:T(8,128)(2,1)S(1)} %rest.1.refs_1_), channel_id=1, source_target_pairs={{0,2},{2,0},{1,3},{3,1},{4,6},{6,4},{5,7},{7,5},{8,10},{10,8},{9,1... | collective-permute-start | bytes 417800 | tf_op jit(solution)/shard_map/ppermute | solution.py:387
  13.8 3.1 %collective-permute-done.4.refs_1_ = bf16[2,2,16512]{2,1,0:T(2,128)(2,1)S(1)} collective-permute-done((bf16[2,2,16512]{2,1,0:T(2,128)(2,1)S(1)}, bf16[2,2,16512]{2,1,0:T(2,128)(2,1)S(1)}, u32[]{:S(2)}, u32[]{:S(2)}) %collective-permute-start.4) | collective-permute-done | bytes 132128 | tf_op jit(solution)/shard_map/ppermute | solution.py:436
  16.9 0.1 collective-permute-start.5
  17.0 2.3 %prepare.1 = (bf16[48,16512]{1,0:T(8,128)(2,1)S(1)}, f32[8,16512]{1,0:T(8,128)S(1)}, f32[8,16512]{1,0:T(8,128)S(1)}, bf16[56,16512]{1,0:T(8,128)(2,1)S(1)}, f32[56,48]{1,0:T(8,128)S(1)}) custom-call(bf16[16,12288]{1,0:T(8,128)(2,1)S(1)} %get-tuple-element.24.first, bf16[16,4352]{1,0:T(8,128)(2,1)S(1)} %rest.1.refs_1_, ...), custom_call_target="tpu_custom_call" | custom-call | tf_op jit(solution)/shard_map/prepare/pallas_call | solution.py:444
  19.3 1.5 %tables.3 = (bf16[56,16512]{1,0:T(8,128)(2,1)S(1)}, f32[56,48]{1,0:T(8,128)S(1)}) custom-call(bf16[48,16512]{1,0:T(8,128)(2,1)S(1)} %get-tuple-element.30.lhs, f32[8,16512]{1,0:T(8,128)S(1)} %get-tuple-element.31.cosines, f32[8,16512]{1,0:T(8,128)S(1)} %get-tuple-element.32.sines, bf16[4,2,16512]{2,1,0:T(2,128)(2,1)S(1)} %collective-permute-done.2.refs_0_), custom_call_target="tpu_custom_call" | custom-call | tf_op jit(solution)/shard_map/tables/pallas_call | solution.py:469
  20.8 0.0 collective-permute-done.5.refs_2_
  20.8 0.0 collective-permute-done.refs_0_.refs_3_
  20.8 1.5 %tables.5 = (bf16[56,16512]{1,0:T(8,128)(2,1)S(1)}, f32[56,48]{1,0:T(8,128)S(1)}, f32[40,16]{1,0:T(8,128)S(1)}) custom-call(bf16[48,16512]{1,0:T(8,128)(2,1)S(1)} %get-tuple-element.30.lhs, f32[8,16512]{1,0:T(8,128)S(1)} %get-tuple-element.31.cosines, f32[8,16512]{1,0:T(8,128)S(1)} %get-tuple-element.32.sines, ...), custom_call_target="tpu_custom_call" | custom-call | tf_op jit(solution)/shard_map/tables/pallas_call | solution.py:469
  22.3 0.0 collective-permute-done.3.refs_0_
  22.3 1.5 %tables.4 = (bf16[56,16512]{1,0:T(8,128)(2,1)S(1)}, f32[56,48]{1,0:T(8,128)S(1)}) custom-call(bf16[48,16512]{1,0:T(8,128)(2,1)S(1)} %get-tuple-element.30.lhs, f32[8,16512]{1,0:T(8,128)S(1)} %get-tuple-element.31.cosines, f32[8,16512]{1,0:T(8,128)S(1)} %get-tuple-element.32.sines, bf16[4,2,16512]{2,1,0:T(2,128)(2,1)S(1)} %collective-permute-done.3.refs_0_), custom_call_target="tpu_custom_call" | custom-call | tf_op jit(solution)/shard_map/tables/pallas_call | solution.py:469
  23.8 0.9 %first.1.refs_11_ = f32[120,16]{1,0:T(8,128)S(1)} custom-call(bf16[56,16512]{1,0:T(8,128)(2,1)S(1)} %get-tuple-element.29.refs_0_.refs_3_, bf16[56,16512]{1,0:T(8,128)(2,1)S(1)} %get-tuple-element.33.refs_1_.refs_4_, bf16[56,16512]{1,0:T(8,128)(2,1)S(1)} %get-tuple-element.34.refs_2_.refs_5_, bf16[16,12288]{1,0:T(8,128)(2,1)S(1)} %collective-permute-done.refs_0_.refs_3_), custom_call_target="tpu_custom_call" | custom-call | tf_op jit(solution)/shard_map/first/pallas_call | solution.py:509
  24.7 0.0 collective-permute-done.1.refs_2_
  24.8 0.9 %last.1 = (f32[1,128]{1,0:T(1,128)S(1)}, f32[1,128]{1,0:T(1,128)S(1)}) custom-call(bf16[16,12288]{1,0:T(8,128)(2,1)S(1)} %collective-permute-done.refs_0_.refs_3_, bf16[16,4352]{1,0:T(8,128)(2,1)S(1)} %rest.1.refs_1_, bf16[16,4352]{1,0:T(8,128)(2,1)S(1)} %collective-permute-done.1.refs_2_, bf16[56,16512]{1,0:T(8,128)(2,1)S(1)} %get-tuple-element.29.refs_0_.refs_3_, ...), custom_call_target="tpu_custom_call" | custom-call | tf_op jit(solution)/shard_map/last/pallas_call | solution.py:481
  25.6 1.4 %collective-permute-start.6 = (f32[1,128]{1,0:T(1,128)S(1)}, f32[1,128]{1,0:T(1,128)S(1)}, u32[]{:S(2)}, u32[]{:S(2)}) collective-permute-start(f32[1,128]{1,0:T(1,128)S(1)} %get-tuple-element.43), channel_id=1, source_target_pairs={{0,2},{2,0},{1,3},{3,1},{4,6},{6,4},{5,7},{7,5},{8,10},{10,8},{9,1... | collective-permute-start | bytes 1544 | tf_op jit(solution)/shard_map/ppermute | solution.py:387
  27.1 2.1 %collective-permute-done.6.refs_1_ = f32[1,128]{1,0:T(1,128)S(1)} collective-permute-done((f32[1,128]{1,0:T(1,128)S(1)}, f32[1,128]{1,0:T(1,128)S(1)}, u32[]{:S(2)}, u32[]{:S(2)}) %collective-permute-start.6) | collective-permute-done | bytes 544 | tf_op jit(solution)/shard_map/ppermute | solution.py:387
  29.2 0.7 %finish.1 = (f32[2,8]{1,0:T(2,128)}, f32[1,8]{1,0:T(1,128)}) custom-call(f32[1,128]{1,0:T(1,128)S(1)} %get-tuple-element.42.refs_0_, f32[1,128]{1,0:T(1,128)S(1)} %collective-permute-done.6.refs_1_), custom_call_target="tpu_custom_call" | custom-call | tf_op jit(solution)/shard_map/finish/pallas_call | solution.py:526
Async XLA Ops:
  0.6 10.5 %collective-permute-start.2 = (bf16[4,2,16512]{2,1,0:T(2,128)(2,1)}, bf16[4,2,16512]{2,1,0:T(2,128)(2,1)S(1)}, u32[]{:S(2)}, u32[]{:S(2)}) collective-permute-start(bf16[4,2,16512]{2,1,0:T(2,128)(2,1)} %bitcast.6), channel_id=1, source_target_pairs={{0,4},{1,13},{4,0},{5,9},{8,12},{9,5},{12,8},{13,1},{2,6},{3,15},{... | collective-permute-start | bytes 792584 | tf_op jit(solution)/shard_map/ppermute | solution.py:382
  5.4 15.4 %collective-permute-start = (bf16[16,12288]{1,0:T(8,128)(2,1)S(1)}, bf16[16,12288]{1,0:T(8,128)(2,1)S(1)}, u32[]{:S(2)}, u32[]{:S(2)}) collective-permute-start(bf16[16,12288]{1,0:T(8,128)(2,1)S(1)} %get-tuple-element.24.first), channel_id=1, source_target_pairs={{0,2},{2,0},{1,3},{3,1},{4,6},{6,4},{5,7},{7,5},{8,10},{10,8},{9,1... | collective-permute-start | bytes 1179656 | tf_op jit(solution)/shard_map/ppermute | solution.py:387
  6.9 10.0 %collective-permute-start.4 = (bf16[2,2,16512]{2,1,0:T(2,128)(2,1)S(1)}, bf16[2,2,16512]{2,1,0:T(2,128)(2,1)S(1)}, u32[]{:S(2)}, u32[]{:S(2)}) collective-permute-start(bf16[2,2,16512]{2,1,0:T(2,128)(2,1)S(1)} %get-tuple-element.35), channel_id=1, source_target_pairs={{0,8},{4,12},{8,0},{12,4},{1,9},{5,13},{9,1},{13,5},{2,10},{6,14},... | collective-permute-start | bytes 396296 | tf_op jit(solution)/shard_map/ppermute | solution.py:436
  11.2 11.2 %collective-permute-start.3 = (bf16[4,2,16512]{2,1,0:T(2,128)(2,1)S(1)}, bf16[4,2,16512]{2,1,0:T(2,128)(2,1)S(1)}, u32[]{:S(2)}, u32[]{:S(2)}) collective-permute-start(bf16[4,2,16512]{2,1,0:T(2,128)(2,1)S(1)} %collective-permute-done.2.refs_0_), channel_id=1, source_target_pairs={{0,1},{1,0},{2,3},{3,2},{4,5},{5,4},{6,7},{7,6},{8,9},{9,8},{10,11... | collective-permute-start | bytes 792584 | tf_op jit(solution)/shard_map/ppermute | solution.py:496
  11.4 13.3 %collective-permute-start.1 = (bf16[16,4352]{1,0:T(8,128)(2,1)S(1)}, bf16[16,4352]{1,0:T(8,128)(2,1)S(1)}, u32[]{:S(2)}, u32[]{:S(2)}) collective-permute-start(bf16[16,4352]{1,0:T(8,128)(2,1)S(1)} %rest.1.refs_1_), channel_id=1, source_target_pairs={{0,2},{2,0},{1,3},{3,1},{4,6},{6,4},{5,7},{7,5},{8,10},{10,8},{9,1... | collective-permute-start | bytes 417800 | tf_op jit(solution)/shard_map/ppermute | solution.py:387
  16.9 3.9 %collective-permute-start.5 = (bf16[2,2,16512]{2,1,0:T(2,128)(2,1)S(1)}, bf16[2,2,16512]{2,1,0:T(2,128)(2,1)S(1)}, u32[]{:S(2)}, u32[]{:S(2)}) collective-permute-start(bf16[2,2,16512]{2,1,0:T(2,128)(2,1)S(1)} %collective-permute-done.4.refs_1_), channel_id=1, source_target_pairs={{0,1},{1,0},{2,3},{3,2},{4,5},{5,4},{6,7},{7,6},{8,9},{9,8},{10,11... | collective-permute-start | bytes 396296 | tf_op jit(solution)/shard_map/ppermute | solution.py:499
  25.6 3.6 %collective-permute-start.6 = (f32[1,128]{1,0:T(1,128)S(1)}, f32[1,128]{1,0:T(1,128)S(1)}, u32[]{:S(2)}, u32[]{:S(2)}) collective-permute-start(f32[1,128]{1,0:T(1,128)S(1)} %get-tuple-element.43), channel_id=1, source_target_pairs={{0,2},{2,0},{1,3},{3,1},{4,6},{6,4},{5,7},{7,5},{8,10},{10,8},{9,1... | collective-permute-start | bytes 1544 | tf_op jit(solution)/shard_map/ppermute | solution.py:387
